TPU v7x, 128 devices: a whole 4x4x4 slice. The times are simulated.
128 devices in a mesh: layer: 2 (over core), latent: 64 (over y, x, z).
Axes of the slice: x: 4, y: 4, z: 4, core: 2. Of those that a mesh axis runs over, the one named last changes fastest.
Arguments:
- activations: bfloat16 [2, 512, 2048], P('layer', 'latent'), may hold values from -15 to 15
- enc_weight: bfloat16 [2, 2048, 65536], P('layer', None, 'latent'), may hold values from -0.09375 to 0.09375
- enc_bias: float32 [65536], P('latent'), may hold values from -3 to 3
- dec_weight: bfloat16 [2, 65536, 2048], P('layer', 'latent'), may hold values from -0.08984375 to 0.08984375
- dec_bias: float32 [2, 2048], P('layer'), may hold values from -3 to 3
- active_mask: int32 [512, 65536], P(None, 'latent'), may hold values 0 or 1
Outputs:
- grad_enc: bfloat16 [2, 2048, 65536], P('layer', None, 'latent')
- grad_dec: bfloat16 [2, 65536, 2048], P('layer', 'latent')
- loss_value: float32 [], replicated
All inputs are finite; a program needn't handle non-finite values. No bound on the sum of `active_mask` on one device may be relied on, other than what follows from the above.
Results may differ from a plain program's by a relative error of at most 0.0065.
Values may be sent and summed in bfloat16 or wider, within the bound.
No kernel may reach another device: no remote copies, remote signals or barrier semaphores. Data moves between devices by JAX's collectives and lax.ppermute only.
A program may use at most 128 MiB of HBM per device.

v0:
```python
import jax
import jax.numpy as jnp
from jax import lax
from jax.sharding import Mesh
from jax.sharding import PartitionSpec as P

LATENT = ("latent_0", "latent_1", "latent_2")
LAYER_LATENT = ("layer", "latent_0", "latent_1", "latent_2")


sparsity_weight = 0.4


def sent_to_all(x, axis):
    count = lax.axis_size(axis)
    return lax.all_to_all(jnp.broadcast_to(x[None], (count, *x.shape)), axis, 0, 0, tiled=True)


def joined_along(blocks, dim):
    blocks = jnp.moveaxis(blocks, 0, dim)
    shape = blocks.shape
    return blocks.reshape(*shape[:dim], shape[dim] * shape[dim + 1], *shape[dim + 2 :])


def collect(x, axis, dim):
    blocks = sent_to_all(x, axis)
    return joined_along(blocks, dim)


def over_axes(x, axes):
    for axis in axes:
        x = lax.psum(x, axis)
    return x


def per_device(activations, enc_weight, enc_bias, dec_weight, dec_bias, active_mask):
    local_rows = activations[0]
    encoder = enc_weight[0]
    decoder = dec_weight[0]
    token_all = collect(local_rows, LATENT, 0)
    layer_pre = jnp.dot(token_all, encoder, preferred_element_type=jnp.float32)
    dec_float = decoder.astype(jnp.float32)
    row_norm = jnp.sqrt(jnp.sum(dec_float * dec_float, axis=1) + 1e-06)
    preact, norm_sum = lax.psum((layer_pre, row_norm), "layer")
    preact = preact + enc_bias
    gating = active_mask.astype(jnp.float32)
    latent_code = preact * gating
    code_b = latent_code.astype(jnp.bfloat16)
    layer_index = lax.axis_index("layer")
    latent_index = lax.axis_index(LATENT)
    partial_value = jnp.dot(code_b, decoder, preferred_element_type=jnp.float32)
    recon = lax.psum(partial_value, LATENT) + dec_bias[0]
    error_full = recon - token_all.astype(jnp.float32)
    error_b = error_full.astype(jnp.bfloat16)
    square_part = jnp.where(latent_index == 0, 0.5 * jnp.sum(error_full * error_full), 0.0)
    layer_grad = jnp.einsum("td,fd->tf", error_b, decoder, preferred_element_type=jnp.float32)
    code_grad = lax.psum(layer_grad, "layer") + sparsity_weight * norm_sum
    preact_grad = (code_grad * gating).astype(jnp.bfloat16)
    grad_enc = jnp.einsum(
        "td,tf->df", token_all, preact_grad, preferred_element_type=jnp.float32
    ).astype(jnp.bfloat16)
    code_total = jnp.sum(latent_code, axis=0)
    shrink = sparsity_weight * code_total[:, None] * dec_float / row_norm[:, None]
    grad_dec = (
        jnp.einsum("tf,td->fd", code_b, error_b, preferred_element_type=jnp.float32) + shrink
    ).astype(jnp.bfloat16)
    sparse_part = jnp.where(
        layer_index == 0, sparsity_weight * jnp.sum(latent_code * norm_sum), 0.0
    )
    loss_total = over_axes(square_part + sparse_part, LAYER_LATENT)
    loss_value = loss_total / (active_mask.shape[0] * token_all.shape[1])
    return (grad_enc[None], grad_dec[None], loss_value)


def solution(mesh):
    torus = Mesh(
        mesh.devices.reshape(mesh.shape["layer"], 4, 4, 4),
        ("layer", "latent_0", "latent_1", "latent_2"),
    )
    placed = (
        P("layer", LATENT, None),
        P("layer", None, LATENT),
        P(LATENT),
        P("layer", LATENT, None),
        P("layer", None),
        P(None, LATENT),
    )
    return jax.shard_map(
        per_device,
        mesh=torus,
        in_specs=placed,
        out_specs=(P("layer", None, LATENT), P("layer", LATENT, None), P()),
        check_vma=False,
    )
```

profile of v0, /device:TPU:1, one launch (start us, length us, event | category | flops | bytes accessed | tf_op | source)
XLA Modules:
  0.0 290.7 jit_solution(14618392666978174406)
XLA Ops:
  7.2 0.0 all-reduce.4.cloned.1.call-start
  7.2 1.0 broadcast_in_dim.9
  8.2 39.7 %all_to_all.5 = bf16[64,8,2048]{2,1,0:T(8,128)(2,1)S(1)} all-to-all(bf16[64,8,2048]{2,1,0:T(8,128)(2,1)S(1)} %broadcast_in_dim.9), channel_id=1, replica_groups=mesh['layer'=2,'latent_0'=4,'latent_1'=4,'latent_2'=4] {'latent_0','late..., dimensions={0} | all-to-all | bytes 4194304 | tf_op jit(solution)/shard_map/all_to_all | solution.py:16
  48.0 3.7 %fusion.8 = f32[512,1024]{1,0:T(8,128)} fusion(bf16[1,2048,1024]{2,1,0:T(8,128)(2,1)S(1)} %copy-done.5, bf16[64,8,2048]{2,1,0:T(8,128)(2,1)S(1)} %all_to_all.5), kind=kOutput, calls=%fused_computation.10 | convolution fusion | flops 2147483648 | bytes 8388608 | tf_op jit(solution)/shard_map/dot_general | solution.py:41
  51.7 0.0 all-reduce.4.cloned.1.call-update
  51.7 0.0 all-reduce.6.cloned.1.call-start
  51.8 3.1 %fusion = f32[1024]{0:T(1024)S(1)} fusion(bf16[1,1024,2048]{2,1,0:T(8,128)(2,1)} %param.9), kind=kLoop, calls=%fused_computation.2 | loop fusion | flops 6290432 | bytes 4198400 | tf_op jit(solution)/shard_map/reduce_sum | solution.py:43
  54.9 5.0 %psum.59 = f32[1024]{0:T(1024)S(1)} all-reduce(f32[1024]{0:T(1024)S(1)} %add_sqrt_fusion), channel_id=1, replica_groups=mesh['layer'=2,'latent_0'=4,'latent_1'=4,'latent_2'=4] {'layer'}, use_global_device_ids=true, to_apply=%region_4.0 | all-reduce | flops 1024 | bytes 8192 | tf_op jit(solution)/shard_map/psum | solution.py:44
  59.8 17.9 %all-reduce.4.cloned.1.call-done = f32[512,1024]{1,0:T(8,128)} async-done(((f32[512,1024]{1,0:T(8,128)}), f32[512,1024]{1,0:T(8,128)}) %all-reduce.4.cloned.1.call-update) | async-done | bytes 2097168 | tf_op jit(solution)/shard_map/psum | solution.py:44
  77.7 3.6 %multiply_reduce_fusion.1 = (f32[]{:T(128)}, f32[1024]{0:T(1024)S(1)}, bf16[512,1024]{1,0:T(8,128)(2,1)S(1)}) fusion(f32[1024]{0:T(1024)S(1)} %psum.59, s32[512,1024]{1,0:T(8,128)} %param.11, f32[512,1024]{1,0:T(8,128)} %all-reduce.4.cloned.1.call-done, f32[1024]{0:T(1024)S(1)} %copy-done.4), kind=kLoop, calls=%fused_computation.19 | loop fusion | flops 3668991 | bytes 5255172 | tf_op jit(solution)/shard_map/reduce_sum | solution.py:68
  81.3 4.4 %fusion.6 = f32[512,2048]{1,0:T(8,128)} fusion(bf16[1,1024,2048]{2,1,0:T(8,128)(2,1)S(1)} %copy-done, bf16[512,1024]{1,0:T(8,128)(2,1)S(1)} %get-tuple-element.8), kind=kOutput, calls=%fused_computation.8 | convolution fusion | flops 2147483648 | bytes 9437184 | tf_op jit(solution)/shard_map/dot_general | solution.py:51
  85.7 0.0 all-reduce.6.cloned.1.call-update
  85.7 0.0 all-reduce.8.cloned.1.call-start
  85.8 138.2 %all-reduce.6.cloned.1.call-done = f32[512,2048]{1,0:T(8,128)} async-done(((f32[512,2048]{1,0:T(8,128)}), f32[512,2048]{1,0:T(8,128)}) %all-reduce.6.cloned.1.call-update) | async-done | bytes 4194320 | tf_op jit(solution)/shard_map/psum | solution.py:52
  224.1 4.0 %multiply_reduce_fusion = (f32[]{:T(128)}, bf16[512,2048]{1,0:T(8,128)(2,1)S(1)}) fusion(f32[512,2048]{1,0:T(8,128)} %all-reduce.6.cloned.1.call-done, bf16[64,8,2048]{2,1,0:T(8,128)(2,1)S(1)} %all_to_all.5, f32[2048]{0:T(1024)S(1)} %bitcast.32), kind=kLoop, calls=%fused_computation.12 | loop fusion | flops 6291455 | bytes 8396804 | tf_op jit(solution)/shard_map/reduce_sum | solution.py:55
  228.1 1.3 copy-done.2
  229.4 3.7 %fusion.4 = f32[512,1024]{1,0:T(8,128)} fusion(bf16[512,2048]{1,0:T(8,128)(2,1)S(1)} %get-tuple-element.10, bf16[1,1024,2048]{2,1,0:T(8,128)(2,1)S(1)} %copy-done.1), kind=kOutput, calls=%fused_computation.6 | convolution fusion | flops 2147483648 | bytes 8388608 | tf_op jit(solution)/shard_map/td,fd->tf/dot_general | solution.py:56
  234.5 4.7 %psum.60 = f32[]{:T(128)} all-reduce(f32[]{:T(128)S(6)} %add.76), channel_id=1, replica_groups=mesh['layer'=2,'latent_0'=4,'latent_1'=4,'latent_2'=4] {'layer'}, use_global_device_ids=true, to_apply=%region_8.9 | all-reduce | flops 1 | bytes 8 | tf_op jit(solution)/shard_map/psum | solution.py:32
  239.2 7.3 %psum.61 = f32[]{:T(128)} all-reduce(f32[]{:T(128)} %psum.60), channel_id=1, replica_groups=mesh['layer'=2,'latent_0'=4,'latent_1'=4,'latent_2'=4] {'latent_0'}, use_global_device_ids=true, to_apply=%region_9.10 | all-reduce | flops 1 | bytes 8 | tf_op jit(solution)/shard_map/psum | solution.py:32
  246.5 8.7 %psum.62 = f32[]{:T(128)} all-reduce(f32[]{:T(128)} %psum.61), channel_id=1, replica_groups=mesh['layer'=2,'latent_0'=4,'latent_1'=4,'latent_2'=4] {'latent_1'}, use_global_device_ids=true, to_apply=%region_10.11 | all-reduce | flops 1 | bytes 8 | tf_op jit(solution)/shard_map/psum | solution.py:32
  255.2 7.5 %psum.63 = f32[]{:T(128)} all-reduce(f32[]{:T(128)} %psum.62), channel_id=1, replica_groups=mesh['layer'=2,'latent_0'=4,'latent_1'=4,'latent_2'=4] {'latent_2'}, use_global_device_ids=true, to_apply=%region_11.12 | all-reduce | flops 1 | bytes 8 | tf_op jit(solution)/shard_map/psum | solution.py:32
  263.3 6.7 %fusion.10 = bf16[1,1024,2048]{2,1,0:T(8,128)(2,1)} fusion(f32[1024]{0:T(1024)S(1)} %add_sqrt_fusion, bf16[1,1024,2048]{2,1,0:T(8,128)(2,1)} %param.9, f32[1024]{0:T(1024)S(1)} %broadcast_multiply_fusion, bf16[512,2048]{1,0:T(8,128)(2,1)} %copy-done.2, bf16[512,1024]{1,0:T(8,128)(2,1)S(1)} %get-tuple-element.8), kind=kOutput, calls=%fused_computation.15 | convolution fusion | flops 2157969408 | bytes 11542528 | tf_op jit(solution)/shard_map/tf,td->fd/dot_general | solution.py:65
  270.0 6.7 %convert_bitcast_fusion = bf16[1,2048,1024]{1,2,0:T(8,128)(2,1)} fusion(bf16[64,8,2048]{2,1,0:T(8,128)(2,1)S(1)} %all_to_all.5, f32[512,1024]{1,0:T(8,128)} %all-reduce.8.cloned.1.call-done, s32[512,1024]{1,0:T(8,128)} %param.11, f32[1024]{0:T(1024)S(1)} %broadcast_multiply_fusion.1), kind=kOutput, calls=%fused_computation.13 | convolution fusion | flops 2151677952 | bytes 10489856 | tf_op jit(solution)/shard_map/td,tf->df/dot_general | solution.py:59
  276.7 6.4 %copy.9 = bf16[1,2048,1024]{2,1,0:T(8,128)(2,1)} copy(bf16[1,2048,1024]{1,2,0:T(8,128)(2,1)} %convert_bitcast_fusion) | data formatting | bytes 8388608
  (16 shorter events, 0.1 us)
Async XLA Ops:
  7.2 70.6 %all-reduce.4.cloned.1.call-start = ((), (), s32[]{:S(2)}) async-start(), calls=%async_computation.1 | async-start | bytes 4194304 | tf_op jit(solution)/shard_map/psum | solution.py:44
  8.2 39.8 %copy-start.5 = (bf16[1,2048,1024]{2,1,0:T(8,128)(2,1)S(1)}, bf16[1,2048,1024]{2,1,0:T(8,128)(2,1)}, u32[]{:S(2)}) copy-start(bf16[1,2048,1024]{2,1,0:T(8,128)(2,1)} %param.7) | copy-start | bytes 12582916
  51.7 26.0 %copy-start.4 = (f32[1024]{0:T(1024)S(1)}, f32[1024]{0:T(1024)}, u32[]{:S(2)}) copy-start(f32[1024]{0:T(1024)} %param.8) | copy-start | bytes 12292
  51.7 172.3 %all-reduce.6.cloned.1.call-start = ((), (), s32[]{:S(2)}) async-start(), calls=%async_computation.2 | async-start | bytes 8388608 | tf_op jit(solution)/shard_map/psum | solution.py:52
  77.7 3.6 %copy-start = (bf16[1,1024,2048]{2,1,0:T(8,128)(2,1)S(1)}, bf16[1,1024,2048]{2,1,0:T(8,128)(2,1)}, u32[]{:S(2)}) copy-start(bf16[1,1024,2048]{2,1,0:T(8,128)(2,1)} %param.9) | copy-start | bytes 12582916
  85.7 138.3 %copy-start.3 = (f32[1,2048]{1,0:T(1,128)S(1)}, f32[1,2048]{1,0:T(1,128)}, u32[]{:S(2)}) copy-start(f32[1,2048]{1,0:T(1,128)} %param.10) | copy-start | bytes 24580
  85.7 184.3 %all-reduce.8.cloned.1.call-start = ((), (), s32[]{:S(2)}) async-start(), calls=%async_computation.3 | async-start | bytes 4194304 | tf_op jit(solution)/shard_map/psum | solution.py:57
  224.1 5.4 %copy-start.1 = (bf16[1,1024,2048]{2,1,0:T(8,128)(2,1)S(1)}, bf16[1,1024,2048]{2,1,0:T(8,128)(2,1)}, u32[]{:S(2)}) copy-start(bf16[1,1024,2048]{2,1,0:T(8,128)(2,1)} %param.9) | copy-start | bytes 12582916
  228.1 1.4 copy-start.2
Sparse Core Ops, SparseCore 0:
  51.8 25.8 all-reduce.3
  85.9 138.1 all-reduce.5
  233.3 26.0 all-reduce.7
where the time goes:
time: 296 us; the launch traced here: 291 us
  waiting for transfers between devices  156 us (53%)
  blocking collectives  72.9 us (25%)
  matrix products  25.1 us (8%)
  between operations  16.9 us (6%)
  other arithmetic  10.7 us (4%)
  local copies, waits for them, and re-layouts  8.76 us (3%)
    psum x1, waiting for transfers between devices, per_device(): recon = lax.psum(partial_value, LATENT) + dec_bias[0]  138 us
    all_to_all x1, blocking collectives, sent_to_all(): lax.all_to_all(jnp.broadcast_to(x[None], (count, *x.shape)), axis, 0, 0,...  39.7 us
    psum x4, blocking collectives, over_axes(): x = lax.psum(x, axis)  28.2 us
    psum x1, waiting for transfers between devices, per_device(): preact, norm_sum = lax.psum((layer_pre, row_norm), 'layer')  17.9 us
    unnamed x13, local copies, waits for them, and re-layouts  7.77 us
    dot_general x1, matrix products, per_device(): jnp.einsum('td,tf->df', token_all, preact_grad, preferred_element_type=jn...  6.68 us
    dot_general x1, matrix products, per_device(): jnp.einsum('tf,td->fd', code_b, error_b, preferred_element_type=jnp.float32)  6.65 us
  transfers between devices with their start and end apart: 3, of which 2 were waited for; matrix products, arithmetic and copies ran while one was open for 3% of the time, Pallas kernels for 0%

commit v1 on v0

v1 whole, which is shorter than its diff:
```python
import functools

import jax
import jax.numpy as jnp
from jax import lax
from jax.experimental import pallas as pl
from jax.experimental.pallas import tpu as pltpu
from jax.sharding import Mesh
from jax.sharding import PartitionSpec as P

LATENT = ("latent_0", "latent_1", "latent_2")
SPARSITY = 0.4
EXTRA = 128
MIB = 1 << 20


def swap_layers(x):
    return lax.ppermute(x, "layer", [(0, 1), (1, 0)])


def send_to_all(x):
    count = lax.axis_size(LATENT)
    return lax.all_to_all(jnp.broadcast_to(x[None], (count, *x.shape)), LATENT, 0, 0, tiled=True)


def split_float(x):
    high = lax.reduce_precision(x, 8, 7)
    middle = lax.reduce_precision(x - high, 8, 7)
    low = lax.reduce_precision(x - high - middle, 8, 7)
    return high, middle, low


def outer_kernel(a_ref, b_ref, o_ref):
    o_ref[...] = lax.dot_general(
        a_ref[...], b_ref[...], (((0,), (0,)), ((), ())), preferred_element_type=jnp.float32
    ).astype(o_ref.dtype)


def grad_encoder(tokens, preact_grad, block=256):
    count, features = tokens.shape
    latents = preact_grad.shape[1]
    return pl.pallas_call(
        outer_kernel,
        out_shape=jax.ShapeDtypeStruct((features, latents), jnp.bfloat16),
        grid=(features // block,),
        in_specs=[
            pl.BlockSpec((count, block), lambda i: (0, i)),
            pl.BlockSpec((count, latents), lambda i: (0, 0)),
        ],
        out_specs=pl.BlockSpec((block, latents), lambda i: (i, 0)),
        compiler_params=pltpu.CompilerParams(vmem_limit_bytes=32 * MIB),
    )(tokens, preact_grad)


def per_device(activations, enc_weight, enc_bias, dec_weight, dec_bias, active_mask):
    rows = activations[0]
    encoder = enc_weight[0]
    decoder = dec_weight[0]
    own, features = rows.shape
    tokens, latents = active_mask.shape
    token_all = send_to_all(rows).reshape(tokens, features)
    layer_pre = jnp.dot(token_all, encoder, preferred_element_type=jnp.float32)
    preact = layer_pre + swap_layers(layer_pre) + enc_bias
    dec_float = decoder.astype(jnp.float32)
    row_norm = jnp.sqrt(jnp.sum(dec_float * dec_float, axis=1) + 1e-06)
    gating = active_mask.astype(jnp.float32)
    latent_code = preact * gating
    code_b = latent_code.astype(jnp.bfloat16)
    code_total = jnp.sum(latent_code, axis=0)
    partial = jnp.dot(code_b, decoder, preferred_element_type=jnp.float32).astype(jnp.bfloat16)
    parts = lax.all_to_all(partial.reshape(-1, own, features), LATENT, 0, 0, tiled=True)
    error = jnp.sum(parts.astype(jnp.float32), axis=0) + dec_bias - rows.astype(jnp.float32)
    loss_part = 0.5 * jnp.sum(error * error) + SPARSITY * jnp.sum(code_total * row_norm)
    terms = jnp.stack(split_float(loss_part))
    extra = jnp.zeros((own, EXTRA), jnp.float32).at[0, :3].set(terms)
    sent = jnp.concatenate([error, extra], axis=1).astype(jnp.bfloat16)
    got = send_to_all(sent)
    error_b = got[:, :, :features].reshape(tokens, features)
    layer_loss = jnp.sum(got[:, 0, features : features + 3].astype(jnp.float32))
    layer_grad = jnp.einsum("td,fd->tf", error_b, decoder, preferred_element_type=jnp.float32)
    layer_grad = layer_grad + SPARSITY * row_norm
    code_grad = layer_grad + swap_layers(layer_grad)
    loss_value = (layer_loss + swap_layers(layer_loss)) / (tokens * features)
    preact_grad = (code_grad * gating).astype(jnp.bfloat16)
    grad_enc = grad_encoder(token_all, preact_grad)
    shrink = SPARSITY * code_total[:, None] * dec_float / row_norm[:, None]
    grad_dec = (
        jnp.einsum("tf,td->fd", code_b, error_b, preferred_element_type=jnp.float32) + shrink
    ).astype(jnp.bfloat16)
    return (grad_enc[None], grad_dec[None], loss_value)


def solution(mesh):
    torus = Mesh(
        mesh.devices.reshape(mesh.shape["layer"], 4, 4, 4),
        ("layer", *LATENT),
    )
    placed = (
        P("layer", LATENT, None),
        P("layer", None, LATENT),
        P(LATENT),
        P("layer", LATENT, None),
        P("layer", None),
        P(None, LATENT),
    )
    return jax.shard_map(
        per_device,
        mesh=torus,
        in_specs=placed,
        out_specs=(P("layer", None, LATENT), P("layer", LATENT, None), P()),
        check_vma=False,
    )
```

time: 296 us -> 159 us (0.54); the launches traced: 291 us -> 158 us
  waiting for transfers between devices: 156 us -> 27.6 us
  starting transfers between devices: 0.12 us -> 12 us
  matrix products: 25.1 us -> 16.4 us
  between operations: 16.9 us -> 8.59 us
  local copies, waits for them, and re-layouts: 8.76 us -> 1.32 us
  Pallas kernels: 0 us -> 5.7 us
    psum x3 -> x0, waiting for transfers between devices: 156 us -> none  [the longest x1 138 us: per_device(): recon = lax.psum(partial_value, LATENT) + dec_bias[0]]
    all_to_all x1 -> x2, blocking collectives: 39.7 us -> 74.6 us  [send_to_all(): lax.all_to_all(jnp.broadcast_to(x[None], (count, *x.shape)), LATENT, 0, 0...]
    psum x5 -> x0, blocking collectives: 33.2 us -> none  [the longest x4 28.2 us: over_axes(): x = lax.psum(x, axis)]
    all_to_all x0 -> x1, waiting for transfers between devices: none -> 23.9 us  [per_device(): lax.all_to_all(partial.reshape(-1, own, features), LATENT, 0, 0, tiled=True)]
    unnamed x13 -> x16, local copies, waits for them, and re-layouts: 7.77 us -> 0.04 us
    dot_general x2 -> x1, matrix products: 11.1 us -> 3.66 us  [per_device(): jnp.dot(code_b, decoder, preferred_element_type=jnp.float32)]
    ppermute x0 -> x3, starting transfers between devices: none -> 6.43 us  [swap_layers(): return lax.ppermute(x, 'layer', [(0, 1), (1, 0)])]
    pallas_call x0 -> x1, Pallas kernels: none -> 5.7 us  [grad_encoder(): pl.pallas_call(outer_kernel, out_shape=jax.ShapeDtypeStruct((features, la...]
  transfers between devices with their start and end apart: 3 -> 4, of which waited for: 2 -> 2; matrix products, arithmetic and copies ran while one was open for 3% -> 7% of each run, Pallas kernels for 0% -> 0%
where the time goes in v1:
time: 159 us; the launch traced here: 158 us
  blocking collectives  74.6 us (47%)
  waiting for transfers between devices  27.6 us (17%)
  matrix products  16.4 us (10%)
  starting transfers between devices  12 us (8%)
  other arithmetic  12 us (8%)
  between operations  8.59 us (5%)
  Pallas kernels  5.7 us (4%)
    all_to_all x2, blocking collectives, send_to_all(): lax.all_to_all(jnp.broadcast_to(x[None], (count, *x.shape)), LATENT, 0, 0...  74.6 us
    all_to_all x1, waiting for transfers between devices, per_device(): lax.all_to_all(partial.reshape(-1, own, features), LATENT, 0, 0, tiled=True)  23.9 us
    dot_general x1, matrix products, per_device(): jnp.einsum('tf,td->fd', code_b, error_b, preferred_element_type=jnp.float32)  6.63 us
    ppermute x3, starting transfers between devices, swap_layers(): return lax.ppermute(x, 'layer', [(0, 1), (1, 0)])  6.43 us
    pallas_call x1, Pallas kernels, grad_encoder(): pl.pallas_call(outer_kernel, out_shape=jax.ShapeDtypeStruct((features, la...  5.7 us
    all_to_all x1, starting transfers between devices, per_device(): lax.all_to_all(partial.reshape(-1, own, features), LATENT, 0, 0, tiled=True)  5.56 us
    ppermute x3, waiting for transfers between devices, swap_layers(): return lax.ppermute(x, 'layer', [(0, 1), (1, 0)])  3.79 us
    dot_general x1, matrix products, per_device(): jnp.einsum('td,fd->tf', error_b, decoder, preferred_element_type=jnp.floa...  3.72 us
  transfers between devices with their start and end apart: 4, of which 2 were waited for; matrix products, arithmetic and copies ran while one was open for 7% of the time, Pallas kernels for 0%

profile of v1, /device:TPU:1, one launch (start us, length us, event | category | flops | bytes accessed | tf_op | source)
XLA Modules:
  0.0 158.2 jit_solution(5309090624999075389)
XLA Ops:
  0.6 1.0 broadcast_in_dim.11
  1.6 0.0 copy-start.7
  1.6 39.7 %all_to_all.15 = bf16[64,8,2048]{2,1,0:T(8,128)(2,1)S(1)} all-to-all(bf16[64,8,2048]{2,1,0:T(8,128)(2,1)S(1)} %broadcast_in_dim.11), channel_id=1, replica_groups=mesh['layer'=2,'latent_0'=4,'latent_1'=4,'latent_2'=4] {'latent_0','late..., dimensions={0} | all-to-all | bytes 4194304 | tf_op jit(solution)/shard_map/all_to_all | solution.py:23
  41.4 2.4 %fusion.8 = f32[512,1024]{1,0:T(8,128)S(1)} fusion(bf16[1,2048,1024]{2,1,0:T(8,128)(2,1)S(1)} %copy-done.7, bf16[64,8,2048]{2,1,0:T(8,128)(2,1)S(1)} %all_to_all.15), kind=kOutput, calls=%fused_computation.10 | convolution fusion | flops 2147483648 | bytes 8388608 | tf_op jit(solution)/shard_map/dot_general | solution.py:62
  43.8 2.9 %collective-permute-start = (f32[512,1024]{1,0:T(8,128)S(1)}, f32[512,1024]{1,0:T(8,128)S(1)}, u32[]{:S(2)}, u32[]{:S(2)}) collective-permute-start(f32[512,1024]{1,0:T(8,128)S(1)} %fusion.8), channel_id=1, source_target_pairs={{0,64},{64,0},{1,65},{65,1},{2,66},{66,2},{3,67},{67,3},{4,68},{68... | collective-permute-start | bytes 6291464 | tf_op jit(solution)/shard_map/ppermute | solution.py:18
  46.7 3.8 %collective-permute-done = f32[512,1024]{1,0:T(8,128)S(1)} collective-permute-done((f32[512,1024]{1,0:T(8,128)S(1)}, f32[512,1024]{1,0:T(8,128)S(1)}, u32[]{:S(2)}, u32[]{:S(2)}) %collective-permute-start) | collective-permute-done | bytes 2097184 | tf_op jit(solution)/shard_map/ppermute | solution.py:18
  50.5 0.8 fusion.26
  51.3 3.7 %fusion.14 = bf16[64,8,2048]{2,1,0:T(8,128)(2,1)} fusion(bf16[1,1024,2048]{2,1,0:T(8,128)(2,1)S(1)} %copy-done.1, bf16[512,1024]{1,0:T(8,128)(2,1)S(1)} %get-tuple-element.16), kind=kOutput, calls=%fused_computation.15 | convolution fusion | flops 2148532224 | bytes 7340032 | tf_op jit(solution)/shard_map/dot_general | solution.py:70
  55.0 5.6 %all-to-all-start.1 = ((bf16[64,8,2048]{2,1,0:T(8,128)(2,1)}), bf16[64,8,2048]{2,1,0:T(8,128)(2,1)}, u32[]{:S(2)}, u32[]{:S(2)}) async-start(bf16[64,8,2048]{2,1,0:T(8,128)(2,1)} %fusion.14), calls=%async_computation.1 | async-start | bytes 4194304 | tf_op jit(solution)/shard_map/all_to_all | solution.py:71
  60.6 3.1 %fusion = f32[1024]{0:T(1024)S(1)} fusion(bf16[1,1024,2048]{2,1,0:T(8,128)(2,1)} %param.11), kind=kLoop, calls=%fused_computation.2 | loop fusion | flops 6290432 | bytes 4198400 | tf_op jit(solution)/shard_map/reduce_sum | solution.py:65
  63.6 0.6 broadcast_multiply_fusion
  64.9 23.9 %all-to-all-done.1 = bf16[64,8,2048]{2,1,0:T(8,128)(2,1)} async-done(((bf16[64,8,2048]{2,1,0:T(8,128)(2,1)}), bf16[64,8,2048]{2,1,0:T(8,128)(2,1)}, u32[]{:S(2)}, u32[]{:S(2)}) %all-to-all-start.1) | async-done | bytes 2097184 | tf_op jit(solution)/shard_map/all_to_all | solution.py:71
  88.8 1.9 %convert_reduce_fusion = f32[8,2048]{1,0:T(8,128)S(1)} fusion(bf16[64,8,2048]{2,1,0:T(8,128)(2,1)} %all-to-all-done.1), kind=kLoop, calls=%fused_computation.12 | loop fusion | flops 2080768 | bytes 2162688 | tf_op jit(solution)/shard_map/reduce_sum | solution.py:72
  90.7 0.6 multiply_reduce_fusion
  96.1 0.7 maximum_bitcast_fusion
  96.8 0.2 broadcast_in_dim.12
  97.0 34.8 %all_to_all.16 = bf16[64,8,2176]{2,1,0:T(8,128)(2,1)S(1)} all-to-all(bf16[64,8,2176]{2,1,0:T(8,128)(2,1)S(1)} %broadcast_in_dim.12), channel_id=1, replica_groups=mesh['layer'=2,'latent_0'=4,'latent_1'=4,'latent_2'=4] {'latent_0','late..., dimensions={0} | all-to-all | bytes 4456448 | tf_op jit(solution)/shard_map/all_to_all | solution.py:23
  131.9 3.7 %fusion.17 = f32[512,1024]{1,0:T(8,128)} fusion(bf16[1,1024,2048]{2,1,0:T(8,128)(2,1)S(1)} %copy-done.2, bf16[64,8,2176]{2,1,0:T(8,128)(2,1)S(1)} %all_to_all.16, f32[1024]{0:T(1024)S(1)} %get-tuple-element.20), kind=kOutput, calls=%fused_computation.19 | convolution fusion | flops 2148007936 | bytes 8392704 | tf_op jit(solution)/shard_map/td,fd->tf/dot_general | solution.py:80
  135.6 3.5 %collective-permute-start.1 = (f32[512,1024]{1,0:T(8,128)}, f32[512,1024]{1,0:T(8,128)}, u32[]{:S(2)}, u32[]{:S(2)}) collective-permute-start(f32[512,1024]{1,0:T(8,128)} %fusion.17), channel_id=1, source_target_pairs={{0,64},{64,0},{1,65},{65,1},{2,66},{66,2},{3,67},{67,3},{4,68},{68... | collective-permute-start | bytes 6291464 | tf_op jit(solution)/shard_map/ppermute | solution.py:18
  139.1 0.1 copy.10
  139.2 0.6 convert_reduce_fusion.1
  139.8 6.6 %fusion.10 = bf16[1,1024,2048]{2,1,0:T(8,128)(2,1)} fusion(f32[1024]{0:T(1024)S(1)} %get-tuple-element.19, bf16[1,1024,2048]{2,1,0:T(8,128)(2,1)} %param.11, f32[1024]{0:T(1024)S(1)} %get-tuple-element.17, bf16[64,8,2176]{2,1,0:T(8,128)(2,1)} %copy-done.3, bf16[512,1024]{1,0:T(8,128)(2,1)S(1)} %get-tuple-element.16), kind=kOutput, calls=%fused_computation.13 | convolution fusion | flops 2157969408 | bytes 11542528 | tf_op jit(solution)/shard_map/tf,td->fd/dot_general | solution.py:88
  147.7 3.6 %multiply_convert_fusion.b_ref = bf16[512,1024]{1,0:T(8,128)(2,1)S(1)} fusion(f32[512,1024]{1,0:T(8,128)} %fusion.17, f32[512,1024]{1,0:T(8,128)} %collective-permute-done.1, s32[512,1024]{1,0:T(8,128)} %param.13), kind=kLoop, calls=%fused_computation.17 | loop fusion | flops 2097152 | bytes 7340032 | tf_op jit(solution)/shard_map/convert_element_type | solution.py:84
  151.4 5.7 %shard_map.85 = bf16[2048,1024]{1,0:T(8,128)(2,1)} custom-call(bf16[512,2048]{1,0:T(8,128)(2,1)S(1)} %bitcast.54, bf16[512,1024]{1,0:T(8,128)(2,1)S(1)} %multiply_convert_fusion.b_ref), custom_call_target="tpu_custom_call" | custom-call | tf_op jit(solution)/shard_map/pallas_call | solution.py:42
  (22 shorter events, 0.1 us)
Async XLA Ops:
  1.6 39.8 %copy-start.7 = (bf16[1,2048,1024]{2,1,0:T(8,128)(2,1)S(1)}, bf16[1,2048,1024]{2,1,0:T(8,128)(2,1)}, u32[]{:S(2)}) copy-start(bf16[1,2048,1024]{2,1,0:T(8,128)(2,1)} %param.9) | copy-start | bytes 12582916
  41.4 9.1 %copy-start = (s32[512,1024]{1,0:T(8,128)S(1)}, s32[512,1024]{1,0:T(8,128)}, u32[]{:S(2)}) copy-start(s32[512,1024]{1,0:T(8,128)} %param.13) | copy-start | bytes 6291460
  41.4 9.1 %copy-start.6 = (f32[1024]{0:T(1024)S(1)}, f32[1024]{0:T(1024)}, u32[]{:S(2)}) copy-start(f32[1024]{0:T(1024)} %param.10) | copy-start | bytes 12292
  43.8 7.5 %copy-start.1 = (bf16[1,1024,2048]{2,1,0:T(8,128)(2,1)S(1)}, bf16[1,1024,2048]{2,1,0:T(8,128)(2,1)}, u32[]{:S(2)}) copy-start(bf16[1,1024,2048]{2,1,0:T(8,128)(2,1)} %param.11) | copy-start | bytes 12582916
  43.8 6.7 %collective-permute-start = (f32[512,1024]{1,0:T(8,128)S(1)}, f32[512,1024]{1,0:T(8,128)S(1)}, u32[]{:S(2)}, u32[]{:S(2)}) collective-permute-start(f32[512,1024]{1,0:T(8,128)S(1)} %fusion.8), channel_id=1, source_target_pairs={{0,64},{64,0},{1,65},{65,1},{2,66},{66,2},{3,67},{67,3},{4,68},{68... | collective-permute-start | bytes 6291464 | tf_op jit(solution)/shard_map/ppermute | solution.py:18
  55.0 33.8 %all-to-all-start.1 = ((bf16[64,8,2048]{2,1,0:T(8,128)(2,1)}), bf16[64,8,2048]{2,1,0:T(8,128)(2,1)}, u32[]{:S(2)}, u32[]{:S(2)}) async-start(bf16[64,8,2048]{2,1,0:T(8,128)(2,1)} %fusion.14), calls=%async_computation.1 | async-start | bytes 4194304 | tf_op jit(solution)/shard_map/all_to_all | solution.py:71
  63.6 27.0 %copy-start.4 = (bf16[1,8,2048]{2,1,0:T(8,128)(2,1)S(1)}, bf16[1,8,2048]{2,1,0:T(8,128)(2,1)}, u32[]{:S(2)}) copy-start(bf16[1,8,2048]{2,1,0:T(8,128)(2,1)} %param.8) | copy-start | bytes 98308
  63.6 27.0 %copy-start.5 = (f32[1,2048]{1,0:T(1,128)S(1)}, f32[1,2048]{1,0:T(1,128)}, u32[]{:S(2)}) copy-start(f32[1,2048]{1,0:T(1,128)} %param.12) | copy-start | bytes 24580
  97.0 34.8 %copy-start.2 = (bf16[1,1024,2048]{2,1,0:T(8,128)(2,1)S(1)}, bf16[1,1024,2048]{2,1,0:T(8,128)(2,1)}, u32[]{:S(2)}) copy-start(bf16[1,1024,2048]{2,1,0:T(8,128)(2,1)} %param.11) | copy-start | bytes 12582916
  131.8 7.2 %copy-start.3 = (bf16[64,8,2176]{2,1,0:T(8,128)(2,1)}, bf16[64,8,2176]{2,1,0:T(8,128)(2,1)S(1)}, u32[]{:S(2)}) copy-start(bf16[64,8,2176]{2,1,0:T(8,128)(2,1)S(1)} %all_to_all.16) | copy-start | bytes 6684676
  135.6 12.2 %collective-permute-start.1 = (f32[512,1024]{1,0:T(8,128)}, f32[512,1024]{1,0:T(8,128)}, u32[]{:S(2)}, u32[]{:S(2)}) collective-permute-start(f32[512,1024]{1,0:T(8,128)} %fusion.17), channel_id=1, source_target_pairs={{0,64},{64,0},{1,65},{65,1},{2,66},{66,2},{3,67},{67,3},{4,68},{68... | collective-permute-start | bytes 6291464 | tf_op jit(solution)/shard_map/ppermute | solution.py:18
  139.8 6.6 %collective-permute-start.2 = (f32[]{:T(128)}, f32[]{:T(128)}, u32[]{:S(2)}, u32[]{:S(2)}) collective-permute-start(f32[]{:T(128)} %convert_reduce_fusion.1), channel_id=1, source_target_pairs={{0,64},{64,0},{1,65},{65,1},{2,66},{66,2},{3,67},{67,3},{4,68},{68... | collective-permute-start | bytes 20 | tf_op jit(solution)/shard_map/ppermute | solution.py:18

commit v2 on v1

v2 whole, which is shorter than its diff:
```python
import functools

import jax
import jax.numpy as jnp
from jax import lax
from jax.experimental import pallas as pl
from jax.experimental.pallas import tpu as pltpu
from jax.sharding import Mesh
from jax.sharding import PartitionSpec as P

LATENT = ("latent_0", "latent_1", "latent_2")
SIDE = 4
CHIPS = SIDE**3
SPARSITY = 0.4
EXTRA = 128
MIB = 1 << 20
F32 = jnp.float32
BF16 = jnp.bfloat16

STEPS = ((0, 1), (1, 0), (0, -1))


def class_groups():
    groups = [[] for _ in range(SIDE)]
    for chip in range(CHIPS):
        l0, l1 = chip // 16, chip // 4 % 4
        groups[(l1 + 2 * l0) % SIDE].append(chip)
    return groups


def moved(step, sign):
    pairs = []
    for chip in range(CHIPS):
        l0, l1, l2 = chip // 16, chip // 4 % 4, chip % 4
        target = (l0 + sign * step[0]) % 4 * 16 + (l1 + sign * step[1]) % 4 * 4 + l2
        pairs.append((chip, target))
    return pairs


def class_exchange(x):
    return lax.all_to_all(x, LATENT, 0, 0, axis_index_groups=class_groups(), tiled=True)


def from_neighbours(x):
    return [lax.ppermute(x, LATENT, moved(step, -1)) for step in STEPS]


def to_neighbours(parts):
    return [lax.ppermute(x, LATENT, moved(step, 1)) for x, step in zip(parts, STEPS)]


def swap_layers(x):
    return lax.ppermute(x, "layer", [(0, 1), (1, 0)])


def params(mib=40):
    return pltpu.CompilerParams(vmem_limit_bytes=mib * MIB)


def cost(flops, *arrays):
    size = sum(a.size * a.dtype.itemsize for a in arrays)
    return pl.CostEstimate(flops=flops, bytes_accessed=size, transcendentals=0)


def whole(shape):
    return pl.BlockSpec(shape, lambda *_: (0,) * len(shape))


def gate_kernel(class_ref, mask_ref, gate_ref):
    gate_ref[...] = mask_ref[...].astype(F32).astype(BF16)


def ordered_gate(mask, chip_class):
    tokens, latents = mask.shape
    rows = tokens // 16

    def source(r, l0, class_ref):
        return (4 * l0 + lax.rem(class_ref[0] + r + 2 * l0, 4), 0)

    return pl.pallas_call(
        gate_kernel,
        out_shape=jax.ShapeDtypeStruct((tokens, latents), BF16),
        grid_spec=pltpu.PrefetchScalarGridSpec(
            num_scalar_prefetch=1,
            grid=(4, 4),
            in_specs=[pl.BlockSpec((rows, latents), source)],
            out_specs=pl.BlockSpec((rows, latents), lambda r, l0, class_ref: (4 * r + l0, 0)),
        ),
        cost_estimate=cost(0, mask),
        compiler_params=params(),
    )(chip_class, mask)


def encode_kernel(count, *refs):
    tokens, weight_ref, out_ref, joined = refs[:count], *refs[count:]
    rows = tokens[0].shape[0]

    @pl.when(pl.program_id(0) == 0)
    def _():
        for i, ref in enumerate(tokens):
            joined[i * rows : (i + 1) * rows, :] = ref[...]

    out_ref[...] = jnp.dot(joined[...], weight_ref[...], preferred_element_type=F32)


def encode(tokens, weight, block=256):
    rows, features = tokens[0].shape
    latents = weight.shape[1]
    total = rows * len(tokens)
    return pl.pallas_call(
        functools.partial(encode_kernel, len(tokens)),
        out_shape=jax.ShapeDtypeStruct((total, latents), F32),
        grid=(latents // block,),
        in_specs=[whole((rows, features))] * len(tokens)
        + [pl.BlockSpec((features, block), lambda i: (0, i))],
        out_specs=pl.BlockSpec((total, block), lambda i: (0, i)),
        scratch_shapes=[pltpu.VMEM((total, features), BF16)],
        cost_estimate=cost(2 * total * features * latents, *tokens, weight),
        compiler_params=params(),
    )(*tokens, weight)


def decode_kernel(count, pre_ref, other_ref, bias_ref, gate_ref, weight_ref, *refs):
    parts, code_ref, total_ref = refs[:count], *refs[count:]
    rows = parts[0].shape[0]

    @pl.when(pl.program_id(0) == 0)
    def _():
        code = (pre_ref[...] + other_ref[...] + bias_ref[...]) * gate_ref[...].astype(F32)
        code_ref[...] = code.astype(BF16)
        total_ref[...] = jnp.sum(code, axis=0, keepdims=True)

    partial = jnp.dot(code_ref[...], weight_ref[...], preferred_element_type=F32)
    for i, ref in enumerate(parts):
        ref[...] = partial[i * rows : (i + 1) * rows, :].astype(ref.dtype)


def decode(pre, other, bias, gate, first, weight, dtype, block=512):
    total, latents = pre.shape
    features = weight.shape[1]
    rows = CHIPS * 8 // 4
    count = total // rows
    gates = pl.BlockSpec((pl.Element(total), pl.Element(latents)), lambda i: (first * rows, 0))
    *parts, code, code_total = pl.pallas_call(
        functools.partial(decode_kernel, count),
        out_shape=[jax.ShapeDtypeStruct((rows, features), dtype)] * count
        + [jax.ShapeDtypeStruct((total, latents), BF16), jax.ShapeDtypeStruct((1, latents), F32)],
        grid=(features // block,),
        in_specs=[
            whole((total, latents)),
            whole((total, latents)),
            whole((1, latents)),
            gates,
            pl.BlockSpec((latents, block), lambda i: (0, i)),
        ],
        out_specs=[pl.BlockSpec((rows, block), lambda i: (0, i))] * count
        + [whole((total, latents)), whole((1, latents))],
        cost_estimate=cost(2 * total * features * latents, pre, other, weight),
        compiler_params=params(),
    )(pre, other, bias, gate, weight)
    return parts, code, code_total


def add_kernel(own_ref, a_ref, b_ref, c_ref, out_ref):
    total = own_ref[...] + a_ref[...].astype(F32) + b_ref[...].astype(F32) + c_ref[...].astype(F32)
    out_ref[...] = total.astype(out_ref.dtype)


def add_quarters(own, others, block=64):
    rows, features = own.shape
    spec = pl.BlockSpec((block, features), lambda i: (i, 0))
    return pl.pallas_call(
        add_kernel,
        out_shape=jax.ShapeDtypeStruct((rows, features), BF16),
        grid=(rows // block,),
        in_specs=[spec] * 4,
        out_specs=spec,
        cost_estimate=cost(0, own, *others),
        compiler_params=params(),
    )(own, *others)


def error_kernel(parts_ref, rows_ref, bias_ref, code_a_ref, code_b_ref, norm_ref, out_ref):
    count, own, features = parts_ref.shape
    total = parts_ref[0].astype(F32)
    for i in range(1, count):
        total = total + parts_ref[i].astype(F32)
    error = total + bias_ref[...] - rows_ref[...].astype(F32)
    sparse = (code_a_ref[...] + code_b_ref[...]) * norm_ref[...]
    square = jnp.sum(jnp.sum(error * error, axis=0, keepdims=True), axis=1, keepdims=True)
    loss = 0.5 * square + SPARSITY * jnp.sum(sparse, axis=1, keepdims=True)
    loss = jnp.broadcast_to(loss, (own, EXTRA))
    high = loss.astype(BF16).astype(F32)
    middle = (loss - high).astype(BF16).astype(F32)
    low = loss - high - middle
    lane = lax.broadcasted_iota(jnp.int32, (own, EXTRA), 1)
    row = lax.broadcasted_iota(jnp.int32, (own, EXTRA), 0)
    terms = jnp.where(lane == 0, high, jnp.where(lane == 1, middle, jnp.where(lane == 2, low, 0.0)))
    terms = jnp.where(row == 0, terms, 0.0)
    sent = error.astype(BF16)
    terms = terms.astype(BF16)
    for i in range(count):
        out_ref[i, :, :features] = sent
        out_ref[i, :, features:] = terms


def error_blocks(parts, rows, bias, code_a, code_b, norm):
    count, own, features = parts.shape
    return pl.pallas_call(
        error_kernel,
        out_shape=jax.ShapeDtypeStruct((count, own, features + EXTRA), BF16),
        compiler_params=params(),
    )(parts, rows, bias, code_a, code_b, norm)


def code_grad_kernel(count, *refs):
    errors, norm_ref, weight_ref, out_ref, joined = refs[:count], *refs[count:]
    rows = errors[0].shape[0]
    features = weight_ref.shape[1]

    @pl.when(pl.program_id(0) == 0)
    def _():
        for i, ref in enumerate(errors):
            joined[i * rows : (i + 1) * rows, :] = ref[:, :features]

    out_ref[...] = (
        lax.dot_general(
            joined[...], weight_ref[...], (((1,), (1,)), ((), ())), preferred_element_type=F32
        )
        + SPARSITY * norm_ref[...]
    )


def code_gradient(errors, norm, weight, block=256):
    rows, width = errors[0].shape
    latents, features = weight.shape
    total = rows * len(errors)
    return pl.pallas_call(
        functools.partial(code_grad_kernel, len(errors)),
        out_shape=jax.ShapeDtypeStruct((total, latents), F32),
        grid=(latents // block,),
        in_specs=[whole((rows, width))] * len(errors)
        + [
            pl.BlockSpec((1, block), lambda i: (0, i)),
            pl.BlockSpec((block, features), lambda i: (i, 0)),
        ],
        out_specs=pl.BlockSpec((total, block), lambda i: (0, i)),
        scratch_shapes=[pltpu.VMEM((total, features), BF16)],
        cost_estimate=cost(2 * total * features * latents, *errors, weight),
        compiler_params=params(),
    )(*errors, norm, weight)


def loss_kernel(rows_per_chip, *refs):
    errors, out_ref = refs[:-1], refs[-1]
    total = jnp.zeros((1, EXTRA), F32)
    for ref in errors:
        total = total + jnp.sum(ref[...].astype(F32), axis=0, keepdims=True)
    out_ref[...] = jnp.broadcast_to(jnp.sum(total, axis=1, keepdims=True), out_ref.shape)


def layer_loss(errors, features):
    rows = errors[0].shape[0]
    spec = pl.BlockSpec((rows, EXTRA), lambda i: (0, features // EXTRA))
    return pl.pallas_call(
        functools.partial(loss_kernel, 8),
        out_shape=jax.ShapeDtypeStruct((8, EXTRA), F32),
        grid=(1,),
        in_specs=[spec] * len(errors),
        out_specs=whole((8, EXTRA)),
        compiler_params=params(),
    )(*errors)


def transpose_kernel(*refs):
    parts, out_ref = refs[:-1], refs[-1]
    start = 0
    for ref in parts:
        rows = ref.shape[0]
        out_ref[:, start : start + rows] = ref[...].T
        start += rows


def transposed(parts, block=512):
    width = parts[0].shape[1]
    total = sum(x.shape[0] for x in parts)
    return pl.pallas_call(
        transpose_kernel,
        out_shape=jax.ShapeDtypeStruct((width, total), BF16),
        grid=(width // block,),
        in_specs=[pl.BlockSpec((x.shape[0], block), lambda i: (0, i)) for x in parts],
        out_specs=pl.BlockSpec((block, total), lambda i: (i, 0)),
        cost_estimate=cost(0, *parts, *parts),
        compiler_params=params(),
    )(*parts)


def grad_dec_kernel(code_ref, e0, e1, e2, e3, scale_ref, weight_ref, out_ref, joined):
    rows = e0.shape[0]
    features = weight_ref.shape[1]

    @pl.when(pl.program_id(0) == 0)
    def _():
        for i, ref in enumerate((e0, e1, e2, e3)):
            joined[i * rows : (i + 1) * rows, :] = ref[:, :features]

    grad = jnp.dot(code_ref[...], joined[...], preferred_element_type=F32)
    shrink = scale_ref[:, :1] * weight_ref[...].astype(F32)
    out_ref[...] = (grad + shrink).astype(BF16)


def grad_decoder(code_t, errors, scale, weight, block=256):
    latents, features = weight.shape
    tokens = code_t.shape[1]
    rows, width = errors[0].shape
    return pl.pallas_call(
        grad_dec_kernel,
        out_shape=jax.ShapeDtypeStruct((latents, features), BF16),
        grid=(latents // block,),
        in_specs=[pl.BlockSpec((block, tokens), lambda i: (i, 0))]
        + [whole((rows, width))] * 4
        + [
            pl.BlockSpec((block, 128), lambda i: (i, 0)),
            pl.BlockSpec((block, features), lambda i: (i, 0)),
        ],
        out_specs=pl.BlockSpec((block, features), lambda i: (i, 0)),
        scratch_shapes=[pltpu.VMEM((tokens, features), BF16)],
        cost_estimate=cost(2 * tokens * features * latents, code_t, *errors, weight, weight),
        compiler_params=params(),
    )(code_t, *errors, scale, weight)


def grad_enc_kernel(token_ref, a_own, b_own, a_rest, b_rest, gate_ref, out_ref, pre_grad):
    rows = a_own.shape[0]

    @pl.when(pl.program_id(0) == 0)
    def _():
        own = (a_own[...] + b_own[...]) * gate_ref[:rows, :].astype(F32)
        pre_grad[:rows, :] = own.astype(BF16)
        rest = (a_rest[...] + b_rest[...]) * gate_ref[rows:, :].astype(F32)
        pre_grad[rows:, :] = rest.astype(BF16)

    out_ref[...] = jnp.dot(token_ref[...], pre_grad[...], preferred_element_type=F32).astype(BF16)


def grad_encoder(token_t, own, own_other, rest, rest_other, gate, block=256):
    features, tokens = token_t.shape
    latents = gate.shape[1]
    return pl.pallas_call(
        grad_enc_kernel,
        out_shape=jax.ShapeDtypeStruct((features, latents), BF16),
        grid=(features // block,),
        in_specs=[pl.BlockSpec((block, tokens), lambda i: (i, 0))]
        + [whole(own.shape)] * 2
        + [whole(rest.shape)] * 2
        + [whole(gate.shape)],
        out_specs=pl.BlockSpec((block, latents), lambda i: (i, 0)),
        scratch_shapes=[pltpu.VMEM((tokens, latents), BF16)],
        compiler_params=params(),
    )(token_t, own, own_other, rest, rest_other, gate)


def per_device(activations, enc_weight, enc_bias, dec_weight, dec_bias, active_mask):
    rows = activations[0]
    encoder = enc_weight[0]
    decoder = dec_weight[0]
    own, features = rows.shape
    tokens, latents = active_mask.shape
    members = CHIPS // 4
    quarter = members * own
    chip_class = lax.rem(lax.axis_index("latent_1") + 2 * lax.axis_index("latent_0"), 4)
    bias = enc_bias[None]

    q0 = class_exchange(jnp.broadcast_to(rows[None], (members, own, features)))
    q0 = q0.reshape(quarter, features)
    q123 = from_neighbours(q0)
    pre0 = encode([q0], encoder)
    other0 = swap_layers(pre0)
    gate = ordered_gate(active_mask, chip_class[None].astype(jnp.int32))
    dec_float = decoder.astype(F32)
    row_norm = jnp.sqrt(jnp.sum(dec_float * dec_float, axis=1) + 1e-06)
    q123, pre0, gate, row_norm = lax.optimization_barrier((q123, pre0, gate, row_norm))
    pre123 = encode(q123, encoder)
    other123 = swap_layers(pre123)

    parts, code123, total123 = decode(pre123, other123, bias, gate, 1, decoder, BF16)
    received = to_neighbours(parts)
    (part0,), code0, total0 = decode(pre0, other0, bias, gate, 0, decoder, F32)
    token_t = transposed([q0, *q123])
    received, part0, token_t = lax.optimization_barrier((received, part0, token_t))
    partial = add_quarters(part0, received)
    parts = class_exchange(partial.reshape(members, own, features))
    sent = error_blocks(parts, rows, dec_bias, total0, total123, row_norm[None])

    e0 = class_exchange(sent).reshape(quarter, features + EXTRA)
    e123 = from_neighbours(e0)
    norm = row_norm[None]
    grad0 = code_gradient([e0], norm, decoder)
    grad_other0 = swap_layers(grad0)
    code_t = transposed([code0, code123])
    scale = SPARSITY * (total0 + total123)[0] / row_norm
    scale = jnp.broadcast_to(scale[:, None], (latents, 128))
    e123, grad0, code_t, scale = lax.optimization_barrier((e123, grad0, code_t, scale))
    grad123 = code_gradient(e123, norm, decoder)
    grad_other123 = swap_layers(grad123)
    loss = layer_loss([e0, *e123], features)
    loss = (loss + swap_layers(loss))[0, 0]
    grad_dec = grad_decoder(code_t, [e0, *e123], scale, decoder)
    grad_enc = grad_encoder(token_t, grad0, grad_other0, grad123, grad_other123, gate)
    return (grad_enc[None], grad_dec[None], loss / (tokens * features))


def solution(mesh):
    torus = Mesh(
        mesh.devices.reshape(mesh.shape["layer"], SIDE, SIDE, SIDE),
        ("layer", *LATENT),
    )
    placed = (
        P("layer", LATENT, None),
        P("layer", None, LATENT),
        P(LATENT),
        P("layer", LATENT, None),
        P("layer", None),
        P(None, LATENT),
    )
    return jax.shard_map(
        per_device,
        mesh=torus,
        in_specs=placed,
        out_specs=(P("layer", None, LATENT), P("layer", LATENT, None), P()),
        check_vma=False,
    )
```

time: 159 us -> 133 us (0.84)
  blocking collectives: 74.6 us -> 31.1 us
  Pallas kernels: 5.7 us -> 27.2 us
  starting transfers between devices: 12 us -> 29.1 us
  matrix products: 16.4 us -> 0 us
  other arithmetic: 12 us -> 3.1 us
  waiting for transfers between devices: 27.6 us -> 35.5 us
  between operations: 8.59 us -> 2.63 us
  local copies, waits for them, and re-layouts: 1.32 us -> 3.92 us
    all_to_all x2, blocking collectives: 74.6 us -> 31.1 us  [class_exchange(): lax.all_to_all(x, LATENT, 0, 0, axis_index_groups=class_groups(), tiled=T...]
    ppermute x0 -> x9, waiting for transfers between devices: none -> 21.8 us  [the longest x6 14.3 us: from_neighbours(): return [lax.ppermute(x, LATENT, moved(step, -1)) for step in STEPS]]
    pallas_call x1 -> x14, Pallas kernels: 5.7 us -> 27.2 us  [the longest x1 5.76 us: grad_encoder(): pl.pallas_call(grad_enc_kernel, out_shape=jax.ShapeDtypeStruct((features,...]
    dot_general x4 -> x0, matrix products: 16.4 us -> none  [the longest x1 6.63 us: per_device(): jnp.einsum('tf,td->fd', code_b, error_b, preferred_element_type=jnp.float32)]
    all_to_all x1, waiting for transfers between devices: 23.9 us -> 10.8 us  [class_exchange(): lax.all_to_all(x, LATENT, 0, 0, axis_index_groups=class_groups(), tiled=T...]
    ppermute x0 -> x9, starting transfers between devices: none -> 8.22 us  [the longest x3 4.2 us: to_neighbours(): lax.ppermute(x, LATENT, moved(step, 1))]
    all_to_all x1, starting transfers between devices: 5.56 us -> 10.9 us  [class_exchange(): lax.all_to_all(x, LATENT, 0, 0, axis_index_groups=class_groups(), tiled=T...]
    reduce_sum x4 -> x0, other arithmetic: 3.92 us -> none  [the longest x1 1.9 us: per_device(): jnp.sum(parts.astype(jnp.float32), axis=0) + dec_bias]
  transfers between devices with their start and end apart: 4 -> 15, of which waited for: 2 -> 10; matrix products, arithmetic and copies ran while one was open for 7% -> 3% of each run, Pallas kernels for 0% -> 12%
where the time goes in v2:
time: 133 us
  waiting for transfers between devices  35.5 us (27%)
  blocking collectives  31.1 us (23%)
  starting transfers between devices  29.1 us (22%)
  Pallas kernels  27.2 us (20%)
  local copies, waits for them, and re-layouts  3.92 us (3%)
  other arithmetic  3.1 us (2%)
  between operations  2.63 us (2%)
    all_to_all x2, blocking collectives, class_exchange(): lax.all_to_all(x, LATENT, 0, 0, axis_index_groups=class_groups(), tiled=T...  31.1 us
    ppermute x6, waiting for transfers between devices, from_neighbours(): return [lax.ppermute(x, LATENT, moved(step, -1)) for step in STEPS]  14.3 us
    all_to_all x1, starting transfers between devices, class_exchange(): lax.all_to_all(x, LATENT, 0, 0, axis_index_groups=class_groups(), tiled=T...  10.9 us
    all_to_all x1, waiting for transfers between devices, class_exchange(): lax.all_to_all(x, LATENT, 0, 0, axis_index_groups=class_groups(), tiled=T...  10.8 us
    ppermute x5, starting transfers between devices, swap_layers(): return lax.ppermute(x, 'layer', [(0, 1), (1, 0)])  9.95 us
    ppermute x3, waiting for transfers between devices, to_neighbours(): lax.ppermute(x, LATENT, moved(step, 1))  7.45 us
    pallas_call x1, Pallas kernels, grad_encoder(): pl.pallas_call(grad_enc_kernel, out_shape=jax.ShapeDtypeStruct((features,...  5.76 us
    pallas_call x2, Pallas kernels, encode(): pl.pallas_call(functools.partial(encode_kernel, len(tokens)), out_shape=j...  5.02 us
  transfers between devices with their start and end apart: 15, of which 10 were waited for; matrix products, arithmetic and copies ran while one was open for 3% of the time, Pallas kernels for 12%

profile of v2, /device:TPU:1, one launch (start us, length us, event | category | flops | bytes accessed | tf_op | source)
XLA Modules:
  0.0 132.5 jit_solution(9745009146555460565)
XLA Ops:
  0.6 1.6 %broadcast_in_dim.30 = bf16[16,8,2048]{2,1,0:T(8,128)(2,1)} broadcast(bf16[8,2048]{1,0:T(8,128)(2,1)} %bitcast.33), dimensions={1,2} | broadcast | bytes 557056 | tf_op jit(solution)/shard_map/broadcast_in_dim | solution.py:374
  2.2 10.9 %all-to-all-start = ((bf16[16,8,2048]{2,1,0:T(8,128)(2,1)}), bf16[16,8,2048]{2,1,0:T(8,128)(2,1)S(1)}, u32[]{:S(2)}, u32[]{:S(2)}) async-start(bf16[16,8,2048]{2,1,0:T(8,128)(2,1)} %broadcast_in_dim.30), calls=%async_computation | async-start | bytes 1048576 | tf_op jit(solution)/shard_map/all_to_all | solution.py:41
  13.1 1.6 %copy-done.2 = s32[512,1024]{1,0:T(8,128)S(1)} copy-done((s32[512,1024]{1,0:T(8,128)S(1)}, s32[512,1024]{1,0:T(8,128)}, u32[]{:S(2)}) %copy-start.2) | copy-done | bytes 2097176
  15.2 10.8 %all-to-all-done = bf16[16,8,2048]{2,1,0:T(8,128)(2,1)S(1)} async-done(((bf16[16,8,2048]{2,1,0:T(8,128)(2,1)}), bf16[16,8,2048]{2,1,0:T(8,128)(2,1)S(1)}, u32[]{:S(2)}, u32[]{:S(2)}) %all-to-all-start) | async-done | bytes 524320 | tf_op jit(solution)/shard_map/all_to_all | solution.py:41
  27.4 3.1 %multiply_reduce_fusion = f32[1024]{0:T(1024)S(1)} fusion(bf16[1,1024,2048]{2,1,0:T(8,128)(2,1)} %param.9), kind=kLoop, calls=%fused_computation | loop fusion | flops 6290432 | bytes 4198400 | tf_op jit(solution)/shard_map/reduce_sum | solution.py:381
  30.5 2.0 %shard_map.85.pre_ref = f32[128,1024]{1,0:T(8,128)S(1)} custom-call(bf16[128,2048]{1,0:T(8,128)(2,1)S(1)} %bitcast.30, bf16[2048,1024]{1,0:T(8,128)(2,1)S(1)} %bitcast.19), custom_call_target="tpu_custom_call" | custom-call | flops 536870912 | bytes 4718592 | tf_op jit(solution)/shard_map/pallas_call | solution.py:110
  32.5 4.8 %collective-permute-done.refs_0_.refs_1_ = bf16[128,2048]{1,0:T(8,128)(2,1)S(1)} collective-permute-done((bf16[128,2048]{1,0:T(8,128)(2,1)S(1)}, bf16[128,2048]{1,0:T(8,128)(2,1)S(1)}, u32[]{:S(2)}, u32[]{:S(2)}) %collective-permute-start) | collective-permute-done | bytes 524320 | tf_op jit(solution)/shard_map/ppermute | solution.py:45
  38.8 3.1 %shard_map.87.pre_ref = f32[384,1024]{1,0:T(8,128)S(1)} custom-call(bf16[128,2048]{1,0:T(8,128)(2,1)S(1)} %collective-permute-done.refs_0_.refs_1_, bf16[128,2048]{1,0:T(8,128)(2,1)S(1)} %collective-permute-done.1.refs_1_.refs_2_, bf16[128,2048]{1,0:T(8,128)(2,1)S(1)} %collective-permute-done.2.refs_2_.refs_3_, bf16[2048,1024]{1,0:T(8,128)(2,1)S(1)} %bitcast.20), custom_call_target="tpu_custom_call" | custom-call | flops 1610612736 | bytes 5767168 | tf_op jit(solution)/shard_map/pallas_call | solution.py:110
  41.9 3.6 %collective-permute-start.3 = (f32[384,1024]{1,0:T(8,128)S(1)}, f32[384,1024]{1,0:T(8,128)S(1)}, u32[]{:S(2)}, u32[]{:S(2)}) collective-permute-start(f32[384,1024]{1,0:T(8,128)S(1)} %shard_map.87.pre_ref), channel_id=1, source_target_pairs={{0,64},{64,0},{1,65},{65,1},{2,66},{66,2},{3,67},{67,3},{4,68},{68... | collective-permute-start | bytes 4718600 | tf_op jit(solution)/shard_map/ppermute | solution.py:53
  45.6 2.9 %collective-permute-done.3.other_ref = f32[384,1024]{1,0:T(8,128)S(1)} collective-permute-done((f32[384,1024]{1,0:T(8,128)S(1)}, f32[384,1024]{1,0:T(8,128)S(1)}, u32[]{:S(2)}, u32[]{:S(2)}) %collective-permute-start.3) | collective-permute-done | bytes 1572896 | tf_op jit(solution)/shard_map/ppermute | solution.py:53
  48.5 3.1 %shard_map.88 = (bf16[128,2048]{1,0:T(8,128)(2,1)S(1)}, bf16[128,2048]{1,0:T(8,128)(2,1)S(1)}, bf16[128,2048]{1,0:T(8,128)(2,1)S(1)}, bf16[384,1024]{1,0:T(8,128)(2,1)S(1)}, f32[1,1024]{1,0:T(1,128)S(1)}) custom-call(f32[384,1024]{1,0:T(8,128)S(1)} %shard_map.87.pre_ref, f32[384,1024]{1,0:T(8,128)S(1)} %collective-permute-done.3.other_ref, ...), custom_call_target="tpu_custom_call" | custom-call | flops 1610612736 | bytes 7340032 | tf_op jit(solution)/shard_map/pallas_call | solution.py:144
  51.7 1.5 %collective-permute-start.5 = (bf16[128,2048]{1,0:T(8,128)(2,1)S(1)}, bf16[128,2048]{1,0:T(8,128)(2,1)S(1)}, u32[]{:S(2)}, u32[]{:S(2)}) collective-permute-start(bf16[128,2048]{1,0:T(8,128)(2,1)S(1)} %get-tuple-element.33), channel_id=1, source_target_pairs={{0,16},{1,17},{2,18},{3,19},{4,20},{5,21},{6,22},{7,23},{8,24},{9,... | collective-permute-start | bytes 1572872 | tf_op jit(solution)/shard_map/ppermute | solution.py:49
  53.3 2.6 %collective-permute-start.6 = (bf16[128,2048]{1,0:T(8,128)(2,1)S(1)}, bf16[128,2048]{1,0:T(8,128)(2,1)S(1)}, u32[]{:S(2)}, u32[]{:S(2)}) collective-permute-start(bf16[128,2048]{1,0:T(8,128)(2,1)S(1)} %get-tuple-element.34), channel_id=1, source_target_pairs={{0,12},{1,13},{2,14},{3,15},{4,0},{5,1},{6,2},{7,3},{8,4},{9,5},{1... | collective-permute-start | bytes 1572872 | tf_op jit(solution)/shard_map/ppermute | solution.py:49
  56.9 1.8 %shard_map.89 = (f32[128,2048]{1,0:T(8,128)S(1)}, bf16[128,1024]{1,0:T(8,128)(2,1)S(1)}, f32[1,1024]{1,0:T(1,128)S(1)}) custom-call(f32[128,1024]{1,0:T(8,128)S(1)} %shard_map.85.pre_ref, f32[128,1024]{1,0:T(8,128)S(1)} %collective-permute-done.7.other_ref, f32[1,1024]{1,0:T(1,128)S(1)} %bitcast.39, bf16[512,1024]{1,0:T(8,128)(2,1)S(1)} %shard_map.86.gate_ref, ...), custom_call_target="tpu_custom_call" | custom-call | flops 536870912 | bytes 5242880 | tf_op jit(solution)/shard_map/pallas_call | solution.py:144
  58.7 7.4 %collective-permute-done.4.a_ref = bf16[128,2048]{1,0:T(8,128)(2,1)S(1)} collective-permute-done((bf16[128,2048]{1,0:T(8,128)(2,1)S(1)}, bf16[128,2048]{1,0:T(8,128)(2,1)S(1)}, u32[]{:S(2)}, u32[]{:S(2)}) %collective-permute-start.4) | collective-permute-done | bytes 524320 | tf_op jit(solution)/shard_map/ppermute | solution.py:49
  66.4 16.5 %all_to_all.15.parts_ref = bf16[16,8,2048]{2,1,0:T(8,128)(2,1)S(1)} all-to-all(bf16[16,8,2048]{2,1,0:T(8,128)(2,1)S(1)} %bitcast.32), channel_id=1, replica_groups={{0,1,2,3,24,25,26,27,32,33,34,35,56,57,58,59},{4,5,6,7,28,29,30,31,36,3..., dimensions={0} | all-to-all | bytes 1048576 | tf_op jit(solution)/shard_map/all_to_all | solution.py:41
  83.1 14.6 %all_to_all.16 = bf16[16,8,2176]{2,1,0:T(8,128)(2,1)S(1)} all-to-all(bf16[16,8,2176]{2,1,0:T(8,128)(2,1)S(1)} %shard_map.92), channel_id=1, replica_groups={{0,1,2,3,24,25,26,27,32,33,34,35,56,57,58,59},{4,5,6,7,28,29,30,31,36,3..., dimensions={0} | all-to-all | bytes 1114112 | tf_op jit(solution)/shard_map/all_to_all | solution.py:41
  100.8 2.1 %shard_map.93.a_own = f32[128,1024]{1,0:T(8,128)S(1)} custom-call(bf16[128,2176]{1,0:T(8,128)(2,1)S(1)} %bitcast.24, f32[1,1024]{1,0:T(1,128)S(1)} %bitcast.36, bf16[1024,2048]{1,0:T(8,128)(2,1)S(1)} %bitcast.16), custom_call_target="tpu_custom_call" | custom-call | flops 536870912 | bytes 4751360 | tf_op jit(solution)/shard_map/pallas_call | solution.py:238
  102.9 4.8 %collective-permute-done.8.refs_0_.e1.refs_1_ = bf16[128,2176]{1,0:T(8,128)(2,1)S(1)} collective-permute-done((bf16[128,2176]{1,0:T(8,128)(2,1)S(1)}, bf16[128,2176]{1,0:T(8,128)(2,1)S(1)}, u32[]{:S(2)}, u32[]{:S(2)}) %collective-permute-start.8) | collective-permute-done | bytes 557088 | tf_op jit(solution)/shard_map/ppermute | solution.py:45
  107.8 3.1 %collective-permute-done.10.refs_2_.e3.refs_3_ = bf16[128,2176]{1,0:T(8,128)(2,1)S(1)} collective-permute-done((bf16[128,2176]{1,0:T(8,128)(2,1)S(1)}, bf16[128,2176]{1,0:T(8,128)(2,1)S(1)}, u32[]{:S(2)}, u32[]{:S(2)}) %collective-permute-start.10) | collective-permute-done | bytes 557088 | tf_op jit(solution)/shard_map/ppermute | solution.py:45
  111.1 2.7 %shard_map.95.a_rest = f32[384,1024]{1,0:T(8,128)S(1)} custom-call(bf16[128,2176]{1,0:T(8,128)(2,1)S(1)} %collective-permute-done.8.refs_0_.e1.refs_1_, bf16[128,2176]{1,0:T(8,128)(2,1)S(1)} %collective-permute-done.9.refs_1_.e2.refs_2_, bf16[128,2176]{1,0:T(8,128)(2,1)S(1)} %collective-permute-done.10.refs_2_.e3.refs_3_, f32[1,1024]{1,0:T(1,128)S(1)} %bitcast.37, ...), custom_call_target="tpu_custom_call" | custom-call | flops 1610612736 | bytes 5865472 | tf_op jit(solution)/shard_map/pallas_call | solution.py:238
  113.8 5.7 %collective-permute-start.12 = (f32[384,1024]{1,0:T(8,128)S(1)}, f32[384,1024]{1,0:T(8,128)S(1)}, u32[]{:S(2)}, u32[]{:S(2)}) collective-permute-start(f32[384,1024]{1,0:T(8,128)S(1)} %shard_map.95.a_rest), channel_id=1, source_target_pairs={{0,64},{64,0},{1,65},{65,1},{2,66},{66,2},{3,67},{67,3},{4,68},{68... | collective-permute-start | bytes 4718600 | tf_op jit(solution)/shard_map/ppermute | solution.py:53
  120.1 4.3 %shard_map.97 = bf16[1024,2048]{1,0:T(8,128)(2,1)} custom-call(bf16[1024,512]{1,0:T(8,128)(2,1)S(1)} %shard_map.94.code_ref, bf16[128,2176]{1,0:T(8,128)(2,1)S(1)} %bitcast.26, bf16[128,2176]{1,0:T(8,128)(2,1)S(1)} %collective-permute-done.8.refs_0_.e1.refs_1_, bf16[128,2176]{1,0:T(8,128)(2,1)S(1)} %collective-permute-done.9.refs_1_.e2.refs_2_, ...), custom_call_target="tpu_custom_call" | custom-call | flops 2147483648 | bytes 11665408 | tf_op jit(solution)/shard_map/pallas_call | solution.py:316
  125.6 5.8 %shard_map.96 = bf16[2048,1024]{1,0:T(8,128)(2,1)} custom-call(bf16[2048,512]{1,0:T(8,128)(2,1)S(1)} %shard_map.90.token_ref, f32[128,1024]{1,0:T(8,128)S(1)} %shard_map.93.a_own, f32[128,1024]{1,0:T(8,128)S(1)} %collective-permute-done.11.b_own, f32[384,1024]{1,0:T(8,128)S(1)} %shard_map.95.a_rest, f32[384,1024]{1,0:T(8,128)S(1)} %collective-permute-done.12.b_rest, ...), custom_call_target="tpu_custom_call" | custom-call | tf_op jit(solution)/shard_map/pallas_call | solution.py:349
  (42 shorter events, 9.6 us)
Async XLA Ops:
  2.2 23.7 %all-to-all-start = ((bf16[16,8,2048]{2,1,0:T(8,128)(2,1)}), bf16[16,8,2048]{2,1,0:T(8,128)(2,1)S(1)}, u32[]{:S(2)}, u32[]{:S(2)}) async-start(bf16[16,8,2048]{2,1,0:T(8,128)(2,1)} %broadcast_in_dim.30), calls=%async_computation | async-start | bytes 1048576 | tf_op jit(solution)/shard_map/all_to_all | solution.py:41
  13.1 1.6 %copy-start.2 = (s32[512,1024]{1,0:T(8,128)S(1)}, s32[512,1024]{1,0:T(8,128)}, u32[]{:S(2)}) copy-start(s32[512,1024]{1,0:T(8,128)} %mask_ref.1) | copy-start | bytes 6291460
  25.9 4.6 %copy-start.1 = (bf16[1,2048,1024]{2,1,0:T(8,128)(2,1)S(1)}, bf16[1,2048,1024]{2,1,0:T(8,128)(2,1)}, u32[]{:S(2)}) copy-start(bf16[1,2048,1024]{2,1,0:T(8,128)(2,1)} %param.7) | copy-start | bytes 12582916
  25.9 11.4 %collective-permute-start = (bf16[128,2048]{1,0:T(8,128)(2,1)S(1)}, bf16[128,2048]{1,0:T(8,128)(2,1)S(1)}, u32[]{:S(2)}, u32[]{:S(2)}) collective-permute-start(bf16[128,2048]{1,0:T(8,128)(2,1)S(1)} %bitcast.27), channel_id=1, source_target_pairs={{0,12},{1,13},{2,14},{3,15},{4,0},{5,1},{6,2},{7,3},{8,4},{9,5},{1... | collective-permute-start | bytes 1572872 | tf_op jit(solution)/shard_map/ppermute | solution.py:45
  26.8 11.1 %collective-permute-start.1 = (bf16[128,2048]{1,0:T(8,128)(2,1)S(1)}, bf16[128,2048]{1,0:T(8,128)(2,1)S(1)}, u32[]{:S(2)}, u32[]{:S(2)}) collective-permute-start(bf16[128,2048]{1,0:T(8,128)(2,1)S(1)} %bitcast.28), channel_id=1, source_target_pairs={{0,48},{1,49},{2,50},{3,51},{4,52},{5,53},{6,54},{7,55},{8,56},{9,... | collective-permute-start | bytes 1572872 | tf_op jit(solution)/shard_map/ppermute | solution.py:45
  26.8 12.0 %collective-permute-start.2 = (bf16[128,2048]{1,0:T(8,128)(2,1)S(1)}, bf16[128,2048]{1,0:T(8,128)(2,1)S(1)}, u32[]{:S(2)}, u32[]{:S(2)}) collective-permute-start(bf16[128,2048]{1,0:T(8,128)(2,1)S(1)} %bitcast.29), channel_id=1, source_target_pairs={{0,4},{1,5},{2,6},{3,7},{4,8},{5,9},{6,10},{7,11},{8,12},{9,13},{1... | collective-permute-start | bytes 1572872 | tf_op jit(solution)/shard_map/ppermute | solution.py:45
  32.5 16.1 %copy-start = (bf16[1,1024,2048]{2,1,0:T(8,128)(2,1)S(1)}, bf16[1,1024,2048]{2,1,0:T(8,128)(2,1)}, u32[]{:S(2)}) copy-start(bf16[1,1024,2048]{2,1,0:T(8,128)(2,1)} %param.9) | copy-start | bytes 12582916
  32.5 16.1 %copy-start.4 = (f32[1024]{0:T(1024)S(1)}, f32[1024]{0:T(1024)}, u32[]{:S(2)}) copy-start(f32[1024]{0:T(1024)} %param.8) | copy-start | bytes 12292
  41.9 6.7 %collective-permute-start.3 = (f32[384,1024]{1,0:T(8,128)S(1)}, f32[384,1024]{1,0:T(8,128)S(1)}, u32[]{:S(2)}, u32[]{:S(2)}) collective-permute-start(f32[384,1024]{1,0:T(8,128)S(1)} %shard_map.87.pre_ref), channel_id=1, source_target_pairs={{0,64},{64,0},{1,65},{65,1},{2,66},{66,2},{3,67},{67,3},{4,68},{68... | collective-permute-start | bytes 4718600 | tf_op jit(solution)/shard_map/ppermute | solution.py:53
  45.5 11.4 %collective-permute-start.7 = (f32[128,1024]{1,0:T(8,128)S(1)}, f32[128,1024]{1,0:T(8,128)S(1)}, u32[]{:S(2)}, u32[]{:S(2)}) collective-permute-start(f32[128,1024]{1,0:T(8,128)S(1)} %shard_map.85.pre_ref), channel_id=1, source_target_pairs={{0,64},{64,0},{1,65},{65,1},{2,66},{66,2},{3,67},{67,3},{4,68},{68... | collective-permute-start | bytes 1572872 | tf_op jit(solution)/shard_map/ppermute | solution.py:53
  51.7 14.4 %collective-permute-start.4 = (bf16[128,2048]{1,0:T(8,128)(2,1)S(1)}, bf16[128,2048]{1,0:T(8,128)(2,1)S(1)}, u32[]{:S(2)}, u32[]{:S(2)}) collective-permute-start(bf16[128,2048]{1,0:T(8,128)(2,1)S(1)} %get-tuple-element.32), channel_id=1, source_target_pairs={{0,4},{1,5},{2,6},{3,7},{4,8},{5,9},{6,10},{7,11},{8,12},{9,13},{1... | collective-permute-start | bytes 1572872 | tf_op jit(solution)/shard_map/ppermute | solution.py:49
  51.7 14.4 %collective-permute-start.5 = (bf16[128,2048]{1,0:T(8,128)(2,1)S(1)}, bf16[128,2048]{1,0:T(8,128)(2,1)S(1)}, u32[]{:S(2)}, u32[]{:S(2)}) collective-permute-start(bf16[128,2048]{1,0:T(8,128)(2,1)S(1)} %get-tuple-element.33), channel_id=1, source_target_pairs={{0,16},{1,17},{2,18},{3,19},{4,20},{5,21},{6,22},{7,23},{8,24},{9,... | collective-permute-start | bytes 1572872 | tf_op jit(solution)/shard_map/ppermute | solution.py:49
  53.3 12.9 %collective-permute-start.6 = (bf16[128,2048]{1,0:T(8,128)(2,1)S(1)}, bf16[128,2048]{1,0:T(8,128)(2,1)S(1)}, u32[]{:S(2)}, u32[]{:S(2)}) collective-permute-start(bf16[128,2048]{1,0:T(8,128)(2,1)S(1)} %get-tuple-element.34), channel_id=1, source_target_pairs={{0,12},{1,13},{2,14},{3,15},{4,0},{5,1},{6,2},{7,3},{8,4},{9,5},{1... | collective-permute-start | bytes 1572872 | tf_op jit(solution)/shard_map/ppermute | solution.py:49
  56.9 26.1 %copy-start.3 = (bf16[1,8,2048]{2,1,0:T(8,128)(2,1)S(1)}, bf16[1,8,2048]{2,1,0:T(8,128)(2,1)}, u32[]{:S(2)}) copy-start(bf16[1,8,2048]{2,1,0:T(8,128)(2,1)} %param.6) | copy-start | bytes 98308
  56.9 26.1 %copy-start.5 = (f32[1,2048]{1,0:T(1,128)S(1)}, f32[1,2048]{1,0:T(1,128)}, u32[]{:S(2)}) copy-start(f32[1,2048]{1,0:T(1,128)} %bias_ref.1) | copy-start | bytes 24580
  97.8 9.9 %collective-permute-start.8 = (bf16[128,2176]{1,0:T(8,128)(2,1)S(1)}, bf16[128,2176]{1,0:T(8,128)(2,1)S(1)}, u32[]{:S(2)}, u32[]{:S(2)}) collective-permute-start(bf16[128,2176]{1,0:T(8,128)(2,1)S(1)} %bitcast.21), channel_id=1, source_target_pairs={{0,12},{1,13},{2,14},{3,15},{4,0},{5,1},{6,2},{7,3},{8,4},{9,5},{1... | collective-permute-start | bytes 1671176 | tf_op jit(solution)/shard_map/ppermute | solution.py:45
  99.0 8.8 %collective-permute-start.9 = (bf16[128,2176]{1,0:T(8,128)(2,1)S(1)}, bf16[128,2176]{1,0:T(8,128)(2,1)S(1)}, u32[]{:S(2)}, u32[]{:S(2)}) collective-permute-start(bf16[128,2176]{1,0:T(8,128)(2,1)S(1)} %bitcast.22), channel_id=1, source_target_pairs={{0,48},{1,49},{2,50},{3,51},{4,52},{5,53},{6,54},{7,55},{8,56},{9,... | collective-permute-start | bytes 1671176 | tf_op jit(solution)/shard_map/ppermute | solution.py:45
  100.3 10.6 %collective-permute-start.10 = (bf16[128,2176]{1,0:T(8,128)(2,1)S(1)}, bf16[128,2176]{1,0:T(8,128)(2,1)S(1)}, u32[]{:S(2)}, u32[]{:S(2)}) collective-permute-start(bf16[128,2176]{1,0:T(8,128)(2,1)S(1)} %bitcast.23), channel_id=1, source_target_pairs={{0,4},{1,5},{2,6},{3,7},{4,8},{5,9},{6,10},{7,11},{8,12},{9,13},{1... | collective-permute-start | bytes 1671176 | tf_op jit(solution)/shard_map/ppermute | solution.py:45
  113.8 11.8 %collective-permute-start.12 = (f32[384,1024]{1,0:T(8,128)S(1)}, f32[384,1024]{1,0:T(8,128)S(1)}, u32[]{:S(2)}, u32[]{:S(2)}) collective-permute-start(f32[384,1024]{1,0:T(8,128)S(1)} %shard_map.95.a_rest), channel_id=1, source_target_pairs={{0,64},{64,0},{1,65},{65,1},{2,66},{66,2},{3,67},{67,3},{4,68},{68... | collective-permute-start | bytes 4718600 | tf_op jit(solution)/shard_map/ppermute | solution.py:53
  119.5 6.1 %collective-permute-start.11 = (f32[128,1024]{1,0:T(8,128)S(1)}, f32[128,1024]{1,0:T(8,128)S(1)}, u32[]{:S(2)}, u32[]{:S(2)}) collective-permute-start(f32[128,1024]{1,0:T(8,128)S(1)} %shard_map.93.a_own), channel_id=1, source_target_pairs={{0,64},{64,0},{1,65},{65,1},{2,66},{66,2},{3,67},{67,3},{4,68},{68... | collective-permute-start | bytes 1572872 | tf_op jit(solution)/shard_map/ppermute | solution.py:53
  119.7 4.7 %collective-permute-start.13 = (f32[8,128]{1,0:T(8,128)S(1)}, f32[8,128]{1,0:T(8,128)S(1)}, u32[]{:S(2)}, u32[]{:S(2)}) collective-permute-start(f32[8,128]{1,0:T(8,128)S(1)} %shard_map.98), channel_id=1, source_target_pairs={{0,64},{64,0},{1,65},{65,1},{2,66},{66,2},{3,67},{67,3},{4,68},{68... | collective-permute-start | bytes 12296 | tf_op jit(solution)/shard_map/ppermute | solution.py:53

commit v3 on v2

v3 whole, which is shorter than its diff:
```python
import jax
import jax.numpy as jnp
from jax import lax
from jax.experimental import pallas as pl
from jax.experimental.pallas import tpu as pltpu
from jax.sharding import Mesh
from jax.sharding import PartitionSpec as P

LATENT = ("latent_0", "latent_1", "latent_2")
EVERY = ("layer", *LATENT)
SIDE = 4
CHIPS = SIDE**3
SPARSITY = 0.4
EXTRA = 128
MIB = 1 << 20
F32 = jnp.float32
BF16 = jnp.bfloat16

STEPS = (
    ((0, 0, 1), (-1, 0, 0), (0, 0, -1)),
    ((0, 1, 0), (1, 0, 0), (0, -1, 0)),
)


def class_groups():
    groups = [[] for _ in range(SIDE)]
    for chip in range(CHIPS):
        l0, l1, l2 = chip // 16, chip // 4 % 4, chip % 4
        groups[(l1 + 2 * l0 + l2) % SIDE].append(chip)
    return groups


def moved(quarter, sign):
    pairs = []
    for layer, steps in enumerate(STEPS):
        for chip in range(CHIPS):
            place = chip // 16, chip // 4 % 4, chip % 4
            target = [(p + sign * d) % SIDE for p, d in zip(place, steps[quarter - 1])]
            target = target[0] * 16 + target[1] * 4 + target[2]
            pairs.append((layer * CHIPS + chip, layer * CHIPS + target))
    return pairs


def class_exchange(x):
    return lax.all_to_all(x, LATENT, 0, 0, axis_index_groups=class_groups(), tiled=True)


def from_neighbours(x):
    return [lax.ppermute(x, EVERY, moved(r, -1)) for r in (1, 2, 3)]


def to_neighbours(parts):
    return [lax.ppermute(x, EVERY, moved(r, 1)) for r, x in zip((1, 2, 3), parts)]


def swap_layers(x):
    return lax.ppermute(x, "layer", [(0, 1), (1, 0)])


def params(mib=16):
    return pltpu.CompilerParams(vmem_limit_bytes=mib * MIB)


def cost(flops, *arrays):
    size = sum(a.size * a.dtype.itemsize for a in arrays)
    return pl.CostEstimate(flops=flops, bytes_accessed=size, transcendentals=0)


def whole(shape):
    return pl.BlockSpec(shape, lambda *_: (0,) * len(shape))


def gate_kernel(order_ref, mask_ref, gate_ref):
    own = 8
    blocks = gate_ref.shape[0] // own
    first = pl.program_id(0) * blocks
    for i in range(0, blocks, 2):
        pair = [
            mask_ref[pl.ds(pl.multiple_of(order_ref[first + j] * own, own), own), :]
            for j in (i, i + 1)
        ]
        gate_ref[i * own : (i + 2) * own, :] = jnp.concatenate(pair).astype(F32).astype(BF16)


def ordered_gate(mask, place):
    tokens, latents = mask.shape
    l0, l1, l2 = place
    index = jnp.arange(CHIPS, dtype=jnp.int32)
    column = index % 16
    row_class = l1 + 2 * l0 + l2 + index // 16
    order = 4 * column + (row_class - column % 4 - 2 * (column // 4) + 12) % 4
    return pl.pallas_call(
        gate_kernel,
        out_shape=jax.ShapeDtypeStruct((tokens, latents), BF16),
        grid_spec=pltpu.PrefetchScalarGridSpec(
            num_scalar_prefetch=1,
            grid=(4,),
            in_specs=[pl.BlockSpec((tokens, latents), lambda i, order_ref: (0, 0))],
            out_specs=pl.BlockSpec((tokens // 4, latents), lambda i, order_ref: (i, 0)),
        ),
        cost_estimate=cost(0, mask),
        compiler_params=params(),
    )(order.astype(jnp.int32), mask)


def add_kernel(own_ref, a_ref, b_ref, c_ref, out_ref):
    total = own_ref[...] + a_ref[...].astype(F32) + b_ref[...].astype(F32) + c_ref[...].astype(F32)
    out_ref[...] = total.astype(out_ref.dtype)


def add_quarters(own, others, block=64):
    rows, features = own.shape
    spec = pl.BlockSpec((block, features), lambda i: (i, 0))
    return pl.pallas_call(
        add_kernel,
        out_shape=jax.ShapeDtypeStruct((rows, features), BF16),
        grid=(rows // block,),
        in_specs=[spec] * 4,
        out_specs=spec,
        cost_estimate=cost(0, own, *others),
        compiler_params=params(),
    )(own, *others)


def error_kernel(parts_ref, rows_ref, bias_ref, code_a_ref, code_b_ref, norm_ref, out_ref):
    count, own, features = parts_ref.shape
    total = parts_ref[0].astype(F32)
    for i in range(1, count):
        total = total + parts_ref[i].astype(F32)
    error = total + bias_ref[...] - rows_ref[...].astype(F32)
    sparse = (code_a_ref[...] + code_b_ref[...]) * norm_ref[...]
    square = jnp.sum(jnp.sum(error * error, axis=0, keepdims=True), axis=1, keepdims=True)
    loss = 0.5 * square + SPARSITY * jnp.sum(sparse, axis=1, keepdims=True)
    loss = jnp.broadcast_to(loss, (own, EXTRA))
    high = loss.astype(BF16).astype(F32)
    middle = (loss - high).astype(BF16).astype(F32)
    low = loss - high - middle
    lane = lax.broadcasted_iota(jnp.int32, (own, EXTRA), 1)
    row = lax.broadcasted_iota(jnp.int32, (own, EXTRA), 0)
    terms = jnp.where(lane == 0, high, jnp.where(lane == 1, middle, jnp.where(lane == 2, low, 0.0)))
    terms = jnp.where(row == 0, terms, 0.0)
    sent = error.astype(BF16)
    terms = terms.astype(BF16)
    for i in range(count):
        out_ref[i, :, :features] = sent
        out_ref[i, :, features:] = terms


def error_blocks(parts, rows, bias, code_a, code_b, norm):
    count, own, features = parts.shape
    return pl.pallas_call(
        error_kernel,
        out_shape=jax.ShapeDtypeStruct((count, own, features + EXTRA), BF16),
        compiler_params=params(),
    )(parts, rows, bias, code_a, code_b, norm)


def code_gradient(error, norm, weight):
    grad = jnp.einsum("td,fd->tf", error, weight, preferred_element_type=F32)
    return grad + SPARSITY * norm


def loss_kernel(*refs):
    errors, out_ref = refs[:-1], refs[-1]
    total = jnp.zeros((1, EXTRA), F32)
    for ref in errors:
        total = total + jnp.sum(ref[...].astype(F32), axis=0, keepdims=True)
    out_ref[0, 0] = jnp.sum(total)


def layer_loss(errors, features):
    rows = errors[0].shape[0]
    spec = pl.BlockSpec((rows, EXTRA), lambda i: (0, features // EXTRA))
    loss = pl.pallas_call(
        loss_kernel,
        out_shape=jax.ShapeDtypeStruct((1, 1), F32),
        grid=(1,),
        in_specs=[spec] * len(errors),
        out_specs=pl.BlockSpec(memory_space=pltpu.SMEM),
        compiler_params=params(),
    )(*errors)
    return loss[0, 0]


def transpose_kernel(*refs):
    parts, out_ref = refs[:-1], refs[-1]
    start = 0
    for ref in parts:
        rows = ref.shape[0]
        out_ref[:, start : start + rows] = ref[...].T
        start += rows


def transposed(parts, block=512):
    width = parts[0].shape[1]
    total = sum(x.shape[0] for x in parts)
    return pl.pallas_call(
        transpose_kernel,
        out_shape=jax.ShapeDtypeStruct((width, total), BF16),
        grid=(width // block,),
        in_specs=[pl.BlockSpec((x.shape[0], block), lambda i: (0, i)) for x in parts],
        out_specs=pl.BlockSpec((block, total), lambda i: (i, 0)),
        cost_estimate=cost(0, *parts, *parts),
        compiler_params=params(),
    )(*parts)


def grad_dec_kernel(code_ref, e0, e1, e2, e3, scale_ref, weight_ref, out_ref, joined):
    rows = e0.shape[0]
    features = weight_ref.shape[1]

    @pl.when(pl.program_id(0) == 0)
    def _():
        for i, ref in enumerate((e0, e1, e2, e3)):
            joined[i * rows : (i + 1) * rows, :] = ref[:, :features]

    grad = jnp.dot(code_ref[...], joined[...], preferred_element_type=F32)
    shrink = scale_ref[:, :1] * weight_ref[...].astype(F32)
    out_ref[...] = (grad + shrink).astype(BF16)


def grad_decoder(code_t, errors, scale, weight, block=256):
    latents, features = weight.shape
    tokens = code_t.shape[1]
    rows, width = errors[0].shape
    return pl.pallas_call(
        grad_dec_kernel,
        out_shape=jax.ShapeDtypeStruct((latents, features), BF16),
        grid=(latents // block,),
        in_specs=[pl.BlockSpec((block, tokens), lambda i: (i, 0))]
        + [whole((rows, width))] * 4
        + [
            pl.BlockSpec((block, 128), lambda i: (i, 0)),
            pl.BlockSpec((block, features), lambda i: (i, 0)),
        ],
        out_specs=pl.BlockSpec((block, features), lambda i: (i, 0)),
        scratch_shapes=[pltpu.VMEM((tokens, features), BF16)],
        cost_estimate=cost(2 * tokens * features * latents, code_t, *errors, weight, weight),
        compiler_params=params(),
    )(code_t, *errors, scale, weight)


def grad_enc_kernel(token_ref, pre_grad_ref, out_ref):
    out_ref[...] = jnp.dot(
        token_ref[...], pre_grad_ref[...], preferred_element_type=F32
    ).astype(BF16)


def grad_encoder(token_t, pre_grad, block=512):
    features, tokens = token_t.shape
    latents = pre_grad.shape[1]
    return pl.pallas_call(
        grad_enc_kernel,
        out_shape=jax.ShapeDtypeStruct((features, latents), BF16),
        grid=(features // block,),
        in_specs=[pl.BlockSpec((block, tokens), lambda i: (i, 0)), whole(pre_grad.shape)],
        out_specs=pl.BlockSpec((block, latents), lambda i: (i, 0)),
        cost_estimate=cost(2 * tokens * features * latents, token_t, token_t, pre_grad),
        compiler_params=params(),
    )(token_t, pre_grad)


def per_device(activations, enc_weight, enc_bias, dec_weight, dec_bias, active_mask):
    rows = activations[0]
    encoder = enc_weight[0]
    decoder = dec_weight[0]
    own, features = rows.shape
    tokens, latents = active_mask.shape
    members = CHIPS // 4
    quarter = members * own
    bias = enc_bias[None]

    q0 = class_exchange(jnp.broadcast_to(rows[None], (members, own, features)))
    q0 = q0.reshape(quarter, features)
    place = [lax.axis_index(name) for name in LATENT]
    q0, active_mask, decoder, place = lax.optimization_barrier(
        (q0, active_mask, decoder, place)
    )
    q123 = from_neighbours(q0)
    pre0 = jnp.dot(q0, encoder, preferred_element_type=F32)
    other0 = swap_layers(pre0)
    gate = ordered_gate(active_mask, place)
    dec_float = decoder.astype(F32)
    row_norm = jnp.sqrt(jnp.sum(dec_float * dec_float, axis=1) + 1e-06)
    q123, pre0, gate, row_norm = lax.optimization_barrier((q123, pre0, gate, row_norm))
    pre123 = jnp.dot(jnp.concatenate(q123), encoder, preferred_element_type=F32)
    other123 = swap_layers(pre123)

    latent_code = (pre123 + other123 + bias) * gate[quarter:].astype(F32)
    total123 = jnp.sum(latent_code, axis=0, keepdims=True)
    code123 = latent_code.astype(BF16)
    parts = jnp.dot(code123, decoder, preferred_element_type=F32).astype(BF16)
    parts, all_tokens = lax.optimization_barrier((parts, [q0, *q123]))
    received = to_neighbours(parts.reshape(3, quarter, features))
    latent_code = (pre0 + other0 + bias) * gate[:quarter].astype(F32)
    total0 = jnp.sum(latent_code, axis=0, keepdims=True)
    code0 = latent_code.astype(BF16)
    part0 = jnp.dot(code0, decoder, preferred_element_type=F32)
    token_t = transposed(all_tokens)
    code_t = transposed([code0, code123])
    received, part0, token_t, code_t = lax.optimization_barrier((received, part0, token_t, code_t))
    partial = add_quarters(part0, received)
    parts = class_exchange(partial.reshape(members, own, features))
    sent = error_blocks(parts, rows, dec_bias, total0, total123, row_norm[None])

    e0 = class_exchange(sent).reshape(quarter, features + EXTRA)
    e123 = from_neighbours(e0)
    norm = row_norm[None]
    grad0 = code_gradient(e0[:, :features], norm, decoder)
    grad_other0 = swap_layers(grad0)
    scale = SPARSITY * (total0 + total123)[0] / row_norm
    scale = jnp.broadcast_to(scale[:, None], (latents, 128))
    e123, grad0, code_t, scale = lax.optimization_barrier((e123, grad0, code_t, scale))
    grad123 = code_gradient(jnp.concatenate([x[:, :features] for x in e123]), norm, decoder)
    grad_other123 = swap_layers(grad123)
    loss = layer_loss([e0, *e123], features)
    loss = loss + swap_layers(loss)
    grad_dec = grad_decoder(code_t, [e0, *e123], scale, decoder)
    pre_grad0 = ((grad0 + grad_other0) * gate[:quarter].astype(F32)).astype(BF16)
    pre_grad123 = ((grad123 + grad_other123) * gate[quarter:].astype(F32)).astype(BF16)
    grad_enc = grad_encoder(token_t, jnp.concatenate([pre_grad0, pre_grad123]))
    return (grad_enc[None], grad_dec[None], loss / (tokens * features))


def solution(mesh):
    torus = Mesh(
        mesh.devices.reshape(mesh.shape["layer"], SIDE, SIDE, SIDE),
        ("layer", *LATENT),
    )
    placed = (
        P("layer", LATENT, None),
        P("layer", None, LATENT),
        P(LATENT),
        P("layer", LATENT, None),
        P("layer", None),
        P(None, LATENT),
    )
    return jax.shard_map(
        per_device,
        mesh=torus,
        in_specs=placed,
        out_specs=(P("layer", None, LATENT), P("layer", LATENT, None), P()),
        check_vma=False,
    )
```

time: 133 us -> 127 us (0.955)
  Pallas kernels: 27.2 us -> 11.7 us
  matrix products: 0 us -> 8.42 us
  waiting for transfers between devices: 35.5 us -> 29.1 us
  other arithmetic: 3.1 us -> 5.89 us
  blocking collectives: 31.1 us -> 32.8 us
    pallas_call x7 -> x1, Pallas kernels: 14.8 us -> 0.68 us  [layer_loss(): pl.pallas_call(loss_kernel, out_shape=jax.ShapeDtypeStruct((1, 1), F32),...]
    dot_general x0 -> x6, matrix products: none -> 8.42 us  [the longest x2 3.35 us: code_gradient(): grad = jnp.einsum('td,fd->tf', error, weight, preferred_element_type=F32)]
    ppermute x9, waiting for transfers between devices: 21.8 us -> 15.5 us  [the longest x6 11.7 us: from_neighbours(): return [lax.ppermute(x, EVERY, moved(r, -1)) for r in (1, 2, 3)]]
    convert_element_type x0 -> x2, other arithmetic: none -> 1.92 us  [the longest x1 1.83 us: per_device(): ((grad123 + grad_other123) * gate[quarter:].astype(F32)).astype(BF16)]
    ppermute x9, starting transfers between devices: 8.22 us -> 10.1 us  [the longest x6 7.2 us: from_neighbours(): return [lax.ppermute(x, EVERY, moved(r, -1)) for r in (1, 2, 3)]]
    all_to_all x2, blocking collectives: 31.1 us -> 32.8 us  [class_exchange(): lax.all_to_all(x, LATENT, 0, 0, axis_index_groups=class_groups(), tiled=T...]
    pallas_call x1, Pallas kernels: 5.76 us -> 4.1 us  [grad_encoder(): pl.pallas_call(grad_enc_kernel, out_shape=jax.ShapeDtypeStruct((features,...]
    unnamed x12 -> x16, local copies, waits for them, and re-layouts: 1.62 us -> 2.92 us
  transfers between devices with their start and end apart: 15 -> 15, of which waited for: 10 -> 9; matrix products, arithmetic and copies ran while one was open for 3% -> 7% of each run, Pallas kernels for 12% -> 6%
where the time goes in v3:
time: 127 us; the launch traced here: 126 us
  blocking collectives  32.8 us (26%)
  starting transfers between devices  30.1 us (24%)
  waiting for transfers between devices  29.1 us (23%)
  Pallas kernels  11.7 us (9%)
  matrix products  8.42 us (7%)
  other arithmetic  5.89 us (5%)
  local copies, waits for them, and re-layouts  4.97 us (4%)
  between operations  3.35 us (3%)
    all_to_all x2, blocking collectives, class_exchange(): lax.all_to_all(x, LATENT, 0, 0, axis_index_groups=class_groups(), tiled=T...  32.8 us
    ppermute x6, waiting for transfers between devices, from_neighbours(): return [lax.ppermute(x, EVERY, moved(r, -1)) for r in (1, 2, 3)]  11.7 us
    all_to_all x1, starting transfers between devices, class_exchange(): lax.all_to_all(x, LATENT, 0, 0, axis_index_groups=class_groups(), tiled=T...  10.9 us
    all_to_all x1, waiting for transfers between devices, class_exchange(): lax.all_to_all(x, LATENT, 0, 0, axis_index_groups=class_groups(), tiled=T...  10.7 us
    ppermute x5, starting transfers between devices, swap_layers(): return lax.ppermute(x, 'layer', [(0, 1), (1, 0)])  9.03 us
    ppermute x6, starting transfers between devices, from_neighbours(): return [lax.ppermute(x, EVERY, moved(r, -1)) for r in (1, 2, 3)]  7.2 us
    pallas_call x1, Pallas kernels, grad_decoder(): pl.pallas_call(grad_dec_kernel, out_shape=jax.ShapeDtypeStruct((latents,...  4.25 us
    pallas_call x1, Pallas kernels, grad_encoder(): pl.pallas_call(grad_enc_kernel, out_shape=jax.ShapeDtypeStruct((features,...  4.1 us
  transfers between devices with their start and end apart: 15, of which 9 were waited for; matrix products, arithmetic and copies ran while one was open for 7% of the time, Pallas kernels for 6%

profile of v3, /device:TPU:1, one launch (start us, length us, event | category | flops | bytes accessed | tf_op | source)
XLA Modules:
  0.0 126.3 jit_solution(16424444364032265699)
XLA Ops:
  0.6 1.6 %broadcast_in_dim.31 = bf16[16,8,2048]{2,1,0:T(8,128)(2,1)} broadcast(bf16[8,2048]{1,0:T(8,128)(2,1)} %bitcast.41), dimensions={1,2} | broadcast | bytes 557056 | tf_op jit(solution)/shard_map/broadcast_in_dim | solution.py:273
  2.2 10.9 %all-to-all-start = ((bf16[16,8,2048]{2,1,0:T(8,128)(2,1)}), bf16[16,8,2048]{2,1,0:T(8,128)(2,1)S(1)}, u32[]{:S(2)}, u32[]{:S(2)}) async-start(bf16[16,8,2048]{2,1,0:T(8,128)(2,1)} %broadcast_in_dim.31), calls=%async_computation | async-start | bytes 1048576 | tf_op jit(solution)/shard_map/all_to_all | solution.py:45
  13.1 10.7 %all-to-all-done = bf16[16,8,2048]{2,1,0:T(8,128)(2,1)S(1)} async-done(((bf16[16,8,2048]{2,1,0:T(8,128)(2,1)}), bf16[16,8,2048]{2,1,0:T(8,128)(2,1)S(1)}, u32[]{:S(2)}, u32[]{:S(2)}) %all-to-all-start) | async-done | bytes 524320 | tf_op jit(solution)/shard_map/all_to_all | solution.py:45
  23.8 3.1 %collective-permute-start.1 = (bf16[128,2048]{1,0:T(8,128)(2,1)S(1)}, bf16[128,2048]{1,0:T(8,128)(2,1)S(1)}, u32[]{:S(2)}, u32[]{:S(2)}) collective-permute-start(bf16[128,2048]{1,0:T(8,128)(2,1)S(1)} %bitcast.36), channel_id=1, source_target_pairs={{0,16},{1,17},{2,18},{3,19},{4,20},{5,21},{6,22},{7,23},{8,24},{9,... | collective-permute-start | bytes 1572872 | tf_op jit(solution)/shard_map/ppermute | solution.py:49
  27.0 3.2 %multiply_reduce_fusion = f32[1024]{0:T(1024)S(1)} fusion(bf16[1024,2048]{1,0:T(8,128)(2,1)} %bitcast.23), kind=kLoop, calls=%fused_computation | loop fusion | flops 6290432 | bytes 4198400 | tf_op jit(solution)/shard_map/reduce_sum | solution.py:284
  33.1 3.4 %collective-permute-done.2.refs_3_ = bf16[128,2048]{1,0:T(8,128)(2,1)S(1)} collective-permute-done((bf16[128,2048]{1,0:T(8,128)(2,1)S(1)}, bf16[128,2048]{1,0:T(8,128)(2,1)S(1)}, u32[]{:S(2)}, u32[]{:S(2)}) %collective-permute-start.2) | collective-permute-done | bytes 524320 | tf_op jit(solution)/shard_map/ppermute | solution.py:49
  36.5 1.8 %fusion = f32[384,1024]{1,0:T(8,128)S(1)} fusion(bf16[1,2048,1024]{2,1,0:T(8,128)(2,1)S(1)} %copy-done.6, bf16[128,2048]{1,0:T(8,128)(2,1)S(1)} %collective-permute-done.2.refs_3_, bf16[128,2048]{1,0:T(8,128)(2,1)S(1)} %collective-permute-done.1.refs_2_, bf16[128,2048]{1,0:T(8,128)(2,1)S(1)} %collective-permute-done.refs_1_), kind=kOutput, calls=%fused_computation.1 | convolution fusion | flops 1615331328 | bytes 7340032 | tf_op jit(solution)/shard_map/dot_general | solution.py:286
  38.3 2.1 %collective-permute-start.3 = (f32[384,1024]{1,0:T(8,128)S(1)}, f32[384,1024]{1,0:T(8,128)S(1)}, u32[]{:S(2)}, u32[]{:S(2)}) collective-permute-start(f32[384,1024]{1,0:T(8,128)S(1)} %fusion), channel_id=1, source_target_pairs={{0,64},{64,0},{1,65},{65,1},{2,66},{66,2},{3,67},{67,3},{4,68},{68... | collective-permute-start | bytes 4718600 | tf_op jit(solution)/shard_map/ppermute | solution.py:57
  40.5 2.9 %collective-permute-done.3 = f32[384,1024]{1,0:T(8,128)S(1)} collective-permute-done((f32[384,1024]{1,0:T(8,128)S(1)}, f32[384,1024]{1,0:T(8,128)S(1)}, u32[]{:S(2)}, u32[]{:S(2)}) %collective-permute-start.3) | collective-permute-done | bytes 1572896 | tf_op jit(solution)/shard_map/ppermute | solution.py:57
  44.0 1.8 %convolution_convert_fusion = bf16[384,2048]{1,0:T(8,128)(2,1)S(1)} fusion(bf16[384,1024]{1,0:T(8,128)(2,1)S(1)} %get-tuple-element.62.refs_1_, bf16[1024,2048]{1,0:T(8,128)(2,1)S(1)} %bitcast.24), kind=kOutput, calls=%fused_computation.5 | convolution fusion | flops 1611399168 | bytes 6553600 | tf_op jit(solution)/shard_map/dot_general | solution.py:292
  47.0 1.8 %collective-permute-start.6 = (bf16[128,2048]{1,0:T(8,128)(2,1)S(1)}, bf16[128,2048]{1,0:T(8,128)(2,1)S(1)}, u32[]{:S(2)}, u32[]{:S(2)}) collective-permute-start(bf16[128,2048]{1,0:T(8,128)(2,1)S(1)} %get-tuple-element.65), channel_id=1, source_target_pairs={{0,3},{1,0},{2,1},{3,2},{4,7},{5,4},{6,5},{7,6},{8,11},{9,8},{10,9... | collective-permute-start | bytes 1572872 | tf_op jit(solution)/shard_map/ppermute | solution.py:53
  52.5 3.0 %collective-permute-done.4.a_ref = bf16[128,2048]{1,0:T(8,128)(2,1)S(1)} collective-permute-done((bf16[128,2048]{1,0:T(8,128)(2,1)S(1)}, bf16[128,2048]{1,0:T(8,128)(2,1)S(1)}, u32[]{:S(2)}, u32[]{:S(2)}) %collective-permute-start.4) | collective-permute-done | bytes 524320 | tf_op jit(solution)/shard_map/ppermute | solution.py:53
  56.5 15.8 %all_to_all.15.parts_ref = bf16[16,8,2048]{2,1,0:T(8,128)(2,1)S(1)} all-to-all(bf16[16,8,2048]{2,1,0:T(8,128)(2,1)S(1)} %bitcast.40), channel_id=1, replica_groups={{0,7,10,13,18,21,24,31,32,39,42,45,50,53,56,63},{1,4,11,14,19,22,25,28,..., dimensions={0} | all-to-all | bytes 1048576 | tf_op jit(solution)/shard_map/all_to_all | solution.py:45
  72.5 17.0 %all_to_all.16 = bf16[16,8,2176]{2,1,0:T(8,128)(2,1)S(1)} all-to-all(bf16[16,8,2176]{2,1,0:T(8,128)(2,1)S(1)} %shard_map.89), channel_id=1, replica_groups={{0,7,10,13,18,21,24,31,32,39,42,45,50,53,56,63},{1,4,11,14,19,22,25,28,..., dimensions={0} | all-to-all | bytes 1114112 | tf_op jit(solution)/shard_map/all_to_all | solution.py:45
  89.6 4.0 %collective-permute-start.8 = (bf16[128,2176]{1,0:T(8,128)(2,1)S(1)}, bf16[128,2176]{1,0:T(8,128)(2,1)S(1)}, u32[]{:S(2)}, u32[]{:S(2)}) collective-permute-start(bf16[128,2176]{1,0:T(8,128)(2,1)S(1)} %bitcast.30), channel_id=1, source_target_pairs={{0,3},{1,0},{2,1},{3,2},{4,7},{5,4},{6,5},{7,6},{8,11},{9,8},{10,9... | collective-permute-start | bytes 1671176 | tf_op jit(solution)/shard_map/ppermute | solution.py:49
  93.6 1.5 %broadcast_add_fusion = f32[128,1024]{1,0:T(8,128)S(1)} fusion(f32[1024]{0:T(1024)S(1)} %get-tuple-element.69, bf16[1024,2048]{1,0:T(8,128)(2,1)S(1)} %bitcast.26, bf16[128,2176]{1,0:T(8,128)(2,1)S(1)} %bitcast.32), kind=kOutput, calls=%fused_computation.27 | convolution fusion | flops 537001984 | bytes 5246976 | tf_op jit(solution)/shard_map/td,fd->tf/dot_general | solution.py:159
  95.2 5.6 %collective-permute-done.10.e3.refs_3_ = bf16[128,2176]{1,0:T(8,128)(2,1)S(1)} collective-permute-done((bf16[128,2176]{1,0:T(8,128)(2,1)S(1)}, bf16[128,2176]{1,0:T(8,128)(2,1)S(1)}, u32[]{:S(2)}, u32[]{:S(2)}) %collective-permute-start.10) | collective-permute-done | bytes 557088 | tf_op jit(solution)/shard_map/ppermute | solution.py:49
  100.8 1.5 %collective-permute-done.9.e2.refs_2_ = bf16[128,2176]{1,0:T(8,128)(2,1)S(1)} collective-permute-done((bf16[128,2176]{1,0:T(8,128)(2,1)S(1)}, bf16[128,2176]{1,0:T(8,128)(2,1)S(1)}, u32[]{:S(2)}, u32[]{:S(2)}) %collective-permute-start.9) | collective-permute-done | bytes 557088 | tf_op jit(solution)/shard_map/ppermute | solution.py:49
  102.6 1.8 %fusion.16 = f32[384,1024]{1,0:T(8,128)S(1)} fusion(bf16[1024,2048]{1,0:T(8,128)(2,1)S(1)} %bitcast.27, bf16[128,2048]{1,0:T(8,128)(2,1)S(1)} %slice.28, bf16[128,2048]{1,0:T(8,128)(2,1)S(1)} %slice.27, bf16[128,2048]{1,0:T(8,128)(2,1)S(1)} %slice.26, f32[1024]{0:T(1024)S(1)} %get-tuple-element.69), kind=kOutput, calls=%fused_computation.20 | convolution fusion | flops 1615724544 | bytes 7344128 | tf_op jit(solution)/shard_map/td,fd->tf/dot_general | solution.py:159
  104.4 6.3 %collective-permute-start.12 = (f32[384,1024]{1,0:T(8,128)S(1)}, f32[384,1024]{1,0:T(8,128)}, u32[]{:S(2)}, u32[]{:S(2)}) collective-permute-start(f32[384,1024]{1,0:T(8,128)S(1)} %fusion.16), channel_id=1, source_target_pairs={{0,64},{64,0},{1,65},{65,1},{2,66},{66,2},{3,67},{67,3},{4,68},{68... | collective-permute-start | bytes 4718600 | tf_op jit(solution)/shard_map/ppermute | solution.py:57
  112.0 4.2 %shard_map.91 = bf16[1024,2048]{1,0:T(8,128)(2,1)} custom-call(bf16[1024,512]{1,0:T(8,128)(2,1)S(1)} %shard_map.87.code_ref, bf16[128,2176]{1,0:T(8,128)(2,1)S(1)} %bitcast.34, bf16[128,2176]{1,0:T(8,128)(2,1)S(1)} %collective-permute-done.8.e1.refs_1_, bf16[128,2176]{1,0:T(8,128)(2,1)S(1)} %collective-permute-done.9.e2.refs_2_, ...), custom_call_target="tpu_custom_call" | custom-call | flops 2147483648 | bytes 11665408 | tf_op jit(solution)/shard_map/pallas_call | solution.py:226
  117.7 1.8 %fusion.4 = bf16[384,1024]{1,0:T(8,128)(2,1)S(1)} fusion(f32[384,1024]{1,0:T(8,128)S(1)} %fusion.16, f32[384,1024]{1,0:T(8,128)} %collective-permute-done.12, bf16[512,1024]{1,0:T(8,128)(2,1)S(1)} %shard_map.85), kind=kLoop, calls=%fused_computation.8 | loop fusion | flops 1572864 | bytes 4718592 | tf_op jit(solution)/shard_map/convert_element_type | solution.py:320
  119.6 1.5 %copy-done.3 = bf16[2048,512]{1,0:T(8,128)(2,1)S(1)} copy-done((bf16[2048,512]{1,0:T(8,128)(2,1)S(1)}, bf16[2048,512]{1,0:T(8,128)(2,1)}, u32[]{:S(2)}) %copy-start.3) | copy-done | bytes 2097176
  121.1 4.1 %shard_map.90 = bf16[2048,1024]{1,0:T(8,128)(2,1)} custom-call(bf16[2048,512]{1,0:T(8,128)(2,1)S(1)} %copy-done.3, bf16[512,1024]{1,0:T(8,128)(2,1)S(1)} %pad_maximum_fusion.pre_grad_ref), custom_call_target="tpu_custom_call" | custom-call | flops 2147483648 | bytes 5242880 | tf_op jit(solution)/shard_map/pallas_call | solution.py:252
  (53 shorter events, 11.4 us)
Async XLA Ops:
  2.2 21.6 %all-to-all-start = ((bf16[16,8,2048]{2,1,0:T(8,128)(2,1)}), bf16[16,8,2048]{2,1,0:T(8,128)(2,1)S(1)}, u32[]{:S(2)}, u32[]{:S(2)}) async-start(bf16[16,8,2048]{2,1,0:T(8,128)(2,1)} %broadcast_in_dim.31), calls=%async_computation | async-start | bytes 1048576 | tf_op jit(solution)/shard_map/all_to_all | solution.py:45
  23.8 8.3 %collective-permute-start = (bf16[128,2048]{1,0:T(8,128)(2,1)S(1)}, bf16[128,2048]{1,0:T(8,128)(2,1)S(1)}, u32[]{:S(2)}, u32[]{:S(2)}) collective-permute-start(bf16[128,2048]{1,0:T(8,128)(2,1)S(1)} %bitcast.35), channel_id=1, source_target_pairs={{0,3},{1,0},{2,1},{3,2},{4,7},{5,4},{6,5},{7,6},{8,11},{9,8},{10,9... | collective-permute-start | bytes 1572872 | tf_op jit(solution)/shard_map/ppermute | solution.py:49
  23.8 9.3 %collective-permute-start.1 = (bf16[128,2048]{1,0:T(8,128)(2,1)S(1)}, bf16[128,2048]{1,0:T(8,128)(2,1)S(1)}, u32[]{:S(2)}, u32[]{:S(2)}) collective-permute-start(bf16[128,2048]{1,0:T(8,128)(2,1)S(1)} %bitcast.36), channel_id=1, source_target_pairs={{0,16},{1,17},{2,18},{3,19},{4,20},{5,21},{6,22},{7,23},{8,24},{9,... | collective-permute-start | bytes 1572872 | tf_op jit(solution)/shard_map/ppermute | solution.py:49
  26.9 9.5 %collective-permute-start.2 = (bf16[128,2048]{1,0:T(8,128)(2,1)S(1)}, bf16[128,2048]{1,0:T(8,128)(2,1)S(1)}, u32[]{:S(2)}, u32[]{:S(2)}) collective-permute-start(bf16[128,2048]{1,0:T(8,128)(2,1)S(1)} %bitcast.37), channel_id=1, source_target_pairs={{0,1},{1,2},{2,3},{3,0},{4,5},{5,6},{6,7},{7,4},{8,9},{9,10},{10,1... | collective-permute-start | bytes 1572872 | tf_op jit(solution)/shard_map/ppermute | solution.py:49
  27.0 3.2 %copy-start.1 = (s32[512,1024]{1,0:T(8,128)S(1)}, s32[512,1024]{1,0:T(8,128)}, u32[]{:S(2)}) copy-start(s32[512,1024]{1,0:T(8,128)} %mask_ref) | copy-start | bytes 6291460
  27.0 4.1 %copy-start.6 = (bf16[1,2048,1024]{2,1,0:T(8,128)(2,1)S(1)}, bf16[1,2048,1024]{2,1,0:T(8,128)(2,1)}, u32[]{:S(2)}) copy-start(bf16[1,2048,1024]{2,1,0:T(8,128)(2,1)} %param.7) | copy-start | bytes 12582916
  31.8 11.7 %copy-start.7 = (f32[1024]{0:T(1024)S(1)}, f32[1024]{0:T(1024)}, u32[]{:S(2)}) copy-start(f32[1024]{0:T(1024)} %param.8) | copy-start | bytes 12292
  38.3 5.7 %copy-start = (bf16[1,1024,2048]{2,1,0:T(8,128)(2,1)S(1)}, bf16[1,1024,2048]{2,1,0:T(8,128)(2,1)}, u32[]{:S(2)}) copy-start(bf16[1,1024,2048]{2,1,0:T(8,128)(2,1)} %param.9) | copy-start | bytes 12582916
  38.3 5.1 %collective-permute-start.3 = (f32[384,1024]{1,0:T(8,128)S(1)}, f32[384,1024]{1,0:T(8,128)S(1)}, u32[]{:S(2)}, u32[]{:S(2)}) collective-permute-start(f32[384,1024]{1,0:T(8,128)S(1)} %fusion), channel_id=1, source_target_pairs={{0,64},{64,0},{1,65},{65,1},{2,66},{66,2},{3,67},{67,3},{4,68},{68... | collective-permute-start | bytes 4718600 | tf_op jit(solution)/shard_map/ppermute | solution.py:57
  40.4 8.4 %collective-permute-start.7 = (f32[128,1024]{1,0:T(8,128)S(1)}, f32[128,1024]{1,0:T(8,128)S(1)}, u32[]{:S(2)}, u32[]{:S(2)}) collective-permute-start(f32[128,1024]{1,0:T(8,128)S(1)} %fusion.2), channel_id=1, source_target_pairs={{0,64},{64,0},{1,65},{65,1},{2,66},{66,2},{3,67},{67,3},{4,68},{68... | collective-permute-start | bytes 1572872 | tf_op jit(solution)/shard_map/ppermute | solution.py:57
  45.9 9.6 %collective-permute-start.4 = (bf16[128,2048]{1,0:T(8,128)(2,1)S(1)}, bf16[128,2048]{1,0:T(8,128)(2,1)S(1)}, u32[]{:S(2)}, u32[]{:S(2)}) collective-permute-start(bf16[128,2048]{1,0:T(8,128)(2,1)S(1)} %get-tuple-element.67), channel_id=1, source_target_pairs={{0,1},{1,2},{2,3},{3,0},{4,5},{5,6},{6,7},{7,4},{8,9},{9,10},{10,1... | collective-permute-start | bytes 1572872 | tf_op jit(solution)/shard_map/ppermute | solution.py:53
  46.5 9.8 %collective-permute-start.5 = (bf16[128,2048]{1,0:T(8,128)(2,1)S(1)}, bf16[128,2048]{1,0:T(8,128)(2,1)S(1)}, u32[]{:S(2)}, u32[]{:S(2)}) collective-permute-start(bf16[128,2048]{1,0:T(8,128)(2,1)S(1)} %get-tuple-element.66), channel_id=1, source_target_pairs={{0,48},{1,49},{2,50},{3,51},{4,52},{5,53},{6,54},{7,55},{8,56},{9,... | collective-permute-start | bytes 1572872 | tf_op jit(solution)/shard_map/ppermute | solution.py:53
  47.0 9.2 %collective-permute-start.6 = (bf16[128,2048]{1,0:T(8,128)(2,1)S(1)}, bf16[128,2048]{1,0:T(8,128)(2,1)S(1)}, u32[]{:S(2)}, u32[]{:S(2)}) collective-permute-start(bf16[128,2048]{1,0:T(8,128)(2,1)S(1)} %get-tuple-element.65), channel_id=1, source_target_pairs={{0,3},{1,0},{2,1},{3,2},{4,7},{5,4},{6,5},{7,6},{8,11},{9,8},{10,9... | collective-permute-start | bytes 1572872 | tf_op jit(solution)/shard_map/ppermute | solution.py:53
  51.2 1.3 %copy-start.2 = (bf16[2048,512]{1,0:T(8,128)(2,1)}, bf16[2048,512]{1,0:T(8,128)(2,1)S(1)}, u32[]{:S(2)}) copy-start(bf16[2048,512]{1,0:T(8,128)(2,1)S(1)} %shard_map.86.token_ref) | copy-start | bytes 6291460
  52.5 19.8 %copy-start.4 = (bf16[1,8,2048]{2,1,0:T(8,128)(2,1)S(1)}, bf16[1,8,2048]{2,1,0:T(8,128)(2,1)}, u32[]{:S(2)}) copy-start(bf16[1,8,2048]{2,1,0:T(8,128)(2,1)} %param.6) | copy-start | bytes 98308
  52.5 19.8 %copy-start.5 = (f32[1,2048]{1,0:T(1,128)S(1)}, f32[1,2048]{1,0:T(1,128)}, u32[]{:S(2)}) copy-start(f32[1,2048]{1,0:T(1,128)} %bias_ref.1) | copy-start | bytes 24580
  89.6 11.2 %collective-permute-start.10 = (bf16[128,2176]{1,0:T(8,128)(2,1)S(1)}, bf16[128,2176]{1,0:T(8,128)(2,1)S(1)}, u32[]{:S(2)}, u32[]{:S(2)}) collective-permute-start(bf16[128,2176]{1,0:T(8,128)(2,1)S(1)} %bitcast.29), channel_id=1, source_target_pairs={{0,1},{1,2},{2,3},{3,0},{4,5},{5,6},{6,7},{7,4},{8,9},{9,10},{10,1... | collective-permute-start | bytes 1671176 | tf_op jit(solution)/shard_map/ppermute | solution.py:49
  89.6 11.2 %collective-permute-start.8 = (bf16[128,2176]{1,0:T(8,128)(2,1)S(1)}, bf16[128,2176]{1,0:T(8,128)(2,1)S(1)}, u32[]{:S(2)}, u32[]{:S(2)}) collective-permute-start(bf16[128,2176]{1,0:T(8,128)(2,1)S(1)} %bitcast.30), channel_id=1, source_target_pairs={{0,3},{1,0},{2,1},{3,2},{4,7},{5,4},{6,5},{7,6},{8,11},{9,8},{10,9... | collective-permute-start | bytes 1671176 | tf_op jit(solution)/shard_map/ppermute | solution.py:49
  93.5 8.7 %collective-permute-start.9 = (bf16[128,2176]{1,0:T(8,128)(2,1)S(1)}, bf16[128,2176]{1,0:T(8,128)(2,1)S(1)}, u32[]{:S(2)}, u32[]{:S(2)}) collective-permute-start(bf16[128,2176]{1,0:T(8,128)(2,1)S(1)} %bitcast.31), channel_id=1, source_target_pairs={{0,16},{1,17},{2,18},{3,19},{4,20},{5,21},{6,22},{7,23},{8,24},{9,... | collective-permute-start | bytes 1671176 | tf_op jit(solution)/shard_map/ppermute | solution.py:49
  104.4 13.2 %collective-permute-start.12 = (f32[384,1024]{1,0:T(8,128)S(1)}, f32[384,1024]{1,0:T(8,128)}, u32[]{:S(2)}, u32[]{:S(2)}) collective-permute-start(f32[384,1024]{1,0:T(8,128)S(1)} %fusion.16), channel_id=1, source_target_pairs={{0,64},{64,0},{1,65},{65,1},{2,66},{66,2},{3,67},{67,3},{4,68},{68... | collective-permute-start | bytes 4718600 | tf_op jit(solution)/shard_map/ppermute | solution.py:57
  110.7 5.5 %collective-permute-start.11 = (f32[128,1024]{1,0:T(8,128)S(1)}, f32[128,1024]{1,0:T(8,128)S(1)}, u32[]{:S(2)}, u32[]{:S(2)}) collective-permute-start(f32[128,1024]{1,0:T(8,128)S(1)} %broadcast_add_fusion), channel_id=1, source_target_pairs={{0,64},{64,0},{1,65},{65,1},{2,66},{66,2},{3,67},{67,3},{4,68},{68... | collective-permute-start | bytes 1572872 | tf_op jit(solution)/shard_map/ppermute | solution.py:57
  111.5 4.8 %collective-permute-start.13 = (f32[]{:T(128)}, f32[]{:T(128)}, u32[]{:S(2)}, u32[]{:S(2)}) collective-permute-start(f32[]{:T(128)} %bitcast.11), channel_id=1, source_target_pairs={{0,64},{64,0},{1,65},{65,1},{2,66},{66,2},{3,67},{67,3},{4,68},{68... | collective-permute-start | bytes 20 | tf_op jit(solution)/shard_map/ppermute | solution.py:57
  119.5 1.6 %copy-start.3 = (bf16[2048,512]{1,0:T(8,128)(2,1)S(1)}, bf16[2048,512]{1,0:T(8,128)(2,1)}, u32[]{:S(2)}) copy-start(bf16[2048,512]{1,0:T(8,128)(2,1)} %copy-done.2) | copy-start | bytes 6291460

commit v4 on v3

--- a/solution.py
+++ b/solution.py
@@ -160,28 +160,6 @@
     return grad + SPARSITY * norm
 
 
-def loss_kernel(*refs):
-    errors, out_ref = refs[:-1], refs[-1]
-    total = jnp.zeros((1, EXTRA), F32)
-    for ref in errors:
-        total = total + jnp.sum(ref[...].astype(F32), axis=0, keepdims=True)
-    out_ref[0, 0] = jnp.sum(total)
-
-
-def layer_loss(errors, features):
-    rows = errors[0].shape[0]
-    spec = pl.BlockSpec((rows, EXTRA), lambda i: (0, features // EXTRA))
-    loss = pl.pallas_call(
-        loss_kernel,
-        out_shape=jax.ShapeDtypeStruct((1, 1), F32),
-        grid=(1,),
-        in_specs=[spec] * len(errors),
-        out_specs=pl.BlockSpec(memory_space=pltpu.SMEM),
-        compiler_params=params(),
-    )(*errors)
-    return loss[0, 0]
-
-
 def transpose_kernel(*refs):
     parts, out_ref = refs[:-1], refs[-1]
     start = 0
@@ -205,14 +183,18 @@
     )(*parts)
 
 
-def grad_dec_kernel(code_ref, e0, e1, e2, e3, scale_ref, weight_ref, out_ref, joined):
+def grad_dec_kernel(code_ref, e0, e1, e2, e3, scale_ref, weight_ref, out_ref, loss_ref, joined):
     rows = e0.shape[0]
     features = weight_ref.shape[1]
 
     @pl.when(pl.program_id(0) == 0)
     def _():
+        loss = jnp.zeros((rows, EXTRA), F32)
         for i, ref in enumerate((e0, e1, e2, e3)):
             joined[i * rows : (i + 1) * rows, :] = ref[:, :features]
+            loss = loss + ref[:, features:].astype(F32)
+        loss = jnp.sum(jnp.sum(loss, axis=0, keepdims=True), axis=1, keepdims=True)
+        loss_ref[...] = jnp.broadcast_to(loss, loss_ref.shape)
 
     grad = jnp.dot(code_ref[...], joined[...], preferred_element_type=F32)
     shrink = scale_ref[:, :1] * weight_ref[...].astype(F32)
@@ -225,7 +207,10 @@
     rows, width = errors[0].shape
     return pl.pallas_call(
         grad_dec_kernel,
-        out_shape=jax.ShapeDtypeStruct((latents, features), BF16),
+        out_shape=(
+            jax.ShapeDtypeStruct((latents, features), BF16),
+            jax.ShapeDtypeStruct((8, EXTRA), F32),
+        ),
         grid=(latents // block,),
         in_specs=[pl.BlockSpec((block, tokens), lambda i: (i, 0))]
         + [whole((rows, width))] * 4
@@ -233,31 +218,14 @@
             pl.BlockSpec((block, 128), lambda i: (i, 0)),
             pl.BlockSpec((block, features), lambda i: (i, 0)),
         ],
-        out_specs=pl.BlockSpec((block, features), lambda i: (i, 0)),
+        out_specs=(
+            pl.BlockSpec((block, features), lambda i: (i, 0)),
+            whole((8, EXTRA)),
+        ),
         scratch_shapes=[pltpu.VMEM((tokens, features), BF16)],
         cost_estimate=cost(2 * tokens * features * latents, code_t, *errors, weight, weight),
         compiler_params=params(),
     )(code_t, *errors, scale, weight)
-
-
-def grad_enc_kernel(token_ref, pre_grad_ref, out_ref):
-    out_ref[...] = jnp.dot(
-        token_ref[...], pre_grad_ref[...], preferred_element_type=F32
-    ).astype(BF16)
-
-
-def grad_encoder(token_t, pre_grad, block=512):
-    features, tokens = token_t.shape
-    latents = pre_grad.shape[1]
-    return pl.pallas_call(
-        grad_enc_kernel,
-        out_shape=jax.ShapeDtypeStruct((features, latents), BF16),
-        grid=(features // block,),
-        in_specs=[pl.BlockSpec((block, tokens), lambda i: (i, 0)), whole(pre_grad.shape)],
-        out_specs=pl.BlockSpec((block, latents), lambda i: (i, 0)),
-        cost_estimate=cost(2 * tokens * features * latents, token_t, token_t, pre_grad),
-        compiler_params=params(),
-    )(token_t, pre_grad)
 
 
 def per_device(activations, enc_weight, enc_bias, dec_weight, dec_bias, active_mask):
@@ -270,9 +238,10 @@
     quarter = members * own
     bias = enc_bias[None]
 
+    place = [lax.axis_index(name) for name in LATENT]
+    rows, place = lax.optimization_barrier((rows, place))
     q0 = class_exchange(jnp.broadcast_to(rows[None], (members, own, features)))
     q0 = q0.reshape(quarter, features)
-    place = [lax.axis_index(name) for name in LATENT]
     q0, active_mask, decoder, place = lax.optimization_barrier(
         (q0, active_mask, decoder, place)
     )
@@ -290,35 +259,37 @@
     total123 = jnp.sum(latent_code, axis=0, keepdims=True)
     code123 = latent_code.astype(BF16)
     parts = jnp.dot(code123, decoder, preferred_element_type=F32).astype(BF16)
-    parts, all_tokens = lax.optimization_barrier((parts, [q0, *q123]))
     received = to_neighbours(parts.reshape(3, quarter, features))
     latent_code = (pre0 + other0 + bias) * gate[:quarter].astype(F32)
     total0 = jnp.sum(latent_code, axis=0, keepdims=True)
     code0 = latent_code.astype(BF16)
     part0 = jnp.dot(code0, decoder, preferred_element_type=F32)
-    token_t = transposed(all_tokens)
     code_t = transposed([code0, code123])
-    received, part0, token_t, code_t = lax.optimization_barrier((received, part0, token_t, code_t))
+    received, part0, code_t = lax.optimization_barrier((received, part0, code_t))
     partial = add_quarters(part0, received)
     parts = class_exchange(partial.reshape(members, own, features))
     sent = error_blocks(parts, rows, dec_bias, total0, total123, row_norm[None])
 
     e0 = class_exchange(sent).reshape(quarter, features + EXTRA)
+    e0, all_tokens = lax.optimization_barrier((e0, [q0, *q123]))
     e123 = from_neighbours(e0)
+    token_t = transposed(all_tokens)
     norm = row_norm[None]
     grad0 = code_gradient(e0[:, :features], norm, decoder)
     grad_other0 = swap_layers(grad0)
     scale = SPARSITY * (total0 + total123)[0] / row_norm
     scale = jnp.broadcast_to(scale[:, None], (latents, 128))
-    e123, grad0, code_t, scale = lax.optimization_barrier((e123, grad0, code_t, scale))
+    e123, grad0, grad_other0, token_t, scale = lax.optimization_barrier(
+        (e123, grad0, grad_other0, token_t, scale)
+    )
     grad123 = code_gradient(jnp.concatenate([x[:, :features] for x in e123]), norm, decoder)
     grad_other123 = swap_layers(grad123)
-    loss = layer_loss([e0, *e123], features)
-    loss = loss + swap_layers(loss)
-    grad_dec = grad_decoder(code_t, [e0, *e123], scale, decoder)
+    grad_dec, loss = grad_decoder(code_t, [e0, *e123], scale, decoder)
+    loss = (loss + swap_layers(loss))[0, 0]
     pre_grad0 = ((grad0 + grad_other0) * gate[:quarter].astype(F32)).astype(BF16)
     pre_grad123 = ((grad123 + grad_other123) * gate[quarter:].astype(F32)).astype(BF16)
-    grad_enc = grad_encoder(token_t, jnp.concatenate([pre_grad0, pre_grad123]))
+    pre_grad = jnp.concatenate([pre_grad0, pre_grad123])
+    grad_enc = jnp.dot(token_t, pre_grad, preferred_element_type=F32).astype(BF16)
     return (grad_enc[None], grad_dec[None], loss / (tokens * features))
 
 

time: 127 us -> 121 us (0.953)
  matrix products: 8.42 us -> 15.1 us
  Pallas kernels: 11.7 us -> 7.05 us
  blocking collectives: 32.8 us -> 37.1 us
  starting transfers between devices: 30.1 us -> 25.9 us
  waiting for transfers between devices: 29.1 us -> 25.6 us
  local copies, waits for them, and re-layouts: 4.97 us -> 2.75 us
  other arithmetic: 5.89 us -> 4.43 us
    ppermute x6, waiting for transfers between devices: 11.7 us -> 5.68 us  [from_neighbours(): return [lax.ppermute(x, EVERY, moved(r, -1)) for r in (1, 2, 3)]]
    all_to_all x1, starting transfers between devices: 10.9 us -> 5.37 us  [class_exchange(): lax.all_to_all(x, LATENT, 0, 0, axis_index_groups=class_groups(), tiled=T...]
    pallas_call x3 -> x1, Pallas kernels: 9.03 us -> 4.36 us  [grad_decoder(): pl.pallas_call(grad_dec_kernel, out_shape=(jax.ShapeDtypeStruct((latents,...]
    dot_general x0 -> x1, matrix products: none -> 4.36 us  [per_device(): jnp.dot(token_t, pre_grad, preferred_element_type=F32).astype(BF16)]
    all_to_all x2, blocking collectives: 32.8 us -> 37.1 us  [class_exchange(): lax.all_to_all(x, LATENT, 0, 0, axis_index_groups=class_groups(), tiled=T...]
    dot_general x2, matrix products: 3.35 us -> 5.64 us  [code_gradient(): grad = jnp.einsum('td,fd->tf', error, weight, preferred_element_type=F32)]
    ppermute x3, waiting for transfers between devices: 3.75 us -> 6.03 us  [to_neighbours(): lax.ppermute(x, EVERY, moved(r, 1))]
    unnamed x16 -> x28, local copies, waits for them, and re-layouts: 2.92 us -> 0.93 us
  transfers between devices with their start and end apart: 15 -> 15, of which waited for: 9 -> 10; matrix products, arithmetic and copies ran while one was open for 7% -> 10% of each run, Pallas kernels for 6% -> 5%
where the time goes in v4:
time: 121 us
  blocking collectives  37.1 us (31%)
  starting transfers between devices  25.9 us (21%)
  waiting for transfers between devices  25.6 us (21%)
  matrix products  15.1 us (12%)
  Pallas kernels  7.05 us (6%)
  other arithmetic  4.43 us (4%)
  local copies, waits for them, and re-layouts  2.75 us (2%)
  between operations  2.72 us (2%)
    all_to_all x2, blocking collectives, class_exchange(): lax.all_to_all(x, LATENT, 0, 0, axis_index_groups=class_groups(), tiled=T...  37.1 us
    all_to_all x1, waiting for transfers between devices, class_exchange(): lax.all_to_all(x, LATENT, 0, 0, axis_index_groups=class_groups(), tiled=T...  9.37 us
    ppermute x5, starting transfers between devices, swap_layers(): return lax.ppermute(x, 'layer', [(0, 1), (1, 0)])  9.25 us
    ppermute x6, starting transfers between devices, from_neighbours(): return [lax.ppermute(x, EVERY, moved(r, -1)) for r in (1, 2, 3)]  8.35 us
    ppermute x3, waiting for transfers between devices, to_neighbours(): lax.ppermute(x, EVERY, moved(r, 1))  6.03 us
    ppermute x6, waiting for transfers between devices, from_neighbours(): return [lax.ppermute(x, EVERY, moved(r, -1)) for r in (1, 2, 3)]  5.68 us
    dot_general x2, matrix products, code_gradient(): grad = jnp.einsum('td,fd->tf', error, weight, preferred_element_type=F32)  5.64 us
    all_to_all x1, starting transfers between devices, class_exchange(): lax.all_to_all(x, LATENT, 0, 0, axis_index_groups=class_groups(), tiled=T...  5.37 us
  transfers between devices with their start and end apart: 15, of which 10 were waited for; matrix products, arithmetic and copies ran while one was open for 10% of the time, Pallas kernels for 5%

profile of v4, /device:TPU:1, one launch (start us, length us, event | category | flops | bytes accessed | tf_op | source)
XLA Modules:
  0.0 120.7 jit_solution(14877248120208974053)
XLA Ops:
  1.4 21.4 %all_to_all.15 = bf16[16,8,2048]{2,1,0:T(8,128)(2,1)S(1)} all-to-all(bf16[16,8,2048]{2,1,0:T(8,128)(2,1)S(1)} %broadcast_in_dim.14), channel_id=1, replica_groups={{0,7,10,13,18,21,24,31,32,39,42,45,50,53,56,63},{1,4,11,14,19,22,25,28,..., dimensions={0} | all-to-all | bytes 1048576 | tf_op jit(solution)/shard_map/all_to_all | solution.py:45
  22.8 3.1 %collective-permute-start.1 = (bf16[128,2048]{1,0:T(8,128)(2,1)S(1)}, bf16[128,2048]{1,0:T(8,128)(2,1)S(1)}, u32[]{:S(2)}, u32[]{:S(2)}) collective-permute-start(bf16[128,2048]{1,0:T(8,128)(2,1)S(1)} %bitcast.37), channel_id=1, source_target_pairs={{0,16},{1,17},{2,18},{3,19},{4,20},{5,21},{6,22},{7,23},{8,24},{9,... | collective-permute-start | bytes 1572872 | tf_op jit(solution)/shard_map/ppermute | solution.py:49
  26.0 3.2 %multiply_reduce_fusion = f32[1024]{0:T(1024)S(1)} fusion(bf16[1024,2048]{1,0:T(8,128)(2,1)} %bitcast.25), kind=kLoop, calls=%fused_computation | loop fusion | flops 6290432 | bytes 4198400 | tf_op jit(solution)/shard_map/reduce_sum | solution.py:253
  31.1 0.9 collective-permute-done.1.refs_2_
  32.1 3.4 %collective-permute-done.2.refs_3_ = bf16[128,2048]{1,0:T(8,128)(2,1)S(1)} collective-permute-done((bf16[128,2048]{1,0:T(8,128)(2,1)S(1)}, bf16[128,2048]{1,0:T(8,128)(2,1)S(1)}, u32[]{:S(2)}, u32[]{:S(2)}) %collective-permute-start.2) | collective-permute-done | bytes 524320 | tf_op jit(solution)/shard_map/ppermute | solution.py:49
  35.5 1.8 %fusion = f32[384,1024]{1,0:T(8,128)S(1)} fusion(bf16[1,2048,1024]{2,1,0:T(8,128)(2,1)S(1)} %copy-done.12, bf16[128,2048]{1,0:T(8,128)(2,1)S(1)} %collective-permute-done.2.refs_3_, bf16[128,2048]{1,0:T(8,128)(2,1)S(1)} %collective-permute-done.1.refs_2_, bf16[128,2048]{1,0:T(8,128)(2,1)S(1)} %collective-permute-done.refs_1_), kind=kOutput, calls=%fused_computation.1 | convolution fusion | flops 1615331328 | bytes 7340032 | tf_op jit(solution)/shard_map/dot_general | solution.py:255
  37.4 2.1 %collective-permute-start.3 = (f32[384,1024]{1,0:T(8,128)S(1)}, f32[384,1024]{1,0:T(8,128)S(1)}, u32[]{:S(2)}, u32[]{:S(2)}) collective-permute-start(f32[384,1024]{1,0:T(8,128)S(1)} %fusion), channel_id=1, source_target_pairs={{0,64},{64,0},{1,65},{65,1},{2,66},{66,2},{3,67},{67,3},{4,68},{68... | collective-permute-start | bytes 4718600 | tf_op jit(solution)/shard_map/ppermute | solution.py:57
  39.6 2.9 %collective-permute-done.3 = f32[384,1024]{1,0:T(8,128)S(1)} collective-permute-done((f32[384,1024]{1,0:T(8,128)S(1)}, f32[384,1024]{1,0:T(8,128)S(1)}, u32[]{:S(2)}, u32[]{:S(2)}) %collective-permute-start.3) | collective-permute-done | bytes 1572896 | tf_op jit(solution)/shard_map/ppermute | solution.py:57
  43.0 1.8 %convolution_convert_fusion = bf16[384,2048]{1,0:T(8,128)(2,1)S(1)} fusion(bf16[384,1024]{1,0:T(8,128)(2,1)S(1)} %get-tuple-element.74.refs_1_, bf16[1024,2048]{1,0:T(8,128)(2,1)S(1)} %bitcast.27), kind=kOutput, calls=%fused_computation.6 | convolution fusion | flops 1611399168 | bytes 6553600 | tf_op jit(solution)/shard_map/dot_general | solution.py:261
  46.2 1.8 %collective-permute-start.6 = (bf16[128,2048]{1,0:T(8,128)(2,1)S(1)}, bf16[128,2048]{1,0:T(8,128)(2,1)S(1)}, u32[]{:S(2)}, u32[]{:S(2)}) collective-permute-start(bf16[128,2048]{1,0:T(8,128)(2,1)S(1)} %get-tuple-element.77), channel_id=1, source_target_pairs={{0,3},{1,0},{2,1},{3,2},{4,7},{5,4},{6,5},{7,6},{8,11},{9,8},{10,9... | collective-permute-start | bytes 1572872 | tf_op jit(solution)/shard_map/ppermute | solution.py:53
  49.4 5.3 %collective-permute-done.4.a_ref = bf16[128,2048]{1,0:T(8,128)(2,1)S(1)} collective-permute-done((bf16[128,2048]{1,0:T(8,128)(2,1)S(1)}, bf16[128,2048]{1,0:T(8,128)(2,1)S(1)}, u32[]{:S(2)}, u32[]{:S(2)}) %collective-permute-start.4) | collective-permute-done | bytes 524320 | tf_op jit(solution)/shard_map/ppermute | solution.py:53
  55.7 15.8 %all_to_all.16.parts_ref = bf16[16,8,2048]{2,1,0:T(8,128)(2,1)S(1)} all-to-all(bf16[16,8,2048]{2,1,0:T(8,128)(2,1)S(1)} %bitcast.41), channel_id=1, replica_groups={{0,7,10,13,18,21,24,31,32,39,42,45,50,53,56,63},{1,4,11,14,19,22,25,28,..., dimensions={0} | all-to-all | bytes 1048576 | tf_op jit(solution)/shard_map/all_to_all | solution.py:45
  72.5 5.4 %all-to-all-start.2 = ((bf16[16,8,2176]{2,1,0:T(8,128)(2,1)}), bf16[16,8,2176]{2,1,0:T(8,128)(2,1)S(1)}, u32[]{:S(2)}, u32[]{:S(2)}) async-start(bf16[16,8,2176]{2,1,0:T(8,128)(2,1)} %copy-done.2), calls=%async_computation.2 | async-start | bytes 1114112 | tf_op jit(solution)/shard_map/all_to_all | solution.py:45
  77.9 9.4 %all-to-all-done.2 = bf16[16,8,2176]{2,1,0:T(8,128)(2,1)S(1)} async-done(((bf16[16,8,2176]{2,1,0:T(8,128)(2,1)}), bf16[16,8,2176]{2,1,0:T(8,128)(2,1)S(1)}, u32[]{:S(2)}, u32[]{:S(2)}) %all-to-all-start.2) | async-done | bytes 557088 | tf_op jit(solution)/shard_map/all_to_all | solution.py:45
  87.3 4.4 %collective-permute-start.8 = (bf16[128,2176]{1,0:T(8,128)(2,1)S(1)}, bf16[128,2176]{1,0:T(8,128)(2,1)S(1)}, u32[]{:S(2)}, u32[]{:S(2)}) collective-permute-start(bf16[128,2176]{1,0:T(8,128)(2,1)S(1)} %bitcast.31), channel_id=1, source_target_pairs={{0,3},{1,0},{2,1},{3,2},{4,7},{5,4},{6,5},{7,6},{8,11},{9,8},{10,9... | collective-permute-start | bytes 1671176 | tf_op jit(solution)/shard_map/ppermute | solution.py:49
  92.5 3.8 %broadcast_add_fusion = f32[128,1024]{1,0:T(8,128)S(1)} fusion(f32[1024]{0:T(1024)S(1)} %get-tuple-element.81, bf16[1024,2048]{1,0:T(8,128)(2,1)} %bitcast.26, bf16[128,2176]{1,0:T(8,128)(2,1)S(1)} %bitcast.34), kind=kOutput, calls=%fused_computation.30 | convolution fusion | flops 537001984 | bytes 5246976 | tf_op jit(solution)/shard_map/td,fd->tf/dot_general | solution.py:159
  96.3 2.7 %collective-permute-start.11 = (f32[128,1024]{1,0:T(8,128)S(1)}, f32[128,1024]{1,0:T(8,128)S(1)}, u32[]{:S(2)}, u32[]{:S(2)}) collective-permute-start(f32[128,1024]{1,0:T(8,128)S(1)} %broadcast_add_fusion), channel_id=1, source_target_pairs={{0,64},{64,0},{1,65},{65,1},{2,66},{66,2},{3,67},{67,3},{4,68},{68... | collective-permute-start | bytes 1572872 | tf_op jit(solution)/shard_map/ppermute | solution.py:57
  99.0 1.0 shard_map.89
  100.5 1.0 collective-permute-done.10.e3
  101.9 1.8 %fusion.16 = f32[384,1024]{1,0:T(8,128)S(1)} fusion(bf16[1024,2048]{1,0:T(8,128)(2,1)S(1)} %bitcast.29, bf16[128,2048]{1,0:T(8,128)(2,1)S(1)} %slice.31, bf16[128,2048]{1,0:T(8,128)(2,1)S(1)} %slice.30, bf16[128,2048]{1,0:T(8,128)(2,1)S(1)} %slice.29, f32[1024]{0:T(1024)S(1)} %get-tuple-element.81), kind=kOutput, calls=%fused_computation.21 | convolution fusion | flops 1615724544 | bytes 7344128 | tf_op jit(solution)/shard_map/td,fd->tf/dot_general | solution.py:159
  103.8 4.3 %collective-permute-start.12 = (f32[384,1024]{1,0:T(8,128)S(1)}, f32[384,1024]{1,0:T(8,128)S(1)}, u32[]{:S(2)}, u32[]{:S(2)}) collective-permute-start(f32[384,1024]{1,0:T(8,128)S(1)} %fusion.16), channel_id=1, source_target_pairs={{0,64},{64,0},{1,65},{65,1},{2,66},{66,2},{3,67},{67,3},{4,68},{68... | collective-permute-start | bytes 4718600 | tf_op jit(solution)/shard_map/ppermute | solution.py:57
  108.1 4.4 %shard_map.90 = (bf16[1024,2048]{1,0:T(8,128)(2,1)}, f32[8,128]{1,0:T(8,128)S(1)}) custom-call(bf16[1024,512]{1,0:T(8,128)(2,1)S(1)} %shard_map.86.code_ref, bf16[128,2176]{1,0:T(8,128)(2,1)S(1)} %bitcast.35, bf16[128,2176]{1,0:T(8,128)(2,1)S(1)} %collective-permute-done.8.e1, bf16[128,2176]{1,0:T(8,128)(2,1)S(1)} %collective-permute-done.9.e2, ...), custom_call_target="tpu_custom_call" | custom-call | flops 2147483648 | bytes 11665408 | tf_op jit(solution)/shard_map/pallas_call | solution.py:208
  112.6 1.0 collective-permute-done.13
  115.2 4.4 %convert_bitcast_fusion = bf16[1,2048,1024]{2,1,0:T(8,128)(2,1)} fusion(bf16[2048,512]{1,0:T(8,128)(2,1)S(1)} %shard_map.89, bf16[384,1024]{1,0:T(8,128)(2,1)S(1)} %fusion.4, bf16[128,1024]{1,0:T(8,128)(2,1)S(1)} %fusion.22), kind=kOutput, calls=%fused_computation.5 | convolution fusion | flops 2151677952 | bytes 7340032 | tf_op jit(solution)/shard_map/dot_general | solution.py:292
  (65 shorter events, 10.9 us)
Async XLA Ops:
  22.8 8.3 %collective-permute-start = (bf16[128,2048]{1,0:T(8,128)(2,1)S(1)}, bf16[128,2048]{1,0:T(8,128)(2,1)S(1)}, u32[]{:S(2)}, u32[]{:S(2)}) collective-permute-start(bf16[128,2048]{1,0:T(8,128)(2,1)S(1)} %bitcast.36), channel_id=1, source_target_pairs={{0,3},{1,0},{2,1},{3,2},{4,7},{5,4},{6,5},{7,6},{8,11},{9,8},{10,9... | collective-permute-start | bytes 1572872 | tf_op jit(solution)/shard_map/ppermute | solution.py:49
  22.8 9.3 %collective-permute-start.1 = (bf16[128,2048]{1,0:T(8,128)(2,1)S(1)}, bf16[128,2048]{1,0:T(8,128)(2,1)S(1)}, u32[]{:S(2)}, u32[]{:S(2)}) collective-permute-start(bf16[128,2048]{1,0:T(8,128)(2,1)S(1)} %bitcast.37), channel_id=1, source_target_pairs={{0,16},{1,17},{2,18},{3,19},{4,20},{5,21},{6,22},{7,23},{8,24},{9,... | collective-permute-start | bytes 1572872 | tf_op jit(solution)/shard_map/ppermute | solution.py:49
  25.9 9.5 %collective-permute-start.2 = (bf16[128,2048]{1,0:T(8,128)(2,1)S(1)}, bf16[128,2048]{1,0:T(8,128)(2,1)S(1)}, u32[]{:S(2)}, u32[]{:S(2)}) collective-permute-start(bf16[128,2048]{1,0:T(8,128)(2,1)S(1)} %bitcast.38), channel_id=1, source_target_pairs={{0,1},{1,2},{2,3},{3,0},{4,5},{5,6},{6,7},{7,4},{8,9},{9,10},{10,1... | collective-permute-start | bytes 1572872 | tf_op jit(solution)/shard_map/ppermute | solution.py:49
  30.8 11.7 %copy-start.13 = (f32[1024]{0:T(1024)S(1)}, f32[1024]{0:T(1024)}, u32[]{:S(2)}) copy-start(f32[1024]{0:T(1024)} %param.8) | copy-start | bytes 12292
  31.1 6.2 %copy-start.4 = (bf16[128,2048]{1,0:T(8,128)(2,1)}, bf16[128,2048]{1,0:T(8,128)(2,1)S(1)}, u32[]{:S(2)}) copy-start(bf16[128,2048]{1,0:T(8,128)(2,1)S(1)} %collective-permute-done.refs_1_) | copy-start | bytes 1572868
  32.1 5.3 %copy-start.6 = (bf16[128,2048]{1,0:T(8,128)(2,1)}, bf16[128,2048]{1,0:T(8,128)(2,1)S(1)}, u32[]{:S(2)}) copy-start(bf16[128,2048]{1,0:T(8,128)(2,1)S(1)} %collective-permute-done.1.refs_2_) | copy-start | bytes 1572868
  37.4 5.7 %copy-start = (bf16[1,1024,2048]{2,1,0:T(8,128)(2,1)S(1)}, bf16[1,1024,2048]{2,1,0:T(8,128)(2,1)}, u32[]{:S(2)}) copy-start(bf16[1,1024,2048]{2,1,0:T(8,128)(2,1)} %param.9) | copy-start | bytes 12582916
  37.4 5.1 %collective-permute-start.3 = (f32[384,1024]{1,0:T(8,128)S(1)}, f32[384,1024]{1,0:T(8,128)S(1)}, u32[]{:S(2)}, u32[]{:S(2)}) collective-permute-start(f32[384,1024]{1,0:T(8,128)S(1)} %fusion), channel_id=1, source_target_pairs={{0,64},{64,0},{1,65},{65,1},{2,66},{66,2},{3,67},{67,3},{4,68},{68... | collective-permute-start | bytes 4718600 | tf_op jit(solution)/shard_map/ppermute | solution.py:57
  39.5 8.5 %collective-permute-start.7 = (f32[128,1024]{1,0:T(8,128)S(1)}, f32[128,1024]{1,0:T(8,128)S(1)}, u32[]{:S(2)}, u32[]{:S(2)}) collective-permute-start(f32[128,1024]{1,0:T(8,128)S(1)} %fusion.2), channel_id=1, source_target_pairs={{0,64},{64,0},{1,65},{65,1},{2,66},{66,2},{3,67},{67,3},{4,68},{68... | collective-permute-start | bytes 1572872 | tf_op jit(solution)/shard_map/ppermute | solution.py:57
  45.0 9.6 %collective-permute-start.4 = (bf16[128,2048]{1,0:T(8,128)(2,1)S(1)}, bf16[128,2048]{1,0:T(8,128)(2,1)S(1)}, u32[]{:S(2)}, u32[]{:S(2)}) collective-permute-start(bf16[128,2048]{1,0:T(8,128)(2,1)S(1)} %get-tuple-element.79), channel_id=1, source_target_pairs={{0,1},{1,2},{2,3},{3,0},{4,5},{5,6},{6,7},{7,4},{8,9},{9,10},{10,1... | collective-permute-start | bytes 1572872 | tf_op jit(solution)/shard_map/ppermute | solution.py:53
  45.6 9.8 %collective-permute-start.5 = (bf16[128,2048]{1,0:T(8,128)(2,1)S(1)}, bf16[128,2048]{1,0:T(8,128)(2,1)S(1)}, u32[]{:S(2)}, u32[]{:S(2)}) collective-permute-start(bf16[128,2048]{1,0:T(8,128)(2,1)S(1)} %get-tuple-element.78), channel_id=1, source_target_pairs={{0,48},{1,49},{2,50},{3,51},{4,52},{5,53},{6,54},{7,55},{8,56},{9,... | collective-permute-start | bytes 1572872 | tf_op jit(solution)/shard_map/ppermute | solution.py:53
  46.2 9.2 %collective-permute-start.6 = (bf16[128,2048]{1,0:T(8,128)(2,1)S(1)}, bf16[128,2048]{1,0:T(8,128)(2,1)S(1)}, u32[]{:S(2)}, u32[]{:S(2)}) collective-permute-start(bf16[128,2048]{1,0:T(8,128)(2,1)S(1)} %get-tuple-element.77), channel_id=1, source_target_pairs={{0,3},{1,0},{2,1},{3,2},{4,7},{5,4},{6,5},{7,6},{8,11},{9,8},{10,9... | collective-permute-start | bytes 1572872 | tf_op jit(solution)/shard_map/ppermute | solution.py:53
  49.4 22.1 %copy-start.10 = (bf16[1,8,2048]{2,1,0:T(8,128)(2,1)S(1)}, bf16[1,8,2048]{2,1,0:T(8,128)(2,1)}, u32[]{:S(2)}) copy-start(bf16[1,8,2048]{2,1,0:T(8,128)(2,1)} %param.6) | copy-start | bytes 98308
  49.4 22.1 %copy-start.11 = (f32[1,2048]{1,0:T(1,128)S(1)}, f32[1,2048]{1,0:T(1,128)}, u32[]{:S(2)}) copy-start(f32[1,2048]{1,0:T(1,128)} %bias_ref.1) | copy-start | bytes 24580
  72.5 14.8 %all-to-all-start.2 = ((bf16[16,8,2176]{2,1,0:T(8,128)(2,1)}), bf16[16,8,2176]{2,1,0:T(8,128)(2,1)S(1)}, u32[]{:S(2)}, u32[]{:S(2)}) async-start(bf16[16,8,2176]{2,1,0:T(8,128)(2,1)} %copy-done.2), calls=%async_computation.2 | async-start | bytes 1114112 | tf_op jit(solution)/shard_map/all_to_all | solution.py:45
  87.3 13.3 %collective-permute-start.8 = (bf16[128,2176]{1,0:T(8,128)(2,1)S(1)}, bf16[128,2176]{1,0:T(8,128)(2,1)S(1)}, u32[]{:S(2)}, u32[]{:S(2)}) collective-permute-start(bf16[128,2176]{1,0:T(8,128)(2,1)S(1)} %bitcast.31), channel_id=1, source_target_pairs={{0,3},{1,0},{2,1},{3,2},{4,7},{5,4},{6,5},{7,6},{8,11},{9,8},{10,9... | collective-permute-start | bytes 1671176 | tf_op jit(solution)/shard_map/ppermute | solution.py:49
  91.7 8.9 %collective-permute-start.9 = (bf16[128,2176]{1,0:T(8,128)(2,1)S(1)}, bf16[128,2176]{1,0:T(8,128)(2,1)S(1)}, u32[]{:S(2)}, u32[]{:S(2)}) collective-permute-start(bf16[128,2176]{1,0:T(8,128)(2,1)S(1)} %bitcast.32), channel_id=1, source_target_pairs={{0,16},{1,17},{2,18},{3,19},{4,20},{5,21},{6,22},{7,23},{8,24},{9,... | collective-permute-start | bytes 1671176 | tf_op jit(solution)/shard_map/ppermute | solution.py:49
  91.7 9.9 %collective-permute-start.10 = (bf16[128,2176]{1,0:T(8,128)(2,1)S(1)}, bf16[128,2176]{1,0:T(8,128)(2,1)S(1)}, u32[]{:S(2)}, u32[]{:S(2)}) collective-permute-start(bf16[128,2176]{1,0:T(8,128)(2,1)S(1)} %bitcast.33), channel_id=1, source_target_pairs={{0,1},{1,2},{2,3},{3,0},{4,5},{5,6},{6,7},{7,4},{8,9},{9,10},{10,1... | collective-permute-start | bytes 1671176 | tf_op jit(solution)/shard_map/ppermute | solution.py:49
  92.5 6.5 %copy-start.5 = (bf16[128,2048]{1,0:T(8,128)(2,1)S(1)}, bf16[128,2048]{1,0:T(8,128)(2,1)}, u32[]{:S(2)}) copy-start(bf16[128,2048]{1,0:T(8,128)(2,1)} %copy-done.4) | copy-start | bytes 1572868
  92.5 6.5 %copy-start.7 = (bf16[128,2048]{1,0:T(8,128)(2,1)S(1)}, bf16[128,2048]{1,0:T(8,128)(2,1)}, u32[]{:S(2)}) copy-start(bf16[128,2048]{1,0:T(8,128)(2,1)} %copy-done.6) | copy-start | bytes 1572868
  92.5 6.5 %copy-start.9 = (bf16[128,2048]{1,0:T(8,128)(2,1)S(1)}, bf16[128,2048]{1,0:T(8,128)(2,1)}, u32[]{:S(2)}) copy-start(bf16[128,2048]{1,0:T(8,128)(2,1)} %copy-done.8) | copy-start | bytes 1572868
  96.3 4.2 %collective-permute-start.11 = (f32[128,1024]{1,0:T(8,128)S(1)}, f32[128,1024]{1,0:T(8,128)S(1)}, u32[]{:S(2)}, u32[]{:S(2)}) collective-permute-start(f32[128,1024]{1,0:T(8,128)S(1)} %broadcast_add_fusion), channel_id=1, source_target_pairs={{0,64},{64,0},{1,65},{65,1},{2,66},{66,2},{3,67},{67,3},{4,68},{68... | collective-permute-start | bytes 1572872 | tf_op jit(solution)/shard_map/ppermute | solution.py:57
  103.8 11.0 %collective-permute-start.12 = (f32[384,1024]{1,0:T(8,128)S(1)}, f32[384,1024]{1,0:T(8,128)S(1)}, u32[]{:S(2)}, u32[]{:S(2)}) collective-permute-start(f32[384,1024]{1,0:T(8,128)S(1)} %fusion.16), channel_id=1, source_target_pairs={{0,64},{64,0},{1,65},{65,1},{2,66},{66,2},{3,67},{67,3},{4,68},{68... | collective-permute-start | bytes 4718600 | tf_op jit(solution)/shard_map/ppermute | solution.py:57
  112.4 1.2 collective-permute-start.13
  (5 other events, 12.9 us)

commit v5 on v4

--- a/solution.py
+++ b/solution.py
@@ -183,7 +183,9 @@
     )(*parts)
 
 
-def grad_dec_kernel(code_ref, e0, e1, e2, e3, scale_ref, weight_ref, out_ref, loss_ref, joined):
+def grad_dec_kernel(
+    code_ref, e0, e1, e2, e3, total_a, total_b, norm_ref, weight_ref, out_ref, loss_ref, joined
+):
     rows = e0.shape[0]
     features = weight_ref.shape[1]
 
@@ -197,11 +199,13 @@
         loss_ref[...] = jnp.broadcast_to(loss, loss_ref.shape)
 
     grad = jnp.dot(code_ref[...], joined[...], preferred_element_type=F32)
-    shrink = scale_ref[:, :1] * weight_ref[...].astype(F32)
+    scale = SPARSITY * (total_a[...] + total_b[...]) / norm_ref[...]
+    scale = jnp.broadcast_to(scale, (128, scale.shape[1])).T
+    shrink = scale[:, :1] * weight_ref[...].astype(F32)
     out_ref[...] = (grad + shrink).astype(BF16)
 
 
-def grad_decoder(code_t, errors, scale, weight, block=256):
+def grad_decoder(code_t, errors, terms, weight, block=512):
     latents, features = weight.shape
     tokens = code_t.shape[1]
     rows, width = errors[0].shape
@@ -214,10 +218,8 @@
         grid=(latents // block,),
         in_specs=[pl.BlockSpec((block, tokens), lambda i: (i, 0))]
         + [whole((rows, width))] * 4
-        + [
-            pl.BlockSpec((block, 128), lambda i: (i, 0)),
-            pl.BlockSpec((block, features), lambda i: (i, 0)),
-        ],
+        + [pl.BlockSpec((1, block), lambda i: (0, i))] * 3
+        + [pl.BlockSpec((block, features), lambda i: (i, 0))],
         out_specs=(
             pl.BlockSpec((block, features), lambda i: (i, 0)),
             whole((8, EXTRA)),
@@ -225,7 +227,27 @@
         scratch_shapes=[pltpu.VMEM((tokens, features), BF16)],
         cost_estimate=cost(2 * tokens * features * latents, code_t, *errors, weight, weight),
         compiler_params=params(),
-    )(code_t, *errors, scale, weight)
+    )(code_t, *errors, *terms, weight)
+
+
+def grad_enc_kernel(token_ref, pre_grad_ref, out_ref):
+    out_ref[...] = jnp.dot(
+        token_ref[...], pre_grad_ref[...], preferred_element_type=F32
+    ).astype(BF16)
+
+
+def grad_encoder(token_t, pre_grad, block=1024):
+    features, tokens = token_t.shape
+    latents = pre_grad.shape[1]
+    return pl.pallas_call(
+        grad_enc_kernel,
+        out_shape=jax.ShapeDtypeStruct((features, latents), BF16),
+        grid=(features // block,),
+        in_specs=[pl.BlockSpec((block, tokens), lambda i: (i, 0)), whole(pre_grad.shape)],
+        out_specs=pl.BlockSpec((block, latents), lambda i: (i, 0)),
+        cost_estimate=cost(2 * tokens * features * latents, token_t, token_t, pre_grad),
+        compiler_params=params(),
+    )(token_t, pre_grad)
 
 
 def per_device(activations, enc_weight, enc_bias, dec_weight, dec_bias, active_mask):
@@ -253,7 +275,7 @@
     row_norm = jnp.sqrt(jnp.sum(dec_float * dec_float, axis=1) + 1e-06)
     q123, pre0, gate, row_norm = lax.optimization_barrier((q123, pre0, gate, row_norm))
     pre123 = jnp.dot(jnp.concatenate(q123), encoder, preferred_element_type=F32)
-    other123 = swap_layers(pre123)
+    other123 = swap_layers(pre123.astype(BF16)).astype(F32)
 
     latent_code = (pre123 + other123 + bias) * gate[quarter:].astype(F32)
     total123 = jnp.sum(latent_code, axis=0, keepdims=True)
@@ -277,19 +299,19 @@
     norm = row_norm[None]
     grad0 = code_gradient(e0[:, :features], norm, decoder)
     grad_other0 = swap_layers(grad0)
-    scale = SPARSITY * (total0 + total123)[0] / row_norm
-    scale = jnp.broadcast_to(scale[:, None], (latents, 128))
-    e123, grad0, grad_other0, token_t, scale = lax.optimization_barrier(
-        (e123, grad0, grad_other0, token_t, scale)
+    e123, grad0, grad_other0, token_t = lax.optimization_barrier(
+        (e123, grad0, grad_other0, token_t)
     )
     grad123 = code_gradient(jnp.concatenate([x[:, :features] for x in e123]), norm, decoder)
     grad_other123 = swap_layers(grad123)
-    grad_dec, loss = grad_decoder(code_t, [e0, *e123], scale, decoder)
-    loss = (loss + swap_layers(loss))[0, 0]
+    grad_dec, loss = grad_decoder(code_t, [e0, *e123], (total0, total123, norm), decoder)
+    other_loss = swap_layers(loss)
     pre_grad0 = ((grad0 + grad_other0) * gate[:quarter].astype(F32)).astype(BF16)
     pre_grad123 = ((grad123 + grad_other123) * gate[quarter:].astype(F32)).astype(BF16)
     pre_grad = jnp.concatenate([pre_grad0, pre_grad123])
-    grad_enc = jnp.dot(token_t, pre_grad, preferred_element_type=F32).astype(BF16)
+    grad_enc = grad_encoder(token_t, pre_grad)
+    grad_enc, loss, other_loss = lax.optimization_barrier((grad_enc, loss, other_loss))
+    loss = (loss + other_loss)[0, 0]
     return (grad_enc[None], grad_dec[None], loss / (tokens * features))
 
 

time: 121 us -> 118 us (0.975)
  Pallas kernels: 7.05 us -> 11.5 us
  matrix products: 15.1 us -> 10.7 us
  waiting for transfers between devices: 25.6 us -> 23.6 us
    dot_general x1 -> x0, matrix products: 4.36 us -> none  [per_device(): jnp.dot(token_t, pre_grad, preferred_element_type=F32).astype(BF16)]
    pallas_call x0 -> x1, Pallas kernels: none -> 3.87 us  [grad_encoder(): pl.pallas_call(grad_enc_kernel, out_shape=jax.ShapeDtypeStruct((features,...]
    ppermute x5, waiting for transfers between devices: 4.51 us -> 2.36 us  [swap_layers(): return lax.ppermute(x, 'layer', [(0, 1), (1, 0)])]
  transfers between devices with their start and end apart: 15 -> 15, of which waited for: 10 -> 9; matrix products, arithmetic and copies ran while one was open for 10% -> 10% of each run, Pallas kernels for 5% -> 9%
where the time goes in v5:
time: 118 us
  blocking collectives  37.1 us (31%)
  starting transfers between devices  25.9 us (22%)
  waiting for transfers between devices  23.6 us (20%)
  Pallas kernels  11.5 us (10%)
  matrix products  10.7 us (9%)
  other arithmetic  4.46 us (4%)
  between operations  2.7 us (2%)
  local copies, waits for them, and re-layouts  1.69 us (1%)
    all_to_all x2, blocking collectives, class_exchange(): lax.all_to_all(x, LATENT, 0, 0, axis_index_groups=class_groups(), tiled=T...  37.1 us
    all_to_all x1, waiting for transfers between devices, class_exchange(): lax.all_to_all(x, LATENT, 0, 0, axis_index_groups=class_groups(), tiled=T...  9.37 us
    ppermute x5, starting transfers between devices, swap_layers(): return lax.ppermute(x, 'layer', [(0, 1), (1, 0)])  9.16 us
    ppermute x6, starting transfers between devices, from_neighbours(): return [lax.ppermute(x, EVERY, moved(r, -1)) for r in (1, 2, 3)]  8.43 us
    ppermute x3, waiting for transfers between devices, to_neighbours(): lax.ppermute(x, EVERY, moved(r, 1))  6.02 us
    ppermute x6, waiting for transfers between devices, from_neighbours(): return [lax.ppermute(x, EVERY, moved(r, -1)) for r in (1, 2, 3)]  5.83 us
    dot_general x2, matrix products, code_gradient(): grad = jnp.einsum('td,fd->tf', error, weight, preferred_element_type=F32)  5.53 us
    all_to_all x1, starting transfers between devices, class_exchange(): lax.all_to_all(x, LATENT, 0, 0, axis_index_groups=class_groups(), tiled=T...  5.37 us
  transfers between devices with their start and end apart: 15, of which 9 were waited for; matrix products, arithmetic and copies ran while one was open for 10% of the time, Pallas kernels for 9%

profile of v5, /device:TPU:1, one launch (start us, length us, event | category | flops | bytes accessed | tf_op | source)
XLA Modules:
  0.0 117.6 jit_solution(15336484689440487766)
XLA Ops:
  1.4 21.4 %all_to_all.15 = bf16[16,8,2048]{2,1,0:T(8,128)(2,1)S(1)} all-to-all(bf16[16,8,2048]{2,1,0:T(8,128)(2,1)S(1)} %broadcast_in_dim.23), channel_id=1, replica_groups={{0,7,10,13,18,21,24,31,32,39,42,45,50,53,56,63},{1,4,11,14,19,22,25,28,..., dimensions={0} | all-to-all | bytes 1048576 | tf_op jit(solution)/shard_map/all_to_all | solution.py:45
  22.8 3.1 %collective-permute-start.1 = (bf16[128,2048]{1,0:T(8,128)(2,1)S(1)}, bf16[128,2048]{1,0:T(8,128)(2,1)S(1)}, u32[]{:S(2)}, u32[]{:S(2)}) collective-permute-start(bf16[128,2048]{1,0:T(8,128)(2,1)S(1)} %bitcast.32), channel_id=1, source_target_pairs={{0,16},{1,17},{2,18},{3,19},{4,20},{5,21},{6,22},{7,23},{8,24},{9,... | collective-permute-start | bytes 1572872 | tf_op jit(solution)/shard_map/ppermute | solution.py:49
  26.0 3.2 %multiply_reduce_fusion = f32[1024]{0:T(1024)S(1)} fusion(bf16[1024,2048]{1,0:T(8,128)(2,1)} %bitcast.25), kind=kLoop, calls=%fused_computation | loop fusion | flops 6290432 | bytes 4198400 | tf_op jit(solution)/shard_map/reduce_sum | solution.py:275
  31.1 0.9 collective-permute-done.1.refs_2_
  32.1 3.4 %collective-permute-done.2.refs_3_ = bf16[128,2048]{1,0:T(8,128)(2,1)S(1)} collective-permute-done((bf16[128,2048]{1,0:T(8,128)(2,1)S(1)}, bf16[128,2048]{1,0:T(8,128)(2,1)S(1)}, u32[]{:S(2)}, u32[]{:S(2)}) %collective-permute-start.2) | collective-permute-done | bytes 524320 | tf_op jit(solution)/shard_map/ppermute | solution.py:49
  35.5 1.8 %fusion.34 = (bf16[384,1024]{1,0:T(8,128)(2,1)S(1)}, f32[384,1024]{1,0:T(8,128)S(1)}) fusion(bf16[1,2048,1024]{2,1,0:T(8,128)(2,1)S(1)} %copy-done.11, bf16[128,2048]{1,0:T(8,128)(2,1)S(1)} %collective-permute-done.2.refs_3_, bf16[128,2048]{1,0:T(8,128)(2,1)S(1)} %collective-permute-done.1.refs_2_, bf16[128,2048]{1,0:T(8,128)(2,1)S(1)} %collective-permute-done.refs_1_), kind=kOutput, calls=%fused_computation.54 | convolution fusion | flops 1615724544 | bytes 8126464 | tf_op jit(solution)/shard_map/dot_general | solution.py:277
  37.4 2.1 %collective-permute-start.3 = (bf16[384,1024]{1,0:T(8,128)(2,1)S(1)}, bf16[384,1024]{1,0:T(8,128)(2,1)S(1)}, u32[]{:S(2)}, u32[]{:S(2)}) collective-permute-start(bf16[384,1024]{1,0:T(8,128)(2,1)S(1)} %get-tuple-element.84), channel_id=1, source_target_pairs={{0,64},{64,0},{1,65},{65,1},{2,66},{66,2},{3,67},{67,3},{4,68},{68... | collective-permute-start | bytes 2359304 | tf_op jit(solution)/shard_map/ppermute | solution.py:57
  39.6 1.8 %collective-permute-done.3 = bf16[384,1024]{1,0:T(8,128)(2,1)S(1)} collective-permute-done((bf16[384,1024]{1,0:T(8,128)(2,1)S(1)}, bf16[384,1024]{1,0:T(8,128)(2,1)S(1)}, u32[]{:S(2)}, u32[]{:S(2)}) %collective-permute-start.3) | collective-permute-done | bytes 786464 | tf_op jit(solution)/shard_map/ppermute | solution.py:57
  41.9 1.8 %convolution_convert_fusion = bf16[384,2048]{1,0:T(8,128)(2,1)S(1)} fusion(bf16[384,1024]{1,0:T(8,128)(2,1)S(1)} %get-tuple-element.78.refs_1_, bf16[1024,2048]{1,0:T(8,128)(2,1)S(1)} %bitcast.27), kind=kOutput, calls=%fused_computation.5 | convolution fusion | flops 1611399168 | bytes 6553600 | tf_op jit(solution)/shard_map/dot_general | solution.py:283
  45.0 1.8 %collective-permute-start.6 = (bf16[128,2048]{1,0:T(8,128)(2,1)S(1)}, bf16[128,2048]{1,0:T(8,128)(2,1)S(1)}, u32[]{:S(2)}, u32[]{:S(2)}) collective-permute-start(bf16[128,2048]{1,0:T(8,128)(2,1)S(1)} %get-tuple-element.81), channel_id=1, source_target_pairs={{0,3},{1,0},{2,1},{3,2},{4,7},{5,4},{6,5},{7,6},{8,11},{9,8},{10,9... | collective-permute-start | bytes 1572872 | tf_op jit(solution)/shard_map/ppermute | solution.py:53
  48.2 5.3 %collective-permute-done.4.a_ref = bf16[128,2048]{1,0:T(8,128)(2,1)S(1)} collective-permute-done((bf16[128,2048]{1,0:T(8,128)(2,1)S(1)}, bf16[128,2048]{1,0:T(8,128)(2,1)S(1)}, u32[]{:S(2)}, u32[]{:S(2)}) %collective-permute-start.4) | collective-permute-done | bytes 524320 | tf_op jit(solution)/shard_map/ppermute | solution.py:53
  54.5 15.8 %all_to_all.16.parts_ref = bf16[16,8,2048]{2,1,0:T(8,128)(2,1)S(1)} all-to-all(bf16[16,8,2048]{2,1,0:T(8,128)(2,1)S(1)} %bitcast.41), channel_id=1, replica_groups={{0,7,10,13,18,21,24,31,32,39,42,45,50,53,56,63},{1,4,11,14,19,22,25,28,..., dimensions={0} | all-to-all | bytes 1048576 | tf_op jit(solution)/shard_map/all_to_all | solution.py:45
  70.3 1.0 shard_map.88
  71.3 5.4 %all-to-all-start.2 = ((bf16[16,8,2176]{2,1,0:T(8,128)(2,1)}), bf16[16,8,2176]{2,1,0:T(8,128)(2,1)S(1)}, u32[]{:S(2)}, u32[]{:S(2)}) async-start(bf16[16,8,2176]{2,1,0:T(8,128)(2,1)} %shard_map.88), calls=%async_computation.2 | async-start | bytes 1114112 | tf_op jit(solution)/shard_map/all_to_all | solution.py:45
  76.6 9.4 %all-to-all-done.2 = bf16[16,8,2176]{2,1,0:T(8,128)(2,1)S(1)} async-done(((bf16[16,8,2176]{2,1,0:T(8,128)(2,1)}), bf16[16,8,2176]{2,1,0:T(8,128)(2,1)S(1)}, u32[]{:S(2)}, u32[]{:S(2)}) %all-to-all-start.2) | async-done | bytes 557088 | tf_op jit(solution)/shard_map/all_to_all | solution.py:45
  86.0 4.4 %collective-permute-start.8 = (bf16[128,2176]{1,0:T(8,128)(2,1)S(1)}, bf16[128,2176]{1,0:T(8,128)(2,1)S(1)}, u32[]{:S(2)}, u32[]{:S(2)}) collective-permute-start(bf16[128,2176]{1,0:T(8,128)(2,1)S(1)} %bitcast.36), channel_id=1, source_target_pairs={{0,3},{1,0},{2,1},{3,2},{4,7},{5,4},{6,5},{7,6},{8,11},{9,8},{10,9... | collective-permute-start | bytes 1671176 | tf_op jit(solution)/shard_map/ppermute | solution.py:49
  91.3 3.7 %broadcast_add_fusion = f32[128,1024]{1,0:T(8,128)S(1)} fusion(f32[1024]{0:T(1024)S(1)} %broadcast_multiply_fusion, bf16[1024,2048]{1,0:T(8,128)(2,1)} %bitcast.26, bf16[128,2176]{1,0:T(8,128)(2,1)S(1)} %bitcast.39), kind=kOutput, calls=%fused_computation.29 | convolution fusion | flops 537001984 | bytes 5246976 | tf_op jit(solution)/shard_map/td,fd->tf/dot_general | solution.py:159
  95.0 2.6 %collective-permute-start.11 = (f32[128,1024]{1,0:T(8,128)S(1)}, f32[128,1024]{1,0:T(8,128)S(1)}, u32[]{:S(2)}, u32[]{:S(2)}) collective-permute-start(f32[128,1024]{1,0:T(8,128)S(1)} %broadcast_add_fusion), channel_id=1, source_target_pairs={{0,64},{64,0},{1,65},{65,1},{2,66},{66,2},{3,67},{67,3},{4,68},{68... | collective-permute-start | bytes 1572872 | tf_op jit(solution)/shard_map/ppermute | solution.py:57
  97.6 1.0 shard_map.89.token_ref
  99.2 1.2 collective-permute-done.10.e3
  100.5 1.8 %fusion.16 = f32[384,1024]{1,0:T(8,128)S(1)} fusion(bf16[1024,2048]{1,0:T(8,128)(2,1)S(1)} %bitcast.29, bf16[128,2048]{1,0:T(8,128)(2,1)S(1)} %slice.31, bf16[128,2048]{1,0:T(8,128)(2,1)S(1)} %slice.30, bf16[128,2048]{1,0:T(8,128)(2,1)S(1)} %slice.29, f32[1024]{0:T(1024)S(1)} %broadcast_multiply_fusion), kind=kOutput, calls=%fused_computation.20 | convolution fusion | flops 1615724544 | bytes 7344128 | tf_op jit(solution)/shard_map/td,fd->tf/dot_general | solution.py:159
  102.3 4.3 %collective-permute-start.12 = (f32[384,1024]{1,0:T(8,128)S(1)}, f32[384,1024]{1,0:T(8,128)S(1)}, u32[]{:S(2)}, u32[]{:S(2)}) collective-permute-start(f32[384,1024]{1,0:T(8,128)S(1)} %fusion.16), channel_id=1, source_target_pairs={{0,64},{64,0},{1,65},{65,1},{2,66},{66,2},{3,67},{67,3},{4,68},{68... | collective-permute-start | bytes 4718600 | tf_op jit(solution)/shard_map/ppermute | solution.py:57
  106.6 4.1 %shard_map.91 = (bf16[1024,2048]{1,0:T(8,128)(2,1)}, f32[8,128]{1,0:T(8,128)S(1)}) custom-call(bf16[1024,512]{1,0:T(8,128)(2,1)S(1)} %shard_map.86.code_ref, bf16[128,2176]{1,0:T(8,128)(2,1)S(1)} %bitcast.40, bf16[128,2176]{1,0:T(8,128)(2,1)S(1)} %collective-permute-done.8.e1, bf16[128,2176]{1,0:T(8,128)(2,1)S(1)} %collective-permute-done.9.e2, ...), custom_call_target="tpu_custom_call" | custom-call | flops 2147483648 | bytes 11665408 | tf_op jit(solution)/shard_map/pallas_call | solution.py:212
  111.4 3.9 %shard_map.90 = bf16[2048,1024]{1,0:T(8,128)(2,1)} custom-call(bf16[2048,512]{1,0:T(8,128)(2,1)S(1)} %shard_map.89.token_ref, bf16[512,1024]{1,0:T(8,128)(2,1)S(1)} %pad_maximum_fusion.pre_grad_ref), custom_call_target="tpu_custom_call" | custom-call | flops 2147483648 | bytes 5242880 | tf_op jit(solution)/shard_map/pallas_call | solution.py:242
  (63 shorter events, 9.7 us)
Async XLA Ops:
  22.8 8.3 %collective-permute-start = (bf16[128,2048]{1,0:T(8,128)(2,1)S(1)}, bf16[128,2048]{1,0:T(8,128)(2,1)S(1)}, u32[]{:S(2)}, u32[]{:S(2)}) collective-permute-start(bf16[128,2048]{1,0:T(8,128)(2,1)S(1)} %bitcast.31), channel_id=1, source_target_pairs={{0,3},{1,0},{2,1},{3,2},{4,7},{5,4},{6,5},{7,6},{8,11},{9,8},{10,9... | collective-permute-start | bytes 1572872 | tf_op jit(solution)/shard_map/ppermute | solution.py:49
  22.8 9.3 %collective-permute-start.1 = (bf16[128,2048]{1,0:T(8,128)(2,1)S(1)}, bf16[128,2048]{1,0:T(8,128)(2,1)S(1)}, u32[]{:S(2)}, u32[]{:S(2)}) collective-permute-start(bf16[128,2048]{1,0:T(8,128)(2,1)S(1)} %bitcast.32), channel_id=1, source_target_pairs={{0,16},{1,17},{2,18},{3,19},{4,20},{5,21},{6,22},{7,23},{8,24},{9,... | collective-permute-start | bytes 1572872 | tf_op jit(solution)/shard_map/ppermute | solution.py:49
  25.9 9.5 %collective-permute-start.2 = (bf16[128,2048]{1,0:T(8,128)(2,1)S(1)}, bf16[128,2048]{1,0:T(8,128)(2,1)S(1)}, u32[]{:S(2)}, u32[]{:S(2)}) collective-permute-start(bf16[128,2048]{1,0:T(8,128)(2,1)S(1)} %bitcast.33), channel_id=1, source_target_pairs={{0,1},{1,2},{2,3},{3,0},{4,5},{5,6},{6,7},{7,4},{8,9},{9,10},{10,1... | collective-permute-start | bytes 1572872 | tf_op jit(solution)/shard_map/ppermute | solution.py:49
  30.8 10.6 %copy-start.12 = (f32[1024]{0:T(1024)S(1)}, f32[1024]{0:T(1024)}, u32[]{:S(2)}) copy-start(f32[1024]{0:T(1024)} %param.8) | copy-start | bytes 12292
  31.1 6.2 %copy-start.3 = (bf16[128,2048]{1,0:T(8,128)(2,1)}, bf16[128,2048]{1,0:T(8,128)(2,1)S(1)}, u32[]{:S(2)}) copy-start(bf16[128,2048]{1,0:T(8,128)(2,1)S(1)} %collective-permute-done.refs_1_) | copy-start | bytes 1572868
  32.1 5.3 %copy-start.5 = (bf16[128,2048]{1,0:T(8,128)(2,1)}, bf16[128,2048]{1,0:T(8,128)(2,1)S(1)}, u32[]{:S(2)}) copy-start(bf16[128,2048]{1,0:T(8,128)(2,1)S(1)} %collective-permute-done.1.refs_2_) | copy-start | bytes 1572868
  35.5 6.4 %copy-start = (bf16[1,1024,2048]{2,1,0:T(8,128)(2,1)S(1)}, bf16[1,1024,2048]{2,1,0:T(8,128)(2,1)}, u32[]{:S(2)}) copy-start(bf16[1,1024,2048]{2,1,0:T(8,128)(2,1)} %param.9) | copy-start | bytes 12582916
  37.4 4.0 %collective-permute-start.3 = (bf16[384,1024]{1,0:T(8,128)(2,1)S(1)}, bf16[384,1024]{1,0:T(8,128)(2,1)S(1)}, u32[]{:S(2)}, u32[]{:S(2)}) collective-permute-start(bf16[384,1024]{1,0:T(8,128)(2,1)S(1)} %get-tuple-element.84), channel_id=1, source_target_pairs={{0,64},{64,0},{1,65},{65,1},{2,66},{66,2},{3,67},{67,3},{4,68},{68... | collective-permute-start | bytes 2359304 | tf_op jit(solution)/shard_map/ppermute | solution.py:57
  39.5 7.3 %collective-permute-start.7 = (f32[128,1024]{1,0:T(8,128)S(1)}, f32[128,1024]{1,0:T(8,128)S(1)}, u32[]{:S(2)}, u32[]{:S(2)}) collective-permute-start(f32[128,1024]{1,0:T(8,128)S(1)} %fusion.2), channel_id=1, source_target_pairs={{0,64},{64,0},{1,65},{65,1},{2,66},{66,2},{3,67},{67,3},{4,68},{68... | collective-permute-start | bytes 1572872 | tf_op jit(solution)/shard_map/ppermute | solution.py:57
  43.8 9.6 %collective-permute-start.4 = (bf16[128,2048]{1,0:T(8,128)(2,1)S(1)}, bf16[128,2048]{1,0:T(8,128)(2,1)S(1)}, u32[]{:S(2)}, u32[]{:S(2)}) collective-permute-start(bf16[128,2048]{1,0:T(8,128)(2,1)S(1)} %get-tuple-element.83), channel_id=1, source_target_pairs={{0,1},{1,2},{2,3},{3,0},{4,5},{5,6},{6,7},{7,4},{8,9},{9,10},{10,1... | collective-permute-start | bytes 1572872 | tf_op jit(solution)/shard_map/ppermute | solution.py:53
  44.4 9.8 %collective-permute-start.5 = (bf16[128,2048]{1,0:T(8,128)(2,1)S(1)}, bf16[128,2048]{1,0:T(8,128)(2,1)S(1)}, u32[]{:S(2)}, u32[]{:S(2)}) collective-permute-start(bf16[128,2048]{1,0:T(8,128)(2,1)S(1)} %get-tuple-element.82), channel_id=1, source_target_pairs={{0,48},{1,49},{2,50},{3,51},{4,52},{5,53},{6,54},{7,55},{8,56},{9,... | collective-permute-start | bytes 1572872 | tf_op jit(solution)/shard_map/ppermute | solution.py:53
  45.0 9.2 %collective-permute-start.6 = (bf16[128,2048]{1,0:T(8,128)(2,1)S(1)}, bf16[128,2048]{1,0:T(8,128)(2,1)S(1)}, u32[]{:S(2)}, u32[]{:S(2)}) collective-permute-start(bf16[128,2048]{1,0:T(8,128)(2,1)S(1)} %get-tuple-element.81), channel_id=1, source_target_pairs={{0,3},{1,0},{2,1},{3,2},{4,7},{5,4},{6,5},{7,6},{8,11},{9,8},{10,9... | collective-permute-start | bytes 1572872 | tf_op jit(solution)/shard_map/ppermute | solution.py:53
  48.1 22.1 %copy-start.9 = (bf16[1,8,2048]{2,1,0:T(8,128)(2,1)S(1)}, bf16[1,8,2048]{2,1,0:T(8,128)(2,1)}, u32[]{:S(2)}) copy-start(bf16[1,8,2048]{2,1,0:T(8,128)(2,1)} %param.6) | copy-start | bytes 98308
  48.1 22.1 %copy-start.10 = (f32[1,2048]{1,0:T(1,128)S(1)}, f32[1,2048]{1,0:T(1,128)}, u32[]{:S(2)}) copy-start(f32[1,2048]{1,0:T(1,128)} %bias_ref.1) | copy-start | bytes 24580
  71.3 14.8 %all-to-all-start.2 = ((bf16[16,8,2176]{2,1,0:T(8,128)(2,1)}), bf16[16,8,2176]{2,1,0:T(8,128)(2,1)S(1)}, u32[]{:S(2)}, u32[]{:S(2)}) async-start(bf16[16,8,2176]{2,1,0:T(8,128)(2,1)} %shard_map.88), calls=%async_computation.2 | async-start | bytes 1114112 | tf_op jit(solution)/shard_map/all_to_all | solution.py:45
  86.0 11.6 %copy-start.4 = (bf16[128,2048]{1,0:T(8,128)(2,1)S(1)}, bf16[128,2048]{1,0:T(8,128)(2,1)}, u32[]{:S(2)}) copy-start(bf16[128,2048]{1,0:T(8,128)(2,1)} %copy-done.3) | copy-start | bytes 1572868
  86.0 11.6 %copy-start.6 = (bf16[128,2048]{1,0:T(8,128)(2,1)S(1)}, bf16[128,2048]{1,0:T(8,128)(2,1)}, u32[]{:S(2)}) copy-start(bf16[128,2048]{1,0:T(8,128)(2,1)} %copy-done.5) | copy-start | bytes 1572868
  86.0 11.6 %copy-start.8 = (bf16[128,2048]{1,0:T(8,128)(2,1)S(1)}, bf16[128,2048]{1,0:T(8,128)(2,1)}, u32[]{:S(2)}) copy-start(bf16[128,2048]{1,0:T(8,128)(2,1)} %copy-done.7) | copy-start | bytes 1572868
  86.0 13.1 %collective-permute-start.8 = (bf16[128,2176]{1,0:T(8,128)(2,1)S(1)}, bf16[128,2176]{1,0:T(8,128)(2,1)S(1)}, u32[]{:S(2)}, u32[]{:S(2)}) collective-permute-start(bf16[128,2176]{1,0:T(8,128)(2,1)S(1)} %bitcast.36), channel_id=1, source_target_pairs={{0,3},{1,0},{2,1},{3,2},{4,7},{5,4},{6,5},{7,6},{8,11},{9,8},{10,9... | collective-permute-start | bytes 1671176 | tf_op jit(solution)/shard_map/ppermute | solution.py:49
  90.4 8.7 %collective-permute-start.9 = (bf16[128,2176]{1,0:T(8,128)(2,1)S(1)}, bf16[128,2176]{1,0:T(8,128)(2,1)S(1)}, u32[]{:S(2)}, u32[]{:S(2)}) collective-permute-start(bf16[128,2176]{1,0:T(8,128)(2,1)S(1)} %bitcast.37), channel_id=1, source_target_pairs={{0,16},{1,17},{2,18},{3,19},{4,20},{5,21},{6,22},{7,23},{8,24},{9,... | collective-permute-start | bytes 1671176 | tf_op jit(solution)/shard_map/ppermute | solution.py:49
  90.4 9.9 %collective-permute-start.10 = (bf16[128,2176]{1,0:T(8,128)(2,1)S(1)}, bf16[128,2176]{1,0:T(8,128)(2,1)S(1)}, u32[]{:S(2)}, u32[]{:S(2)}) collective-permute-start(bf16[128,2176]{1,0:T(8,128)(2,1)S(1)} %bitcast.38), channel_id=1, source_target_pairs={{0,1},{1,2},{2,3},{3,0},{4,5},{5,6},{6,7},{7,4},{8,9},{9,10},{10,1... | collective-permute-start | bytes 1671176 | tf_op jit(solution)/shard_map/ppermute | solution.py:49
  95.0 4.1 %collective-permute-start.11 = (f32[128,1024]{1,0:T(8,128)S(1)}, f32[128,1024]{1,0:T(8,128)S(1)}, u32[]{:S(2)}, u32[]{:S(2)}) collective-permute-start(f32[128,1024]{1,0:T(8,128)S(1)} %broadcast_add_fusion), channel_id=1, source_target_pairs={{0,64},{64,0},{1,65},{65,1},{2,66},{66,2},{3,67},{67,3},{4,68},{68... | collective-permute-start | bytes 1572872 | tf_op jit(solution)/shard_map/ppermute | solution.py:57
  102.3 8.6 %collective-permute-start.12 = (f32[384,1024]{1,0:T(8,128)S(1)}, f32[384,1024]{1,0:T(8,128)S(1)}, u32[]{:S(2)}, u32[]{:S(2)}) collective-permute-start(f32[384,1024]{1,0:T(8,128)S(1)} %fusion.16), channel_id=1, source_target_pairs={{0,64},{64,0},{1,65},{65,1},{2,66},{66,2},{3,67},{67,3},{4,68},{68... | collective-permute-start | bytes 4718600 | tf_op jit(solution)/shard_map/ppermute | solution.py:57
  110.8 4.5 %collective-permute-start.13 = (f32[8,128]{1,0:T(8,128)S(1)}, f32[8,128]{1,0:T(8,128)S(1)}, u32[]{:S(2)}, u32[]{:S(2)}) collective-permute-start(f32[8,128]{1,0:T(8,128)S(1)} %get-tuple-element.75), channel_id=1, source_target_pairs={{0,64},{64,0},{1,65},{65,1},{2,66},{66,2},{3,67},{67,3},{4,68},{68... | collective-permute-start | bytes 12296 | tf_op jit(solution)/shard_map/ppermute | solution.py:57
  (4 other events, 12.1 us)

commit v6 on v5

--- a/solution.py
+++ b/solution.py
@@ -303,7 +303,7 @@
         (e123, grad0, grad_other0, token_t)
     )
     grad123 = code_gradient(jnp.concatenate([x[:, :features] for x in e123]), norm, decoder)
-    grad_other123 = swap_layers(grad123)
+    grad_other123 = swap_layers(grad123.astype(BF16)).astype(F32)
     grad_dec, loss = grad_decoder(code_t, [e0, *e123], (total0, total123, norm), decoder)
     other_loss = swap_layers(loss)
     pre_grad0 = ((grad0 + grad_other0) * gate[:quarter].astype(F32)).astype(BF16)

time: 118 us -> 116 us (0.983)
  waiting for transfers between devices: 23.6 us -> 21.4 us
    ppermute x6, waiting for transfers between devices: 5.83 us -> 1.62 us  [from_neighbours(): return [lax.ppermute(x, EVERY, moved(r, -1)) for r in (1, 2, 3)]]
    ppermute x3, waiting for transfers between devices: 6.02 us -> 8.12 us  [to_neighbours(): lax.ppermute(x, EVERY, moved(r, 1))]
    ppermute x5, starting transfers between devices: 9.16 us -> 11 us  [swap_layers(): return lax.ppermute(x, 'layer', [(0, 1), (1, 0)])]
  transfers between devices with their start and end apart: 15 -> 15, of which waited for: 9 -> 7; matrix products, arithmetic and copies ran while one was open for 10% -> 10% of each run, Pallas kernels for 9% -> 9%
where the time goes in v6:
time: 116 us
  blocking collectives  36 us (31%)
  starting transfers between devices  26.7 us (23%)
  waiting for transfers between devices  21.4 us (18%)
  Pallas kernels  11.5 us (10%)
  matrix products  10.7 us (9%)
  other arithmetic  4.45 us (4%)
  between operations  2.7 us (2%)
  local copies, waits for them, and re-layouts  2.17 us (2%)
    all_to_all x2, blocking collectives, class_exchange(): lax.all_to_all(x, LATENT, 0, 0, axis_index_groups=class_groups(), tiled=T...  36 us
    ppermute x5, starting transfers between devices, swap_layers(): return lax.ppermute(x, 'layer', [(0, 1), (1, 0)])  11 us
    all_to_all x1, waiting for transfers between devices, class_exchange(): lax.all_to_all(x, LATENT, 0, 0, axis_index_groups=class_groups(), tiled=T...  9.29 us
    ppermute x3, waiting for transfers between devices, to_neighbours(): lax.ppermute(x, EVERY, moved(r, 1))  8.12 us
    ppermute x6, starting transfers between devices, from_neighbours(): return [lax.ppermute(x, EVERY, moved(r, -1)) for r in (1, 2, 3)]  7.81 us
    all_to_all x1, starting transfers between devices, class_exchange(): lax.all_to_all(x, LATENT, 0, 0, axis_index_groups=class_groups(), tiled=T...  5.59 us
    dot_general x2, matrix products, code_gradient(): grad = jnp.einsum('td,fd->tf', error, weight, preferred_element_type=F32)  5.56 us
    pallas_call x1, Pallas kernels, grad_decoder(): pl.pallas_call(grad_dec_kernel, out_shape=(jax.ShapeDtypeStruct((latents,...  4.18 us
  transfers between devices with their start and end apart: 15, of which 7 were waited for; matrix products, arithmetic and copies ran while one was open for 10% of the time, Pallas kernels for 9%

profile of v6, /device:TPU:1, one launch (start us, length us, event | category | flops | bytes accessed | tf_op | source)
XLA Modules:
  0.0 115.6 jit_solution(17292113806186963783)
XLA Ops:
  1.4 21.4 %all_to_all.15 = bf16[16,8,2048]{2,1,0:T(8,128)(2,1)S(1)} all-to-all(bf16[16,8,2048]{2,1,0:T(8,128)(2,1)S(1)} %broadcast_in_dim.23), channel_id=1, replica_groups={{0,7,10,13,18,21,24,31,32,39,42,45,50,53,56,63},{1,4,11,14,19,22,25,28,..., dimensions={0} | all-to-all | bytes 1048576 | tf_op jit(solution)/shard_map/all_to_all | solution.py:45
  22.8 1.1 collective-permute-start.2
  24.0 2.7 %collective-permute-start = (bf16[128,2048]{1,0:T(8,128)(2,1)S(1)}, bf16[128,2048]{1,0:T(8,128)(2,1)S(1)}, u32[]{:S(2)}, u32[]{:S(2)}) collective-permute-start(bf16[128,2048]{1,0:T(8,128)(2,1)S(1)} %bitcast.33), channel_id=1, source_target_pairs={{0,3},{1,0},{2,1},{3,2},{4,7},{5,4},{6,5},{7,6},{8,11},{9,8},{10,9... | collective-permute-start | bytes 1572872 | tf_op jit(solution)/shard_map/ppermute | solution.py:49
  26.7 3.2 %multiply_reduce_fusion = f32[1024]{0:T(1024)S(1)} fusion(bf16[1024,2048]{1,0:T(8,128)(2,1)} %bitcast.25), kind=kLoop, calls=%fused_computation | loop fusion | flops 6290432 | bytes 4198400 | tf_op jit(solution)/shard_map/reduce_sum | solution.py:275
  33.1 1.8 %fusion.31 = (bf16[384,1024]{1,0:T(8,128)(2,1)S(1)}, f32[384,1024]{1,0:T(8,128)S(1)}) fusion(bf16[1,2048,1024]{2,1,0:T(8,128)(2,1)S(1)} %copy-done.11, bf16[128,2048]{1,0:T(8,128)(2,1)S(1)} %collective-permute-done.2.refs_3_, bf16[128,2048]{1,0:T(8,128)(2,1)S(1)} %collective-permute-done.1.refs_2_, bf16[128,2048]{1,0:T(8,128)(2,1)S(1)} %collective-permute-done.refs_1_), kind=kOutput, calls=%fused_computation.54 | convolution fusion | flops 1615724544 | bytes 8126464 | tf_op jit(solution)/shard_map/dot_general | solution.py:277
  35.0 3.2 %collective-permute-start.3 = (bf16[384,1024]{1,0:T(8,128)(2,1)S(1)}, bf16[384,1024]{1,0:T(8,128)(2,1)S(1)}, u32[]{:S(2)}, u32[]{:S(2)}) collective-permute-start(bf16[384,1024]{1,0:T(8,128)(2,1)S(1)} %get-tuple-element.84), channel_id=1, source_target_pairs={{0,64},{64,0},{1,65},{65,1},{2,66},{66,2},{3,67},{67,3},{4,68},{68... | collective-permute-start | bytes 2359304 | tf_op jit(solution)/shard_map/ppermute | solution.py:57
  38.4 1.8 %collective-permute-done.3 = bf16[384,1024]{1,0:T(8,128)(2,1)S(1)} collective-permute-done((bf16[384,1024]{1,0:T(8,128)(2,1)S(1)}, bf16[384,1024]{1,0:T(8,128)(2,1)S(1)}, u32[]{:S(2)}, u32[]{:S(2)}) %collective-permute-start.3) | collective-permute-done | bytes 786464 | tf_op jit(solution)/shard_map/ppermute | solution.py:57
  40.7 1.8 %convolution_convert_fusion = bf16[384,2048]{1,0:T(8,128)(2,1)S(1)} fusion(bf16[384,1024]{1,0:T(8,128)(2,1)S(1)} %get-tuple-element.78.refs_1_, bf16[1024,2048]{1,0:T(8,128)(2,1)S(1)} %bitcast.27), kind=kOutput, calls=%fused_computation.5 | convolution fusion | flops 1611399168 | bytes 6553600 | tf_op jit(solution)/shard_map/dot_general | solution.py:283
  42.6 2.3 %collective-permute-start.6 = (bf16[128,2048]{1,0:T(8,128)(2,1)S(1)}, bf16[128,2048]{1,0:T(8,128)(2,1)S(1)}, u32[]{:S(2)}, u32[]{:S(2)}) collective-permute-start(bf16[128,2048]{1,0:T(8,128)(2,1)S(1)} %get-tuple-element.81), channel_id=1, source_target_pairs={{0,3},{1,0},{2,1},{3,2},{4,7},{5,4},{6,5},{7,6},{8,11},{9,8},{10,9... | collective-permute-start | bytes 1572872 | tf_op jit(solution)/shard_map/ppermute | solution.py:53
  46.4 4.7 %collective-permute-done.6.c_ref = bf16[128,2048]{1,0:T(8,128)(2,1)S(1)} collective-permute-done((bf16[128,2048]{1,0:T(8,128)(2,1)S(1)}, bf16[128,2048]{1,0:T(8,128)(2,1)S(1)}, u32[]{:S(2)}, u32[]{:S(2)}) %collective-permute-start.6) | collective-permute-done | bytes 524320 | tf_op jit(solution)/shard_map/ppermute | solution.py:53
  51.1 3.4 %collective-permute-done.5.b_ref = bf16[128,2048]{1,0:T(8,128)(2,1)S(1)} collective-permute-done((bf16[128,2048]{1,0:T(8,128)(2,1)S(1)}, bf16[128,2048]{1,0:T(8,128)(2,1)S(1)}, u32[]{:S(2)}, u32[]{:S(2)}) %collective-permute-start.5) | collective-permute-done | bytes 524320 | tf_op jit(solution)/shard_map/ppermute | solution.py:53
  54.8 14.6 %all_to_all.16.parts_ref = bf16[16,8,2048]{2,1,0:T(8,128)(2,1)S(1)} all-to-all(bf16[16,8,2048]{2,1,0:T(8,128)(2,1)S(1)} %bitcast.41), channel_id=1, replica_groups={{0,7,10,13,18,21,24,31,32,39,42,45,50,53,56,63},{1,4,11,14,19,22,25,28,..., dimensions={0} | all-to-all | bytes 1048576 | tf_op jit(solution)/shard_map/all_to_all | solution.py:45
  69.4 1.0 shard_map.88
  70.4 5.6 %all-to-all-start.2 = ((bf16[16,8,2176]{2,1,0:T(8,128)(2,1)}), bf16[16,8,2176]{2,1,0:T(8,128)(2,1)S(1)}, u32[]{:S(2)}, u32[]{:S(2)}) async-start(bf16[16,8,2176]{2,1,0:T(8,128)(2,1)} %shard_map.88), calls=%async_computation.2 | async-start | bytes 1114112 | tf_op jit(solution)/shard_map/all_to_all | solution.py:45
  76.0 9.3 %all-to-all-done.2 = bf16[16,8,2176]{2,1,0:T(8,128)(2,1)S(1)} async-done(((bf16[16,8,2176]{2,1,0:T(8,128)(2,1)}), bf16[16,8,2176]{2,1,0:T(8,128)(2,1)S(1)}, u32[]{:S(2)}, u32[]{:S(2)}) %all-to-all-start.2) | async-done | bytes 557088 | tf_op jit(solution)/shard_map/all_to_all | solution.py:45
  85.3 1.3 %collective-permute-start.10 = (bf16[128,2176]{1,0:T(8,128)(2,1)S(1)}, bf16[128,2176]{1,0:T(8,128)(2,1)S(1)}, u32[]{:S(2)}, u32[]{:S(2)}) collective-permute-start(bf16[128,2176]{1,0:T(8,128)(2,1)S(1)} %bitcast.36), channel_id=1, source_target_pairs={{0,1},{1,2},{2,3},{3,0},{4,5},{5,6},{6,7},{7,4},{8,9},{9,10},{10,1... | collective-permute-start | bytes 1671176 | tf_op jit(solution)/shard_map/ppermute | solution.py:49
  86.8 2.5 %collective-permute-start.8 = (bf16[128,2176]{1,0:T(8,128)(2,1)S(1)}, bf16[128,2176]{1,0:T(8,128)(2,1)S(1)}, u32[]{:S(2)}, u32[]{:S(2)}) collective-permute-start(bf16[128,2176]{1,0:T(8,128)(2,1)S(1)} %bitcast.38), channel_id=1, source_target_pairs={{0,3},{1,0},{2,1},{3,2},{4,7},{5,4},{6,5},{7,6},{8,11},{9,8},{10,9... | collective-permute-start | bytes 1671176 | tf_op jit(solution)/shard_map/ppermute | solution.py:49
  89.3 3.7 %broadcast_add_fusion = f32[128,1024]{1,0:T(8,128)S(1)} fusion(f32[1024]{0:T(1024)S(1)} %broadcast_multiply_fusion, bf16[1024,2048]{1,0:T(8,128)(2,1)} %bitcast.26, bf16[128,2176]{1,0:T(8,128)(2,1)S(1)} %bitcast.39), kind=kOutput, calls=%fused_computation.29 | convolution fusion | flops 537001984 | bytes 5246976 | tf_op jit(solution)/shard_map/td,fd->tf/dot_general | solution.py:159
  93.0 5.3 %collective-permute-start.11 = (f32[128,1024]{1,0:T(8,128)S(1)}, f32[128,1024]{1,0:T(8,128)S(1)}, u32[]{:S(2)}, u32[]{:S(2)}) collective-permute-start(f32[128,1024]{1,0:T(8,128)S(1)} %broadcast_add_fusion), channel_id=1, source_target_pairs={{0,64},{64,0},{1,65},{65,1},{2,66},{66,2},{3,67},{67,3},{4,68},{68... | collective-permute-start | bytes 1572872 | tf_op jit(solution)/shard_map/ppermute | solution.py:57
  98.2 1.0 shard_map.89.token_ref
  100.4 1.9 %add_convert_fusion = (bf16[384,1024]{1,0:T(8,128)(2,1)S(1)}, f32[384,1024]{1,0:T(8,128)S(1)}) fusion(f32[1024]{0:T(1024)S(1)} %broadcast_multiply_fusion, bf16[1024,2048]{1,0:T(8,128)(2,1)S(1)} %bitcast.29, bf16[128,2048]{1,0:T(8,128)(2,1)S(1)} %slice.31, bf16[128,2048]{1,0:T(8,128)(2,1)S(1)} %slice.30, bf16[128,2048]{1,0:T(8,128)(2,1)S(1)} %slice.29), kind=kOutput, calls=%fused_computation.20 | convolution fusion | flops 1616117760 | bytes 8130560 | tf_op jit(solution)/shard_map/td,fd->tf/dot_general | solution.py:159
  102.3 2.3 %collective-permute-start.12 = (bf16[384,1024]{1,0:T(8,128)(2,1)S(1)}, bf16[384,1024]{1,0:T(8,128)(2,1)S(1)}, u32[]{:S(2)}, u32[]{:S(2)}) collective-permute-start(bf16[384,1024]{1,0:T(8,128)(2,1)S(1)} %get-tuple-element.86), channel_id=1, source_target_pairs={{0,64},{64,0},{1,65},{65,1},{2,66},{66,2},{3,67},{67,3},{4,68},{68... | collective-permute-start | bytes 2359304 | tf_op jit(solution)/shard_map/ppermute | solution.py:57
  104.6 4.2 %shard_map.91 = (bf16[1024,2048]{1,0:T(8,128)(2,1)}, f32[8,128]{1,0:T(8,128)S(1)}) custom-call(bf16[1024,512]{1,0:T(8,128)(2,1)S(1)} %shard_map.86.code_ref, bf16[128,2176]{1,0:T(8,128)(2,1)S(1)} %bitcast.40, bf16[128,2176]{1,0:T(8,128)(2,1)S(1)} %collective-permute-done.8.e1, bf16[128,2176]{1,0:T(8,128)(2,1)S(1)} %collective-permute-done.9.e2, ...), custom_call_target="tpu_custom_call" | custom-call | flops 2147483648 | bytes 11665408 | tf_op jit(solution)/shard_map/pallas_call | solution.py:212
  109.5 3.9 %shard_map.90 = bf16[2048,1024]{1,0:T(8,128)(2,1)} custom-call(bf16[2048,512]{1,0:T(8,128)(2,1)S(1)} %shard_map.89.token_ref, bf16[512,1024]{1,0:T(8,128)(2,1)S(1)} %pad_maximum_fusion.pre_grad_ref), custom_call_target="tpu_custom_call" | custom-call | flops 2147483648 | bytes 5242880 | tf_op jit(solution)/shard_map/pallas_call | solution.py:242
  (63 shorter events, 8.9 us)
Async XLA Ops:
  22.8 9.5 %collective-permute-start.2 = (bf16[128,2048]{1,0:T(8,128)(2,1)S(1)}, bf16[128,2048]{1,0:T(8,128)(2,1)S(1)}, u32[]{:S(2)}, u32[]{:S(2)}) collective-permute-start(bf16[128,2048]{1,0:T(8,128)(2,1)S(1)} %bitcast.31), channel_id=1, source_target_pairs={{0,1},{1,2},{2,3},{3,0},{4,5},{5,6},{6,7},{7,4},{8,9},{9,10},{10,1... | collective-permute-start | bytes 1572872 | tf_op jit(solution)/shard_map/ppermute | solution.py:49
  23.9 8.5 %collective-permute-start.1 = (bf16[128,2048]{1,0:T(8,128)(2,1)S(1)}, bf16[128,2048]{1,0:T(8,128)(2,1)S(1)}, u32[]{:S(2)}, u32[]{:S(2)}) collective-permute-start(bf16[128,2048]{1,0:T(8,128)(2,1)S(1)} %bitcast.32), channel_id=1, source_target_pairs={{0,16},{1,17},{2,18},{3,19},{4,20},{5,21},{6,22},{7,23},{8,24},{9,... | collective-permute-start | bytes 1572872 | tf_op jit(solution)/shard_map/ppermute | solution.py:49
  24.0 9.2 %collective-permute-start = (bf16[128,2048]{1,0:T(8,128)(2,1)S(1)}, bf16[128,2048]{1,0:T(8,128)(2,1)S(1)}, u32[]{:S(2)}, u32[]{:S(2)}) collective-permute-start(bf16[128,2048]{1,0:T(8,128)(2,1)S(1)} %bitcast.33), channel_id=1, source_target_pairs={{0,3},{1,0},{2,1},{3,2},{4,7},{5,4},{6,5},{7,6},{8,11},{9,8},{10,9... | collective-permute-start | bytes 1572872 | tf_op jit(solution)/shard_map/ppermute | solution.py:49
  26.7 3.2 %copy-start.2 = (s32[512,1024]{1,0:T(8,128)S(1)}, s32[512,1024]{1,0:T(8,128)}, u32[]{:S(2)}) copy-start(s32[512,1024]{1,0:T(8,128)} %mask_ref) | copy-start | bytes 6291460
  26.7 4.1 %copy-start.11 = (bf16[1,2048,1024]{2,1,0:T(8,128)(2,1)S(1)}, bf16[1,2048,1024]{2,1,0:T(8,128)(2,1)}, u32[]{:S(2)}) copy-start(bf16[1,2048,1024]{2,1,0:T(8,128)(2,1)} %param.7) | copy-start | bytes 12582916
  31.5 8.7 %copy-start.12 = (f32[1024]{0:T(1024)S(1)}, f32[1024]{0:T(1024)}, u32[]{:S(2)}) copy-start(f32[1024]{0:T(1024)} %param.8) | copy-start | bytes 12292
  33.1 7.5 %copy-start = (bf16[1,1024,2048]{2,1,0:T(8,128)(2,1)S(1)}, bf16[1,1024,2048]{2,1,0:T(8,128)(2,1)}, u32[]{:S(2)}) copy-start(bf16[1,1024,2048]{2,1,0:T(8,128)(2,1)} %param.9) | copy-start | bytes 12582916
  35.0 5.2 %collective-permute-start.3 = (bf16[384,1024]{1,0:T(8,128)(2,1)S(1)}, bf16[384,1024]{1,0:T(8,128)(2,1)S(1)}, u32[]{:S(2)}, u32[]{:S(2)}) collective-permute-start(bf16[384,1024]{1,0:T(8,128)(2,1)S(1)} %get-tuple-element.84), channel_id=1, source_target_pairs={{0,64},{64,0},{1,65},{65,1},{2,66},{66,2},{3,67},{67,3},{4,68},{68... | collective-permute-start | bytes 2359304 | tf_op jit(solution)/shard_map/ppermute | solution.py:57
  38.3 6.7 %collective-permute-start.7 = (f32[128,1024]{1,0:T(8,128)S(1)}, f32[128,1024]{1,0:T(8,128)S(1)}, u32[]{:S(2)}, u32[]{:S(2)}) collective-permute-start(f32[128,1024]{1,0:T(8,128)S(1)} %fusion.2), channel_id=1, source_target_pairs={{0,64},{64,0},{1,65},{65,1},{2,66},{66,2},{3,67},{67,3},{4,68},{68... | collective-permute-start | bytes 1572872 | tf_op jit(solution)/shard_map/ppermute | solution.py:57
  42.6 8.5 %collective-permute-start.6 = (bf16[128,2048]{1,0:T(8,128)(2,1)S(1)}, bf16[128,2048]{1,0:T(8,128)(2,1)S(1)}, u32[]{:S(2)}, u32[]{:S(2)}) collective-permute-start(bf16[128,2048]{1,0:T(8,128)(2,1)S(1)} %get-tuple-element.81), channel_id=1, source_target_pairs={{0,3},{1,0},{2,1},{3,2},{4,7},{5,4},{6,5},{7,6},{8,11},{9,8},{10,9... | collective-permute-start | bytes 1572872 | tf_op jit(solution)/shard_map/ppermute | solution.py:53
  44.9 9.5 %collective-permute-start.5 = (bf16[128,2048]{1,0:T(8,128)(2,1)S(1)}, bf16[128,2048]{1,0:T(8,128)(2,1)S(1)}, u32[]{:S(2)}, u32[]{:S(2)}) collective-permute-start(bf16[128,2048]{1,0:T(8,128)(2,1)S(1)} %get-tuple-element.82), channel_id=1, source_target_pairs={{0,48},{1,49},{2,50},{3,51},{4,52},{5,53},{6,54},{7,55},{8,56},{9,... | collective-permute-start | bytes 1572872 | tf_op jit(solution)/shard_map/ppermute | solution.py:53
  45.0 9.5 %collective-permute-start.4 = (bf16[128,2048]{1,0:T(8,128)(2,1)S(1)}, bf16[128,2048]{1,0:T(8,128)(2,1)S(1)}, u32[]{:S(2)}, u32[]{:S(2)}) collective-permute-start(bf16[128,2048]{1,0:T(8,128)(2,1)S(1)} %get-tuple-element.83), channel_id=1, source_target_pairs={{0,1},{1,2},{2,3},{3,0},{4,5},{5,6},{6,7},{7,4},{8,9},{9,10},{10,1... | collective-permute-start | bytes 1572872 | tf_op jit(solution)/shard_map/ppermute | solution.py:53
  46.4 23.0 %copy-start.9 = (bf16[1,8,2048]{2,1,0:T(8,128)(2,1)S(1)}, bf16[1,8,2048]{2,1,0:T(8,128)(2,1)}, u32[]{:S(2)}) copy-start(bf16[1,8,2048]{2,1,0:T(8,128)(2,1)} %param.6) | copy-start | bytes 98308
  46.4 23.0 %copy-start.10 = (f32[1,2048]{1,0:T(1,128)S(1)}, f32[1,2048]{1,0:T(1,128)}, u32[]{:S(2)}) copy-start(f32[1,2048]{1,0:T(1,128)} %bias_ref.1) | copy-start | bytes 24580
  70.4 14.9 %all-to-all-start.2 = ((bf16[16,8,2176]{2,1,0:T(8,128)(2,1)}), bf16[16,8,2176]{2,1,0:T(8,128)(2,1)S(1)}, u32[]{:S(2)}, u32[]{:S(2)}) async-start(bf16[16,8,2176]{2,1,0:T(8,128)(2,1)} %shard_map.88), calls=%async_computation.2 | async-start | bytes 1114112 | tf_op jit(solution)/shard_map/all_to_all | solution.py:45
  85.3 12.9 %copy-start.4 = (bf16[128,2048]{1,0:T(8,128)(2,1)S(1)}, bf16[128,2048]{1,0:T(8,128)(2,1)}, u32[]{:S(2)}) copy-start(bf16[128,2048]{1,0:T(8,128)(2,1)} %copy-done.3) | copy-start | bytes 1572868
  85.3 12.9 %copy-start.6 = (bf16[128,2048]{1,0:T(8,128)(2,1)S(1)}, bf16[128,2048]{1,0:T(8,128)(2,1)}, u32[]{:S(2)}) copy-start(bf16[128,2048]{1,0:T(8,128)(2,1)} %copy-done.5) | copy-start | bytes 1572868
  85.3 12.9 %copy-start.8 = (bf16[128,2048]{1,0:T(8,128)(2,1)S(1)}, bf16[128,2048]{1,0:T(8,128)(2,1)}, u32[]{:S(2)}) copy-start(bf16[128,2048]{1,0:T(8,128)(2,1)} %copy-done.7) | copy-start | bytes 1572868
  85.3 14.5 %collective-permute-start.10 = (bf16[128,2176]{1,0:T(8,128)(2,1)S(1)}, bf16[128,2176]{1,0:T(8,128)(2,1)S(1)}, u32[]{:S(2)}, u32[]{:S(2)}) collective-permute-start(bf16[128,2176]{1,0:T(8,128)(2,1)S(1)} %bitcast.36), channel_id=1, source_target_pairs={{0,1},{1,2},{2,3},{3,0},{4,5},{5,6},{6,7},{7,4},{8,9},{9,10},{10,1... | collective-permute-start | bytes 1671176 | tf_op jit(solution)/shard_map/ppermute | solution.py:49
  86.6 13.1 %collective-permute-start.9 = (bf16[128,2176]{1,0:T(8,128)(2,1)S(1)}, bf16[128,2176]{1,0:T(8,128)(2,1)S(1)}, u32[]{:S(2)}, u32[]{:S(2)}) collective-permute-start(bf16[128,2176]{1,0:T(8,128)(2,1)S(1)} %bitcast.37), channel_id=1, source_target_pairs={{0,16},{1,17},{2,18},{3,19},{4,20},{5,21},{6,22},{7,23},{8,24},{9,... | collective-permute-start | bytes 1671176 | tf_op jit(solution)/shard_map/ppermute | solution.py:49
  86.8 13.0 %collective-permute-start.8 = (bf16[128,2176]{1,0:T(8,128)(2,1)S(1)}, bf16[128,2176]{1,0:T(8,128)(2,1)S(1)}, u32[]{:S(2)}, u32[]{:S(2)}) collective-permute-start(bf16[128,2176]{1,0:T(8,128)(2,1)S(1)} %bitcast.38), channel_id=1, source_target_pairs={{0,3},{1,0},{2,1},{3,2},{4,7},{5,4},{6,5},{7,6},{8,11},{9,8},{10,9... | collective-permute-start | bytes 1671176 | tf_op jit(solution)/shard_map/ppermute | solution.py:49
  93.0 6.8 %collective-permute-start.11 = (f32[128,1024]{1,0:T(8,128)S(1)}, f32[128,1024]{1,0:T(8,128)S(1)}, u32[]{:S(2)}, u32[]{:S(2)}) collective-permute-start(f32[128,1024]{1,0:T(8,128)S(1)} %broadcast_add_fusion), channel_id=1, source_target_pairs={{0,64},{64,0},{1,65},{65,1},{2,66},{66,2},{3,67},{67,3},{4,68},{68... | collective-permute-start | bytes 1572872 | tf_op jit(solution)/shard_map/ppermute | solution.py:57
  102.3 6.7 %collective-permute-start.12 = (bf16[384,1024]{1,0:T(8,128)(2,1)S(1)}, bf16[384,1024]{1,0:T(8,128)(2,1)S(1)}, u32[]{:S(2)}, u32[]{:S(2)}) collective-permute-start(bf16[384,1024]{1,0:T(8,128)(2,1)S(1)} %get-tuple-element.86), channel_id=1, source_target_pairs={{0,64},{64,0},{1,65},{65,1},{2,66},{66,2},{3,67},{67,3},{4,68},{68... | collective-permute-start | bytes 2359304 | tf_op jit(solution)/shard_map/ppermute | solution.py:57
  108.8 4.5 %collective-permute-start.13 = (f32[8,128]{1,0:T(8,128)S(1)}, f32[8,128]{1,0:T(8,128)S(1)}, u32[]{:S(2)}, u32[]{:S(2)}) collective-permute-start(f32[8,128]{1,0:T(8,128)S(1)} %get-tuple-element.75), channel_id=1, source_target_pairs={{0,64},{64,0},{1,65},{65,1},{2,66},{66,2},{3,67},{67,3},{4,68},{68... | collective-permute-start | bytes 12296 | tf_op jit(solution)/shard_map/ppermute | solution.py:57
  (4 other events, 9.4 us)

commit v7 on v6

--- a/solution.py
+++ b/solution.py
@@ -269,7 +269,7 @@
     )
     q123 = from_neighbours(q0)
     pre0 = jnp.dot(q0, encoder, preferred_element_type=F32)
-    other0 = swap_layers(pre0)
+    other0 = swap_layers(pre0.astype(BF16)).astype(F32)
     gate = ordered_gate(active_mask, place)
     dec_float = decoder.astype(F32)
     row_norm = jnp.sqrt(jnp.sum(dec_float * dec_float, axis=1) + 1e-06)
@@ -298,7 +298,7 @@
     token_t = transposed(all_tokens)
     norm = row_norm[None]
     grad0 = code_gradient(e0[:, :features], norm, decoder)
-    grad_other0 = swap_layers(grad0)
+    grad_other0 = swap_layers(grad0.astype(BF16)).astype(F32)
     e123, grad0, grad_other0, token_t = lax.optimization_barrier(
         (e123, grad0, grad_other0, token_t)
     )

time: 116 us -> 116 us (level)
  no operation moved by 1% of the time
where the time goes in v7:
time: 116 us
  blocking collectives  36 us (31%)
  starting transfers between devices  26.7 us (23%)
  waiting for transfers between devices  21 us (18%)
  Pallas kernels  11.5 us (10%)
  matrix products  10.7 us (9%)
  other arithmetic  4.49 us (4%)
  between operations  2.72 us (2%)
  local copies, waits for them, and re-layouts  2.48 us (2%)
    all_to_all x2, blocking collectives, class_exchange(): lax.all_to_all(x, LATENT, 0, 0, axis_index_groups=class_groups(), tiled=T...  36 us
    ppermute x5, starting transfers between devices, swap_layers(): return lax.ppermute(x, 'layer', [(0, 1), (1, 0)])  11 us
    all_to_all x1, waiting for transfers between devices, class_exchange(): lax.all_to_all(x, LATENT, 0, 0, axis_index_groups=class_groups(), tiled=T...  9.3 us
    ppermute x3, waiting for transfers between devices, to_neighbours(): lax.ppermute(x, EVERY, moved(r, 1))  8.12 us
    ppermute x6, starting transfers between devices, from_neighbours(): return [lax.ppermute(x, EVERY, moved(r, -1)) for r in (1, 2, 3)]  7.8 us
    all_to_all x1, starting transfers between devices, class_exchange(): lax.all_to_all(x, LATENT, 0, 0, axis_index_groups=class_groups(), tiled=T...  5.59 us
    dot_general x2, matrix products, code_gradient(): grad = jnp.einsum('td,fd->tf', error, weight, preferred_element_type=F32)  5.56 us
    pallas_call x1, Pallas kernels, grad_decoder(): pl.pallas_call(grad_dec_kernel, out_shape=(jax.ShapeDtypeStruct((latents,...  4.18 us
  transfers between devices with their start and end apart: 15, of which 7 were waited for; matrix products, arithmetic and copies ran while one was open for 10% of the time, Pallas kernels for 9%

profile of v7, /device:TPU:1, one launch (start us, length us, event | category | flops | bytes accessed | tf_op | source)
XLA Modules:
  0.0 115.6 jit_solution(3212418464386520352)
XLA Ops:
  1.4 21.4 %all_to_all.15 = bf16[16,8,2048]{2,1,0:T(8,128)(2,1)S(1)} all-to-all(bf16[16,8,2048]{2,1,0:T(8,128)(2,1)S(1)} %broadcast_in_dim.23), channel_id=1, replica_groups={{0,7,10,13,18,21,24,31,32,39,42,45,50,53,56,63},{1,4,11,14,19,22,25,28,..., dimensions={0} | all-to-all | bytes 1048576 | tf_op jit(solution)/shard_map/all_to_all | solution.py:45
  22.8 1.1 collective-permute-start.2
  24.0 2.7 %collective-permute-start = (bf16[128,2048]{1,0:T(8,128)(2,1)S(1)}, bf16[128,2048]{1,0:T(8,128)(2,1)S(1)}, u32[]{:S(2)}, u32[]{:S(2)}) collective-permute-start(bf16[128,2048]{1,0:T(8,128)(2,1)S(1)} %bitcast.35), channel_id=1, source_target_pairs={{0,3},{1,0},{2,1},{3,2},{4,7},{5,4},{6,5},{7,6},{8,11},{9,8},{10,9... | collective-permute-start | bytes 1572872 | tf_op jit(solution)/shard_map/ppermute | solution.py:49
  26.7 3.2 %multiply_reduce_fusion = f32[1024]{0:T(1024)S(1)} fusion(bf16[1024,2048]{1,0:T(8,128)(2,1)} %bitcast.27), kind=kLoop, calls=%fused_computation | loop fusion | flops 6290432 | bytes 4198400 | tf_op jit(solution)/shard_map/reduce_sum | solution.py:275
  33.1 1.8 %fusion.32 = (bf16[384,1024]{1,0:T(8,128)(2,1)S(1)}, f32[384,1024]{1,0:T(8,128)S(1)}) fusion(bf16[1,2048,1024]{2,1,0:T(8,128)(2,1)S(1)} %copy-done.11, bf16[128,2048]{1,0:T(8,128)(2,1)S(1)} %collective-permute-done.2.refs_3_, bf16[128,2048]{1,0:T(8,128)(2,1)S(1)} %collective-permute-done.1.refs_2_, bf16[128,2048]{1,0:T(8,128)(2,1)S(1)} %collective-permute-done.refs_1_), kind=kOutput, calls=%fused_computation.55 | convolution fusion | flops 1615724544 | bytes 8126464 | tf_op jit(solution)/shard_map/dot_general | solution.py:277
  35.0 3.3 %collective-permute-start.3 = (bf16[384,1024]{1,0:T(8,128)(2,1)S(1)}, bf16[384,1024]{1,0:T(8,128)(2,1)S(1)}, u32[]{:S(2)}, u32[]{:S(2)}) collective-permute-start(bf16[384,1024]{1,0:T(8,128)(2,1)S(1)} %get-tuple-element.86), channel_id=1, source_target_pairs={{0,64},{64,0},{1,65},{65,1},{2,66},{66,2},{3,67},{67,3},{4,68},{68... | collective-permute-start | bytes 2359304 | tf_op jit(solution)/shard_map/ppermute | solution.py:57
  38.4 1.8 %collective-permute-done.3 = bf16[384,1024]{1,0:T(8,128)(2,1)S(1)} collective-permute-done((bf16[384,1024]{1,0:T(8,128)(2,1)S(1)}, bf16[384,1024]{1,0:T(8,128)(2,1)S(1)}, u32[]{:S(2)}, u32[]{:S(2)}) %collective-permute-start.3) | collective-permute-done | bytes 786464 | tf_op jit(solution)/shard_map/ppermute | solution.py:57
  40.7 1.8 %convolution_convert_fusion = bf16[384,2048]{1,0:T(8,128)(2,1)S(1)} fusion(bf16[384,1024]{1,0:T(8,128)(2,1)S(1)} %get-tuple-element.80.refs_1_, bf16[1024,2048]{1,0:T(8,128)(2,1)S(1)} %bitcast.29), kind=kOutput, calls=%fused_computation.5 | convolution fusion | flops 1611399168 | bytes 6553600 | tf_op jit(solution)/shard_map/dot_general | solution.py:283
  42.6 2.3 %collective-permute-start.6 = (bf16[128,2048]{1,0:T(8,128)(2,1)S(1)}, bf16[128,2048]{1,0:T(8,128)(2,1)S(1)}, u32[]{:S(2)}, u32[]{:S(2)}) collective-permute-start(bf16[128,2048]{1,0:T(8,128)(2,1)S(1)} %get-tuple-element.83), channel_id=1, source_target_pairs={{0,3},{1,0},{2,1},{3,2},{4,7},{5,4},{6,5},{7,6},{8,11},{9,8},{10,9... | collective-permute-start | bytes 1572872 | tf_op jit(solution)/shard_map/ppermute | solution.py:53
  46.4 4.7 %collective-permute-done.6.c_ref = bf16[128,2048]{1,0:T(8,128)(2,1)S(1)} collective-permute-done((bf16[128,2048]{1,0:T(8,128)(2,1)S(1)}, bf16[128,2048]{1,0:T(8,128)(2,1)S(1)}, u32[]{:S(2)}, u32[]{:S(2)}) %collective-permute-start.6) | collective-permute-done | bytes 524320 | tf_op jit(solution)/shard_map/ppermute | solution.py:53
  51.1 3.4 %collective-permute-done.5.b_ref = bf16[128,2048]{1,0:T(8,128)(2,1)S(1)} collective-permute-done((bf16[128,2048]{1,0:T(8,128)(2,1)S(1)}, bf16[128,2048]{1,0:T(8,128)(2,1)S(1)}, u32[]{:S(2)}, u32[]{:S(2)}) %collective-permute-start.5) | collective-permute-done | bytes 524320 | tf_op jit(solution)/shard_map/ppermute | solution.py:53
  54.8 14.6 %all_to_all.16.parts_ref = bf16[16,8,2048]{2,1,0:T(8,128)(2,1)S(1)} all-to-all(bf16[16,8,2048]{2,1,0:T(8,128)(2,1)S(1)} %bitcast.43), channel_id=1, replica_groups={{0,7,10,13,18,21,24,31,32,39,42,45,50,53,56,63},{1,4,11,14,19,22,25,28,..., dimensions={0} | all-to-all | bytes 1048576 | tf_op jit(solution)/shard_map/all_to_all | solution.py:45
  69.4 1.0 shard_map.88
  70.4 5.6 %all-to-all-start.2 = ((bf16[16,8,2176]{2,1,0:T(8,128)(2,1)}), bf16[16,8,2176]{2,1,0:T(8,128)(2,1)S(1)}, u32[]{:S(2)}, u32[]{:S(2)}) async-start(bf16[16,8,2176]{2,1,0:T(8,128)(2,1)} %shard_map.88), calls=%async_computation.2 | async-start | bytes 1114112 | tf_op jit(solution)/shard_map/all_to_all | solution.py:45
  76.0 9.3 %all-to-all-done.2 = bf16[16,8,2176]{2,1,0:T(8,128)(2,1)S(1)} async-done(((bf16[16,8,2176]{2,1,0:T(8,128)(2,1)}), bf16[16,8,2176]{2,1,0:T(8,128)(2,1)S(1)}, u32[]{:S(2)}, u32[]{:S(2)}) %all-to-all-start.2) | async-done | bytes 557088 | tf_op jit(solution)/shard_map/all_to_all | solution.py:45
  85.3 1.3 %collective-permute-start.10 = (bf16[128,2176]{1,0:T(8,128)(2,1)S(1)}, bf16[128,2176]{1,0:T(8,128)(2,1)S(1)}, u32[]{:S(2)}, u32[]{:S(2)}) collective-permute-start(bf16[128,2176]{1,0:T(8,128)(2,1)S(1)} %bitcast.38), channel_id=1, source_target_pairs={{0,1},{1,2},{2,3},{3,0},{4,5},{5,6},{6,7},{7,4},{8,9},{9,10},{10,1... | collective-permute-start | bytes 1671176 | tf_op jit(solution)/shard_map/ppermute | solution.py:49
  86.8 2.5 %collective-permute-start.8 = (bf16[128,2176]{1,0:T(8,128)(2,1)S(1)}, bf16[128,2176]{1,0:T(8,128)(2,1)S(1)}, u32[]{:S(2)}, u32[]{:S(2)}) collective-permute-start(bf16[128,2176]{1,0:T(8,128)(2,1)S(1)} %bitcast.40), channel_id=1, source_target_pairs={{0,3},{1,0},{2,1},{3,2},{4,7},{5,4},{6,5},{7,6},{8,11},{9,8},{10,9... | collective-permute-start | bytes 1671176 | tf_op jit(solution)/shard_map/ppermute | solution.py:49
  89.3 3.7 %fusion.30 = (bf16[128,1024]{1,0:T(8,128)(2,1)S(1)}, f32[128,1024]{1,0:T(8,128)S(1)}) fusion(f32[1024]{0:T(1024)S(1)} %broadcast_multiply_fusion, bf16[1024,2048]{1,0:T(8,128)(2,1)} %bitcast.28, bf16[128,2176]{1,0:T(8,128)(2,1)S(1)} %bitcast.41), kind=kOutput, calls=%fused_computation.53 | convolution fusion | flops 537133056 | bytes 5509120 | tf_op jit(solution)/shard_map/td,fd->tf/dot_general | solution.py:159
  93.0 5.3 %collective-permute-start.11 = (bf16[128,1024]{1,0:T(8,128)(2,1)S(1)}, bf16[128,1024]{1,0:T(8,128)(2,1)S(1)}, u32[]{:S(2)}, u32[]{:S(2)}) collective-permute-start(bf16[128,1024]{1,0:T(8,128)(2,1)S(1)} %get-tuple-element.77), channel_id=1, source_target_pairs={{0,64},{64,0},{1,65},{65,1},{2,66},{66,2},{3,67},{67,3},{4,68},{68... | collective-permute-start | bytes 786440 | tf_op jit(solution)/shard_map/ppermute | solution.py:57
  98.3 1.0 shard_map.89.token_ref
  100.4 1.9 %add_convert_fusion = (bf16[384,1024]{1,0:T(8,128)(2,1)S(1)}, f32[384,1024]{1,0:T(8,128)S(1)}) fusion(f32[1024]{0:T(1024)S(1)} %broadcast_multiply_fusion, bf16[1024,2048]{1,0:T(8,128)(2,1)S(1)} %bitcast.31, bf16[128,2048]{1,0:T(8,128)(2,1)S(1)} %slice.31, bf16[128,2048]{1,0:T(8,128)(2,1)S(1)} %slice.30, bf16[128,2048]{1,0:T(8,128)(2,1)S(1)} %slice.29), kind=kOutput, calls=%fused_computation.20 | convolution fusion | flops 1616117760 | bytes 8130560 | tf_op jit(solution)/shard_map/td,fd->tf/dot_general | solution.py:159
  102.3 2.3 %collective-permute-start.12 = (bf16[384,1024]{1,0:T(8,128)(2,1)S(1)}, bf16[384,1024]{1,0:T(8,128)(2,1)S(1)}, u32[]{:S(2)}, u32[]{:S(2)}) collective-permute-start(bf16[384,1024]{1,0:T(8,128)(2,1)S(1)} %get-tuple-element.90), channel_id=1, source_target_pairs={{0,64},{64,0},{1,65},{65,1},{2,66},{66,2},{3,67},{67,3},{4,68},{68... | collective-permute-start | bytes 2359304 | tf_op jit(solution)/shard_map/ppermute | solution.py:57
  104.6 4.2 %shard_map.91 = (bf16[1024,2048]{1,0:T(8,128)(2,1)}, f32[8,128]{1,0:T(8,128)S(1)}) custom-call(bf16[1024,512]{1,0:T(8,128)(2,1)S(1)} %shard_map.86.code_ref, bf16[128,2176]{1,0:T(8,128)(2,1)S(1)} %bitcast.42, bf16[128,2176]{1,0:T(8,128)(2,1)S(1)} %collective-permute-done.8.e1, bf16[128,2176]{1,0:T(8,128)(2,1)S(1)} %collective-permute-done.9.e2, ...), custom_call_target="tpu_custom_call" | custom-call | flops 2147483648 | bytes 11665408 | tf_op jit(solution)/shard_map/pallas_call | solution.py:212
  109.5 3.9 %shard_map.90 = bf16[2048,1024]{1,0:T(8,128)(2,1)} custom-call(bf16[2048,512]{1,0:T(8,128)(2,1)S(1)} %shard_map.89.token_ref, bf16[512,1024]{1,0:T(8,128)(2,1)S(1)} %pad_maximum_fusion.pre_grad_ref), custom_call_target="tpu_custom_call" | custom-call | flops 2147483648 | bytes 5242880 | tf_op jit(solution)/shard_map/pallas_call | solution.py:242
  (64 shorter events, 8.9 us)
Async XLA Ops:
  22.8 9.5 %collective-permute-start.2 = (bf16[128,2048]{1,0:T(8,128)(2,1)S(1)}, bf16[128,2048]{1,0:T(8,128)(2,1)S(1)}, u32[]{:S(2)}, u32[]{:S(2)}) collective-permute-start(bf16[128,2048]{1,0:T(8,128)(2,1)S(1)} %bitcast.33), channel_id=1, source_target_pairs={{0,1},{1,2},{2,3},{3,0},{4,5},{5,6},{6,7},{7,4},{8,9},{9,10},{10,1... | collective-permute-start | bytes 1572872 | tf_op jit(solution)/shard_map/ppermute | solution.py:49
  23.9 8.5 %collective-permute-start.1 = (bf16[128,2048]{1,0:T(8,128)(2,1)S(1)}, bf16[128,2048]{1,0:T(8,128)(2,1)S(1)}, u32[]{:S(2)}, u32[]{:S(2)}) collective-permute-start(bf16[128,2048]{1,0:T(8,128)(2,1)S(1)} %bitcast.34), channel_id=1, source_target_pairs={{0,16},{1,17},{2,18},{3,19},{4,20},{5,21},{6,22},{7,23},{8,24},{9,... | collective-permute-start | bytes 1572872 | tf_op jit(solution)/shard_map/ppermute | solution.py:49
  24.0 9.2 %collective-permute-start = (bf16[128,2048]{1,0:T(8,128)(2,1)S(1)}, bf16[128,2048]{1,0:T(8,128)(2,1)S(1)}, u32[]{:S(2)}, u32[]{:S(2)}) collective-permute-start(bf16[128,2048]{1,0:T(8,128)(2,1)S(1)} %bitcast.35), channel_id=1, source_target_pairs={{0,3},{1,0},{2,1},{3,2},{4,7},{5,4},{6,5},{7,6},{8,11},{9,8},{10,9... | collective-permute-start | bytes 1572872 | tf_op jit(solution)/shard_map/ppermute | solution.py:49
  26.7 3.2 %copy-start.2 = (s32[512,1024]{1,0:T(8,128)S(1)}, s32[512,1024]{1,0:T(8,128)}, u32[]{:S(2)}) copy-start(s32[512,1024]{1,0:T(8,128)} %mask_ref) | copy-start | bytes 6291460
  26.7 4.1 %copy-start.11 = (bf16[1,2048,1024]{2,1,0:T(8,128)(2,1)S(1)}, bf16[1,2048,1024]{2,1,0:T(8,128)(2,1)}, u32[]{:S(2)}) copy-start(bf16[1,2048,1024]{2,1,0:T(8,128)(2,1)} %param.7) | copy-start | bytes 12582916
  33.1 7.1 %copy-start.12 = (f32[1024]{0:T(1024)S(1)}, f32[1024]{0:T(1024)}, u32[]{:S(2)}) copy-start(f32[1024]{0:T(1024)} %param.8) | copy-start | bytes 12292
  33.1 7.5 %copy-start = (bf16[1,1024,2048]{2,1,0:T(8,128)(2,1)S(1)}, bf16[1,1024,2048]{2,1,0:T(8,128)(2,1)}, u32[]{:S(2)}) copy-start(bf16[1,1024,2048]{2,1,0:T(8,128)(2,1)} %param.9) | copy-start | bytes 12582916
  35.0 5.2 %collective-permute-start.3 = (bf16[384,1024]{1,0:T(8,128)(2,1)S(1)}, bf16[384,1024]{1,0:T(8,128)(2,1)S(1)}, u32[]{:S(2)}, u32[]{:S(2)}) collective-permute-start(bf16[384,1024]{1,0:T(8,128)(2,1)S(1)} %get-tuple-element.86), channel_id=1, source_target_pairs={{0,64},{64,0},{1,65},{65,1},{2,66},{66,2},{3,67},{67,3},{4,68},{68... | collective-permute-start | bytes 2359304 | tf_op jit(solution)/shard_map/ppermute | solution.py:57
  38.3 6.7 %collective-permute-start.7 = (bf16[128,1024]{1,0:T(8,128)(2,1)S(1)}, bf16[128,1024]{1,0:T(8,128)(2,1)S(1)}, u32[]{:S(2)}, u32[]{:S(2)}) collective-permute-start(bf16[128,1024]{1,0:T(8,128)(2,1)S(1)} %get-tuple-element.88), channel_id=1, source_target_pairs={{0,64},{64,0},{1,65},{65,1},{2,66},{66,2},{3,67},{67,3},{4,68},{68... | collective-permute-start | bytes 786440 | tf_op jit(solution)/shard_map/ppermute | solution.py:57
  42.6 8.5 %collective-permute-start.6 = (bf16[128,2048]{1,0:T(8,128)(2,1)S(1)}, bf16[128,2048]{1,0:T(8,128)(2,1)S(1)}, u32[]{:S(2)}, u32[]{:S(2)}) collective-permute-start(bf16[128,2048]{1,0:T(8,128)(2,1)S(1)} %get-tuple-element.83), channel_id=1, source_target_pairs={{0,3},{1,0},{2,1},{3,2},{4,7},{5,4},{6,5},{7,6},{8,11},{9,8},{10,9... | collective-permute-start | bytes 1572872 | tf_op jit(solution)/shard_map/ppermute | solution.py:53
  45.0 9.5 %collective-permute-start.5 = (bf16[128,2048]{1,0:T(8,128)(2,1)S(1)}, bf16[128,2048]{1,0:T(8,128)(2,1)S(1)}, u32[]{:S(2)}, u32[]{:S(2)}) collective-permute-start(bf16[128,2048]{1,0:T(8,128)(2,1)S(1)} %get-tuple-element.84), channel_id=1, source_target_pairs={{0,48},{1,49},{2,50},{3,51},{4,52},{5,53},{6,54},{7,55},{8,56},{9,... | collective-permute-start | bytes 1572872 | tf_op jit(solution)/shard_map/ppermute | solution.py:53
  45.0 9.5 %collective-permute-start.4 = (bf16[128,2048]{1,0:T(8,128)(2,1)S(1)}, bf16[128,2048]{1,0:T(8,128)(2,1)S(1)}, u32[]{:S(2)}, u32[]{:S(2)}) collective-permute-start(bf16[128,2048]{1,0:T(8,128)(2,1)S(1)} %get-tuple-element.85), channel_id=1, source_target_pairs={{0,1},{1,2},{2,3},{3,0},{4,5},{5,6},{6,7},{7,4},{8,9},{9,10},{10,1... | collective-permute-start | bytes 1572872 | tf_op jit(solution)/shard_map/ppermute | solution.py:53
  46.4 23.0 %copy-start.9 = (bf16[1,8,2048]{2,1,0:T(8,128)(2,1)S(1)}, bf16[1,8,2048]{2,1,0:T(8,128)(2,1)}, u32[]{:S(2)}) copy-start(bf16[1,8,2048]{2,1,0:T(8,128)(2,1)} %param.6) | copy-start | bytes 98308
  46.4 23.0 %copy-start.10 = (f32[1,2048]{1,0:T(1,128)S(1)}, f32[1,2048]{1,0:T(1,128)}, u32[]{:S(2)}) copy-start(f32[1,2048]{1,0:T(1,128)} %bias_ref.1) | copy-start | bytes 24580
  70.4 14.9 %all-to-all-start.2 = ((bf16[16,8,2176]{2,1,0:T(8,128)(2,1)}), bf16[16,8,2176]{2,1,0:T(8,128)(2,1)S(1)}, u32[]{:S(2)}, u32[]{:S(2)}) async-start(bf16[16,8,2176]{2,1,0:T(8,128)(2,1)} %shard_map.88), calls=%async_computation.2 | async-start | bytes 1114112 | tf_op jit(solution)/shard_map/all_to_all | solution.py:45
  85.3 12.9 %copy-start.4 = (bf16[128,2048]{1,0:T(8,128)(2,1)S(1)}, bf16[128,2048]{1,0:T(8,128)(2,1)}, u32[]{:S(2)}) copy-start(bf16[128,2048]{1,0:T(8,128)(2,1)} %copy-done.3) | copy-start | bytes 1572868
  85.3 12.9 %copy-start.6 = (bf16[128,2048]{1,0:T(8,128)(2,1)S(1)}, bf16[128,2048]{1,0:T(8,128)(2,1)}, u32[]{:S(2)}) copy-start(bf16[128,2048]{1,0:T(8,128)(2,1)} %copy-done.5) | copy-start | bytes 1572868
  85.3 12.9 %copy-start.8 = (bf16[128,2048]{1,0:T(8,128)(2,1)S(1)}, bf16[128,2048]{1,0:T(8,128)(2,1)}, u32[]{:S(2)}) copy-start(bf16[128,2048]{1,0:T(8,128)(2,1)} %copy-done.7) | copy-start | bytes 1572868
  85.3 14.1 %collective-permute-start.10 = (bf16[128,2176]{1,0:T(8,128)(2,1)S(1)}, bf16[128,2176]{1,0:T(8,128)(2,1)S(1)}, u32[]{:S(2)}, u32[]{:S(2)}) collective-permute-start(bf16[128,2176]{1,0:T(8,128)(2,1)S(1)} %bitcast.38), channel_id=1, source_target_pairs={{0,1},{1,2},{2,3},{3,0},{4,5},{5,6},{6,7},{7,4},{8,9},{9,10},{10,1... | collective-permute-start | bytes 1671176 | tf_op jit(solution)/shard_map/ppermute | solution.py:49
  86.6 12.8 %collective-permute-start.9 = (bf16[128,2176]{1,0:T(8,128)(2,1)S(1)}, bf16[128,2176]{1,0:T(8,128)(2,1)S(1)}, u32[]{:S(2)}, u32[]{:S(2)}) collective-permute-start(bf16[128,2176]{1,0:T(8,128)(2,1)S(1)} %bitcast.39), channel_id=1, source_target_pairs={{0,16},{1,17},{2,18},{3,19},{4,20},{5,21},{6,22},{7,23},{8,24},{9,... | collective-permute-start | bytes 1671176 | tf_op jit(solution)/shard_map/ppermute | solution.py:49
  86.8 12.7 %collective-permute-start.8 = (bf16[128,2176]{1,0:T(8,128)(2,1)S(1)}, bf16[128,2176]{1,0:T(8,128)(2,1)S(1)}, u32[]{:S(2)}, u32[]{:S(2)}) collective-permute-start(bf16[128,2176]{1,0:T(8,128)(2,1)S(1)} %bitcast.40), channel_id=1, source_target_pairs={{0,3},{1,0},{2,1},{3,2},{4,7},{5,4},{6,5},{7,6},{8,11},{9,8},{10,9... | collective-permute-start | bytes 1671176 | tf_op jit(solution)/shard_map/ppermute | solution.py:49
  93.0 6.4 %collective-permute-start.11 = (bf16[128,1024]{1,0:T(8,128)(2,1)S(1)}, bf16[128,1024]{1,0:T(8,128)(2,1)S(1)}, u32[]{:S(2)}, u32[]{:S(2)}) collective-permute-start(bf16[128,1024]{1,0:T(8,128)(2,1)S(1)} %get-tuple-element.77), channel_id=1, source_target_pairs={{0,64},{64,0},{1,65},{65,1},{2,66},{66,2},{3,67},{67,3},{4,68},{68... | collective-permute-start | bytes 786440 | tf_op jit(solution)/shard_map/ppermute | solution.py:57
  102.3 6.7 %collective-permute-start.12 = (bf16[384,1024]{1,0:T(8,128)(2,1)S(1)}, bf16[384,1024]{1,0:T(8,128)(2,1)S(1)}, u32[]{:S(2)}, u32[]{:S(2)}) collective-permute-start(bf16[384,1024]{1,0:T(8,128)(2,1)S(1)} %get-tuple-element.90), channel_id=1, source_target_pairs={{0,64},{64,0},{1,65},{65,1},{2,66},{66,2},{3,67},{67,3},{4,68},{68... | collective-permute-start | bytes 2359304 | tf_op jit(solution)/shard_map/ppermute | solution.py:57
  108.8 4.5 %collective-permute-start.13 = (f32[8,128]{1,0:T(8,128)S(1)}, f32[8,128]{1,0:T(8,128)S(1)}, u32[]{:S(2)}, u32[]{:S(2)}) collective-permute-start(f32[8,128]{1,0:T(8,128)S(1)} %get-tuple-element.75), channel_id=1, source_target_pairs={{0,64},{64,0},{1,65},{65,1},{2,66},{66,2},{3,67},{67,3},{4,68},{68... | collective-permute-start | bytes 12296 | tf_op jit(solution)/shard_map/ppermute | solution.py:57
  (4 other events, 9.4 us)

commit v8 on v6

--- a/solution.py
+++ b/solution.py
@@ -151,6 +151,7 @@
     return pl.pallas_call(
         error_kernel,
         out_shape=jax.ShapeDtypeStruct((count, own, features + EXTRA), BF16),
+        cost_estimate=cost(0, parts, parts),
         compiler_params=params(),
     )(parts, rows, bias, code_a, code_b, norm)
 
@@ -311,7 +312,7 @@
     pre_grad = jnp.concatenate([pre_grad0, pre_grad123])
     grad_enc = grad_encoder(token_t, pre_grad)
     grad_enc, loss, other_loss = lax.optimization_barrier((grad_enc, loss, other_loss))
-    loss = (loss + other_loss)[0, 0]
+    loss = jnp.max(loss + other_loss)
     return (grad_enc[None], grad_dec[None], loss / (tokens * features))
 
 

time: 116 us -> 116 us (level)
  no operation moved by 1% of the time
where the time goes in v8:
time: 116 us
  blocking collectives  36 us (31%)
  starting transfers between devices  26.7 us (23%)
  waiting for transfers between devices  21.4 us (18%)
  Pallas kernels  11.5 us (10%)
  matrix products  10.7 us (9%)
  other arithmetic  5.04 us (4%)
  between operations  2.7 us (2%)
  local copies, waits for them, and re-layouts  1.66 us (1%)
    all_to_all x2, blocking collectives, class_exchange(): lax.all_to_all(x, LATENT, 0, 0, axis_index_groups=class_groups(), tiled=T...  36 us
    ppermute x5, starting transfers between devices, swap_layers(): return lax.ppermute(x, 'layer', [(0, 1), (1, 0)])  11 us
    all_to_all x1, waiting for transfers between devices, class_exchange(): lax.all_to_all(x, LATENT, 0, 0, axis_index_groups=class_groups(), tiled=T...  9.29 us
    ppermute x3, waiting for transfers between devices, to_neighbours(): lax.ppermute(x, EVERY, moved(r, 1))  8.12 us
    ppermute x6, starting transfers between devices, from_neighbours(): return [lax.ppermute(x, EVERY, moved(r, -1)) for r in (1, 2, 3)]  7.81 us
    all_to_all x1, starting transfers between devices, class_exchange(): lax.all_to_all(x, LATENT, 0, 0, axis_index_groups=class_groups(), tiled=T...  5.59 us
    dot_general x2, matrix products, code_gradient(): grad = jnp.einsum('td,fd->tf', error, weight, preferred_element_type=F32)  5.56 us
    pallas_call x1, Pallas kernels, grad_decoder(): pl.pallas_call(grad_dec_kernel, out_shape=(jax.ShapeDtypeStruct((latents,...  4.18 us
  transfers between devices with their start and end apart: 15, of which 7 were waited for; matrix products, arithmetic and copies ran while one was open for 10% of the time, Pallas kernels for 9%

profile of v8, /device:TPU:1, one launch (start us, length us, event | category | flops | bytes accessed | tf_op | source)
XLA Modules:
  0.0 115.7 jit_solution(10317186516769996467)
XLA Ops:
  1.4 21.4 %all_to_all.15 = bf16[16,8,2048]{2,1,0:T(8,128)(2,1)S(1)} all-to-all(bf16[16,8,2048]{2,1,0:T(8,128)(2,1)S(1)} %broadcast_in_dim.23), channel_id=1, replica_groups={{0,7,10,13,18,21,24,31,32,39,42,45,50,53,56,63},{1,4,11,14,19,22,25,28,..., dimensions={0} | all-to-all | bytes 1048576 | tf_op jit(solution)/shard_map/all_to_all | solution.py:45
  22.8 1.1 collective-permute-start.2
  24.0 2.7 %collective-permute-start = (bf16[128,2048]{1,0:T(8,128)(2,1)S(1)}, bf16[128,2048]{1,0:T(8,128)(2,1)S(1)}, u32[]{:S(2)}, u32[]{:S(2)}) collective-permute-start(bf16[128,2048]{1,0:T(8,128)(2,1)S(1)} %bitcast.32), channel_id=1, source_target_pairs={{0,3},{1,0},{2,1},{3,2},{4,7},{5,4},{6,5},{7,6},{8,11},{9,8},{10,9... | collective-permute-start | bytes 1572872 | tf_op jit(solution)/shard_map/ppermute | solution.py:49
  26.7 3.2 %multiply_reduce_fusion = f32[1024]{0:T(1024)S(1)} fusion(bf16[1024,2048]{1,0:T(8,128)(2,1)} %bitcast.24), kind=kLoop, calls=%fused_computation | loop fusion | flops 6290432 | bytes 4198400 | tf_op jit(solution)/shard_map/reduce_sum | solution.py:276
  33.1 1.8 %fusion.31 = (bf16[384,1024]{1,0:T(8,128)(2,1)S(1)}, f32[384,1024]{1,0:T(8,128)S(1)}) fusion(bf16[1,2048,1024]{2,1,0:T(8,128)(2,1)S(1)} %copy-done.11, bf16[128,2048]{1,0:T(8,128)(2,1)S(1)} %collective-permute-done.2.refs_3_, bf16[128,2048]{1,0:T(8,128)(2,1)S(1)} %collective-permute-done.1.refs_2_, bf16[128,2048]{1,0:T(8,128)(2,1)S(1)} %collective-permute-done.refs_1_), kind=kOutput, calls=%fused_computation.55 | convolution fusion | flops 1615724544 | bytes 8126464 | tf_op jit(solution)/shard_map/dot_general | solution.py:278
  35.0 3.2 %collective-permute-start.3 = (bf16[384,1024]{1,0:T(8,128)(2,1)S(1)}, bf16[384,1024]{1,0:T(8,128)(2,1)S(1)}, u32[]{:S(2)}, u32[]{:S(2)}) collective-permute-start(bf16[384,1024]{1,0:T(8,128)(2,1)S(1)} %get-tuple-element.84), channel_id=1, source_target_pairs={{0,64},{64,0},{1,65},{65,1},{2,66},{66,2},{3,67},{67,3},{4,68},{68... | collective-permute-start | bytes 2359304 | tf_op jit(solution)/shard_map/ppermute | solution.py:57
  38.4 1.8 %collective-permute-done.3 = bf16[384,1024]{1,0:T(8,128)(2,1)S(1)} collective-permute-done((bf16[384,1024]{1,0:T(8,128)(2,1)S(1)}, bf16[384,1024]{1,0:T(8,128)(2,1)S(1)}, u32[]{:S(2)}, u32[]{:S(2)}) %collective-permute-start.3) | collective-permute-done | bytes 786464 | tf_op jit(solution)/shard_map/ppermute | solution.py:57
  40.7 1.8 %convolution_convert_fusion = bf16[384,2048]{1,0:T(8,128)(2,1)S(1)} fusion(bf16[384,1024]{1,0:T(8,128)(2,1)S(1)} %get-tuple-element.78.refs_1_, bf16[1024,2048]{1,0:T(8,128)(2,1)S(1)} %bitcast.26), kind=kOutput, calls=%fused_computation.5 | convolution fusion | flops 1611399168 | bytes 6553600 | tf_op jit(solution)/shard_map/dot_general | solution.py:284
  42.6 2.3 %collective-permute-start.6 = (bf16[128,2048]{1,0:T(8,128)(2,1)S(1)}, bf16[128,2048]{1,0:T(8,128)(2,1)S(1)}, u32[]{:S(2)}, u32[]{:S(2)}) collective-permute-start(bf16[128,2048]{1,0:T(8,128)(2,1)S(1)} %get-tuple-element.81), channel_id=1, source_target_pairs={{0,3},{1,0},{2,1},{3,2},{4,7},{5,4},{6,5},{7,6},{8,11},{9,8},{10,9... | collective-permute-start | bytes 1572872 | tf_op jit(solution)/shard_map/ppermute | solution.py:53
  46.4 4.7 %collective-permute-done.6.c_ref = bf16[128,2048]{1,0:T(8,128)(2,1)S(1)} collective-permute-done((bf16[128,2048]{1,0:T(8,128)(2,1)S(1)}, bf16[128,2048]{1,0:T(8,128)(2,1)S(1)}, u32[]{:S(2)}, u32[]{:S(2)}) %collective-permute-start.6) | collective-permute-done | bytes 524320 | tf_op jit(solution)/shard_map/ppermute | solution.py:53
  51.1 3.4 %collective-permute-done.5.b_ref = bf16[128,2048]{1,0:T(8,128)(2,1)S(1)} collective-permute-done((bf16[128,2048]{1,0:T(8,128)(2,1)S(1)}, bf16[128,2048]{1,0:T(8,128)(2,1)S(1)}, u32[]{:S(2)}, u32[]{:S(2)}) %collective-permute-start.5) | collective-permute-done | bytes 524320 | tf_op jit(solution)/shard_map/ppermute | solution.py:53
  54.8 14.6 %all_to_all.16.parts_ref = bf16[16,8,2048]{2,1,0:T(8,128)(2,1)S(1)} all-to-all(bf16[16,8,2048]{2,1,0:T(8,128)(2,1)S(1)} %bitcast.40), channel_id=1, replica_groups={{0,7,10,13,18,21,24,31,32,39,42,45,50,53,56,63},{1,4,11,14,19,22,25,28,..., dimensions={0} | all-to-all | bytes 1048576 | tf_op jit(solution)/shard_map/all_to_all | solution.py:45
  69.4 1.0 shard_map.88
  70.4 5.6 %all-to-all-start.2 = ((bf16[16,8,2176]{2,1,0:T(8,128)(2,1)}), bf16[16,8,2176]{2,1,0:T(8,128)(2,1)S(1)}, u32[]{:S(2)}, u32[]{:S(2)}) async-start(bf16[16,8,2176]{2,1,0:T(8,128)(2,1)} %shard_map.88), calls=%async_computation.2 | async-start | bytes 1114112 | tf_op jit(solution)/shard_map/all_to_all | solution.py:45
  76.0 9.3 %all-to-all-done.2 = bf16[16,8,2176]{2,1,0:T(8,128)(2,1)S(1)} async-done(((bf16[16,8,2176]{2,1,0:T(8,128)(2,1)}), bf16[16,8,2176]{2,1,0:T(8,128)(2,1)S(1)}, u32[]{:S(2)}, u32[]{:S(2)}) %all-to-all-start.2) | async-done | bytes 557088 | tf_op jit(solution)/shard_map/all_to_all | solution.py:45
  85.3 1.3 %collective-permute-start.10 = (bf16[128,2176]{1,0:T(8,128)(2,1)S(1)}, bf16[128,2176]{1,0:T(8,128)(2,1)S(1)}, u32[]{:S(2)}, u32[]{:S(2)}) collective-permute-start(bf16[128,2176]{1,0:T(8,128)(2,1)S(1)} %bitcast.35), channel_id=1, source_target_pairs={{0,1},{1,2},{2,3},{3,0},{4,5},{5,6},{6,7},{7,4},{8,9},{9,10},{10,1... | collective-permute-start | bytes 1671176 | tf_op jit(solution)/shard_map/ppermute | solution.py:49
  86.8 2.5 %collective-permute-start.8 = (bf16[128,2176]{1,0:T(8,128)(2,1)S(1)}, bf16[128,2176]{1,0:T(8,128)(2,1)S(1)}, u32[]{:S(2)}, u32[]{:S(2)}) collective-permute-start(bf16[128,2176]{1,0:T(8,128)(2,1)S(1)} %bitcast.37), channel_id=1, source_target_pairs={{0,3},{1,0},{2,1},{3,2},{4,7},{5,4},{6,5},{7,6},{8,11},{9,8},{10,9... | collective-permute-start | bytes 1671176 | tf_op jit(solution)/shard_map/ppermute | solution.py:49
  89.3 3.7 %broadcast_add_fusion = f32[128,1024]{1,0:T(8,128)S(1)} fusion(f32[1024]{0:T(1024)S(1)} %broadcast_multiply_fusion, bf16[1024,2048]{1,0:T(8,128)(2,1)} %bitcast.25, bf16[128,2176]{1,0:T(8,128)(2,1)S(1)} %bitcast.38), kind=kOutput, calls=%fused_computation.29 | convolution fusion | flops 537001984 | bytes 5246976 | tf_op jit(solution)/shard_map/td,fd->tf/dot_general | solution.py:160
  93.0 5.3 %collective-permute-start.11 = (f32[128,1024]{1,0:T(8,128)S(1)}, f32[128,1024]{1,0:T(8,128)S(1)}, u32[]{:S(2)}, u32[]{:S(2)}) collective-permute-start(f32[128,1024]{1,0:T(8,128)S(1)} %broadcast_add_fusion), channel_id=1, source_target_pairs={{0,64},{64,0},{1,65},{65,1},{2,66},{66,2},{3,67},{67,3},{4,68},{68... | collective-permute-start | bytes 1572872 | tf_op jit(solution)/shard_map/ppermute | solution.py:57
  98.2 1.0 shard_map.89.token_ref
  100.4 1.9 %add_convert_fusion = (bf16[384,1024]{1,0:T(8,128)(2,1)S(1)}, f32[384,1024]{1,0:T(8,128)S(1)}) fusion(f32[1024]{0:T(1024)S(1)} %broadcast_multiply_fusion, bf16[1024,2048]{1,0:T(8,128)(2,1)S(1)} %bitcast.28, bf16[128,2048]{1,0:T(8,128)(2,1)S(1)} %slice.28, bf16[128,2048]{1,0:T(8,128)(2,1)S(1)} %slice.27, bf16[128,2048]{1,0:T(8,128)(2,1)S(1)} %slice.26), kind=kOutput, calls=%fused_computation.20 | convolution fusion | flops 1616117760 | bytes 8130560 | tf_op jit(solution)/shard_map/td,fd->tf/dot_general | solution.py:160
  102.3 2.3 %collective-permute-start.12 = (bf16[384,1024]{1,0:T(8,128)(2,1)S(1)}, bf16[384,1024]{1,0:T(8,128)(2,1)S(1)}, u32[]{:S(2)}, u32[]{:S(2)}) collective-permute-start(bf16[384,1024]{1,0:T(8,128)(2,1)S(1)} %get-tuple-element.86), channel_id=1, source_target_pairs={{0,64},{64,0},{1,65},{65,1},{2,66},{66,2},{3,67},{67,3},{4,68},{68... | collective-permute-start | bytes 2359304 | tf_op jit(solution)/shard_map/ppermute | solution.py:57
  104.6 4.2 %shard_map.91 = (bf16[1024,2048]{1,0:T(8,128)(2,1)}, f32[8,128]{1,0:T(8,128)S(1)}) custom-call(bf16[1024,512]{1,0:T(8,128)(2,1)S(1)} %shard_map.86.code_ref, bf16[128,2176]{1,0:T(8,128)(2,1)S(1)} %bitcast.39, bf16[128,2176]{1,0:T(8,128)(2,1)S(1)} %collective-permute-done.8.e1, bf16[128,2176]{1,0:T(8,128)(2,1)S(1)} %collective-permute-done.9.e2, ...), custom_call_target="tpu_custom_call" | custom-call | flops 2147483648 | bytes 11665408 | tf_op jit(solution)/shard_map/pallas_call | solution.py:213
  109.5 3.9 %shard_map.90 = bf16[2048,1024]{1,0:T(8,128)(2,1)} custom-call(bf16[2048,512]{1,0:T(8,128)(2,1)S(1)} %shard_map.89.token_ref, bf16[512,1024]{1,0:T(8,128)(2,1)S(1)} %pad_maximum_fusion.pre_grad_ref), custom_call_target="tpu_custom_call" | custom-call | flops 2147483648 | bytes 5242880 | tf_op jit(solution)/shard_map/pallas_call | solution.py:243
  (62 shorter events, 9.0 us)
Async XLA Ops:
  22.8 9.5 %collective-permute-start.2 = (bf16[128,2048]{1,0:T(8,128)(2,1)S(1)}, bf16[128,2048]{1,0:T(8,128)(2,1)S(1)}, u32[]{:S(2)}, u32[]{:S(2)}) collective-permute-start(bf16[128,2048]{1,0:T(8,128)(2,1)S(1)} %bitcast.30), channel_id=1, source_target_pairs={{0,1},{1,2},{2,3},{3,0},{4,5},{5,6},{6,7},{7,4},{8,9},{9,10},{10,1... | collective-permute-start | bytes 1572872 | tf_op jit(solution)/shard_map/ppermute | solution.py:49
  23.9 8.5 %collective-permute-start.1 = (bf16[128,2048]{1,0:T(8,128)(2,1)S(1)}, bf16[128,2048]{1,0:T(8,128)(2,1)S(1)}, u32[]{:S(2)}, u32[]{:S(2)}) collective-permute-start(bf16[128,2048]{1,0:T(8,128)(2,1)S(1)} %bitcast.31), channel_id=1, source_target_pairs={{0,16},{1,17},{2,18},{3,19},{4,20},{5,21},{6,22},{7,23},{8,24},{9,... | collective-permute-start | bytes 1572872 | tf_op jit(solution)/shard_map/ppermute | solution.py:49
  24.0 9.2 %collective-permute-start = (bf16[128,2048]{1,0:T(8,128)(2,1)S(1)}, bf16[128,2048]{1,0:T(8,128)(2,1)S(1)}, u32[]{:S(2)}, u32[]{:S(2)}) collective-permute-start(bf16[128,2048]{1,0:T(8,128)(2,1)S(1)} %bitcast.32), channel_id=1, source_target_pairs={{0,3},{1,0},{2,1},{3,2},{4,7},{5,4},{6,5},{7,6},{8,11},{9,8},{10,9... | collective-permute-start | bytes 1572872 | tf_op jit(solution)/shard_map/ppermute | solution.py:49
  26.7 3.2 %copy-start.2 = (s32[512,1024]{1,0:T(8,128)S(1)}, s32[512,1024]{1,0:T(8,128)}, u32[]{:S(2)}) copy-start(s32[512,1024]{1,0:T(8,128)} %mask_ref) | copy-start | bytes 6291460
  26.7 4.1 %copy-start.11 = (bf16[1,2048,1024]{2,1,0:T(8,128)(2,1)S(1)}, bf16[1,2048,1024]{2,1,0:T(8,128)(2,1)}, u32[]{:S(2)}) copy-start(bf16[1,2048,1024]{2,1,0:T(8,128)(2,1)} %param.7) | copy-start | bytes 12582916
  31.5 8.7 %copy-start.12 = (f32[1024]{0:T(1024)S(1)}, f32[1024]{0:T(1024)}, u32[]{:S(2)}) copy-start(f32[1024]{0:T(1024)} %param.8) | copy-start | bytes 12292
  33.1 7.5 %copy-start = (bf16[1,1024,2048]{2,1,0:T(8,128)(2,1)S(1)}, bf16[1,1024,2048]{2,1,0:T(8,128)(2,1)}, u32[]{:S(2)}) copy-start(bf16[1,1024,2048]{2,1,0:T(8,128)(2,1)} %param.9) | copy-start | bytes 12582916
  35.0 5.2 %collective-permute-start.3 = (bf16[384,1024]{1,0:T(8,128)(2,1)S(1)}, bf16[384,1024]{1,0:T(8,128)(2,1)S(1)}, u32[]{:S(2)}, u32[]{:S(2)}) collective-permute-start(bf16[384,1024]{1,0:T(8,128)(2,1)S(1)} %get-tuple-element.84), channel_id=1, source_target_pairs={{0,64},{64,0},{1,65},{65,1},{2,66},{66,2},{3,67},{67,3},{4,68},{68... | collective-permute-start | bytes 2359304 | tf_op jit(solution)/shard_map/ppermute | solution.py:57
  38.3 6.7 %collective-permute-start.7 = (f32[128,1024]{1,0:T(8,128)S(1)}, f32[128,1024]{1,0:T(8,128)S(1)}, u32[]{:S(2)}, u32[]{:S(2)}) collective-permute-start(f32[128,1024]{1,0:T(8,128)S(1)} %fusion.2), channel_id=1, source_target_pairs={{0,64},{64,0},{1,65},{65,1},{2,66},{66,2},{3,67},{67,3},{4,68},{68... | collective-permute-start | bytes 1572872 | tf_op jit(solution)/shard_map/ppermute | solution.py:57
  42.6 8.5 %collective-permute-start.6 = (bf16[128,2048]{1,0:T(8,128)(2,1)S(1)}, bf16[128,2048]{1,0:T(8,128)(2,1)S(1)}, u32[]{:S(2)}, u32[]{:S(2)}) collective-permute-start(bf16[128,2048]{1,0:T(8,128)(2,1)S(1)} %get-tuple-element.81), channel_id=1, source_target_pairs={{0,3},{1,0},{2,1},{3,2},{4,7},{5,4},{6,5},{7,6},{8,11},{9,8},{10,9... | collective-permute-start | bytes 1572872 | tf_op jit(solution)/shard_map/ppermute | solution.py:53
  44.9 9.5 %collective-permute-start.5 = (bf16[128,2048]{1,0:T(8,128)(2,1)S(1)}, bf16[128,2048]{1,0:T(8,128)(2,1)S(1)}, u32[]{:S(2)}, u32[]{:S(2)}) collective-permute-start(bf16[128,2048]{1,0:T(8,128)(2,1)S(1)} %get-tuple-element.82), channel_id=1, source_target_pairs={{0,48},{1,49},{2,50},{3,51},{4,52},{5,53},{6,54},{7,55},{8,56},{9,... | collective-permute-start | bytes 1572872 | tf_op jit(solution)/shard_map/ppermute | solution.py:53
  45.0 9.5 %collective-permute-start.4 = (bf16[128,2048]{1,0:T(8,128)(2,1)S(1)}, bf16[128,2048]{1,0:T(8,128)(2,1)S(1)}, u32[]{:S(2)}, u32[]{:S(2)}) collective-permute-start(bf16[128,2048]{1,0:T(8,128)(2,1)S(1)} %get-tuple-element.83), channel_id=1, source_target_pairs={{0,1},{1,2},{2,3},{3,0},{4,5},{5,6},{6,7},{7,4},{8,9},{9,10},{10,1... | collective-permute-start | bytes 1572872 | tf_op jit(solution)/shard_map/ppermute | solution.py:53
  46.4 23.0 %copy-start.9 = (bf16[1,8,2048]{2,1,0:T(8,128)(2,1)S(1)}, bf16[1,8,2048]{2,1,0:T(8,128)(2,1)}, u32[]{:S(2)}) copy-start(bf16[1,8,2048]{2,1,0:T(8,128)(2,1)} %param.6) | copy-start | bytes 98308
  46.4 23.0 %copy-start.10 = (f32[1,2048]{1,0:T(1,128)S(1)}, f32[1,2048]{1,0:T(1,128)}, u32[]{:S(2)}) copy-start(f32[1,2048]{1,0:T(1,128)} %bias_ref.1) | copy-start | bytes 24580
  70.4 14.9 %all-to-all-start.2 = ((bf16[16,8,2176]{2,1,0:T(8,128)(2,1)}), bf16[16,8,2176]{2,1,0:T(8,128)(2,1)S(1)}, u32[]{:S(2)}, u32[]{:S(2)}) async-start(bf16[16,8,2176]{2,1,0:T(8,128)(2,1)} %shard_map.88), calls=%async_computation.2 | async-start | bytes 1114112 | tf_op jit(solution)/shard_map/all_to_all | solution.py:45
  85.3 12.9 %copy-start.4 = (bf16[128,2048]{1,0:T(8,128)(2,1)S(1)}, bf16[128,2048]{1,0:T(8,128)(2,1)}, u32[]{:S(2)}) copy-start(bf16[128,2048]{1,0:T(8,128)(2,1)} %copy-done.3) | copy-start | bytes 1572868
  85.3 12.9 %copy-start.6 = (bf16[128,2048]{1,0:T(8,128)(2,1)S(1)}, bf16[128,2048]{1,0:T(8,128)(2,1)}, u32[]{:S(2)}) copy-start(bf16[128,2048]{1,0:T(8,128)(2,1)} %copy-done.5) | copy-start | bytes 1572868
  85.3 12.9 %copy-start.8 = (bf16[128,2048]{1,0:T(8,128)(2,1)S(1)}, bf16[128,2048]{1,0:T(8,128)(2,1)}, u32[]{:S(2)}) copy-start(bf16[128,2048]{1,0:T(8,128)(2,1)} %copy-done.7) | copy-start | bytes 1572868
  85.3 14.5 %collective-permute-start.10 = (bf16[128,2176]{1,0:T(8,128)(2,1)S(1)}, bf16[128,2176]{1,0:T(8,128)(2,1)S(1)}, u32[]{:S(2)}, u32[]{:S(2)}) collective-permute-start(bf16[128,2176]{1,0:T(8,128)(2,1)S(1)} %bitcast.35), channel_id=1, source_target_pairs={{0,1},{1,2},{2,3},{3,0},{4,5},{5,6},{6,7},{7,4},{8,9},{9,10},{10,1... | collective-permute-start | bytes 1671176 | tf_op jit(solution)/shard_map/ppermute | solution.py:49
  86.6 13.1 %collective-permute-start.9 = (bf16[128,2176]{1,0:T(8,128)(2,1)S(1)}, bf16[128,2176]{1,0:T(8,128)(2,1)S(1)}, u32[]{:S(2)}, u32[]{:S(2)}) collective-permute-start(bf16[128,2176]{1,0:T(8,128)(2,1)S(1)} %bitcast.36), channel_id=1, source_target_pairs={{0,16},{1,17},{2,18},{3,19},{4,20},{5,21},{6,22},{7,23},{8,24},{9,... | collective-permute-start | bytes 1671176 | tf_op jit(solution)/shard_map/ppermute | solution.py:49
  86.8 13.0 %collective-permute-start.8 = (bf16[128,2176]{1,0:T(8,128)(2,1)S(1)}, bf16[128,2176]{1,0:T(8,128)(2,1)S(1)}, u32[]{:S(2)}, u32[]{:S(2)}) collective-permute-start(bf16[128,2176]{1,0:T(8,128)(2,1)S(1)} %bitcast.37), channel_id=1, source_target_pairs={{0,3},{1,0},{2,1},{3,2},{4,7},{5,4},{6,5},{7,6},{8,11},{9,8},{10,9... | collective-permute-start | bytes 1671176 | tf_op jit(solution)/shard_map/ppermute | solution.py:49
  93.0 6.8 %collective-permute-start.11 = (f32[128,1024]{1,0:T(8,128)S(1)}, f32[128,1024]{1,0:T(8,128)S(1)}, u32[]{:S(2)}, u32[]{:S(2)}) collective-permute-start(f32[128,1024]{1,0:T(8,128)S(1)} %broadcast_add_fusion), channel_id=1, source_target_pairs={{0,64},{64,0},{1,65},{65,1},{2,66},{66,2},{3,67},{67,3},{4,68},{68... | collective-permute-start | bytes 1572872 | tf_op jit(solution)/shard_map/ppermute | solution.py:57
  102.3 6.7 %collective-permute-start.12 = (bf16[384,1024]{1,0:T(8,128)(2,1)S(1)}, bf16[384,1024]{1,0:T(8,128)(2,1)S(1)}, u32[]{:S(2)}, u32[]{:S(2)}) collective-permute-start(bf16[384,1024]{1,0:T(8,128)(2,1)S(1)} %get-tuple-element.86), channel_id=1, source_target_pairs={{0,64},{64,0},{1,65},{65,1},{2,66},{66,2},{3,67},{67,3},{4,68},{68... | collective-permute-start | bytes 2359304 | tf_op jit(solution)/shard_map/ppermute | solution.py:57
  108.8 4.5 %collective-permute-start.13 = (f32[8,128]{1,0:T(8,128)S(1)}, f32[8,128]{1,0:T(8,128)S(1)}, u32[]{:S(2)}, u32[]{:S(2)}) collective-permute-start(f32[8,128]{1,0:T(8,128)S(1)} %get-tuple-element.75), channel_id=1, source_target_pairs={{0,64},{64,0},{1,65},{65,1},{2,66},{66,2},{3,67},{67,3},{4,68},{68... | collective-permute-start | bytes 12296 | tf_op jit(solution)/shard_map/ppermute | solution.py:57
  (4 other events, 9.4 us)
